TPU v7x, 32 devices: a whole 2x2x4 slice. The times are simulated.
32 devices in a mesh: bins: 4 (over y, x), batch: 4 (over z), fsdp: 2 (over core).
Axes of the slice: x: 2, y: 2, z: 4, core: 2. Of those that a mesh axis runs over, the one named last changes fastest.
Arguments:
- track_in: bfloat16 [64, 1024, 768], P(('batch', 'fsdp'), 'bins'), may hold values from -6 to 6
- black_mask: int32 [64, 1024], P(('batch', 'fsdp'), 'bins'), may hold values 0 or 1
- unmap_mask: int32 [64, 1024], P(('batch', 'fsdp'), 'bins'), may hold values 0 or 1
- seq_valid: int32 [64], P(('batch', 'fsdp')), may hold values from 256 to 1024
- dilated_weight: float32 [2304, 384], P(('batch', 'fsdp')), may hold values from -0.125 to 0.125
- point_weight: float32 [384, 768], P(('batch', 'fsdp')), may hold values from -0.30618622 to 0.30618622
- point_bias: float32 [768], P(('batch', 'fsdp')), may hold values from -3 to 3
- gain_first: float32 [768], P(('batch', 'fsdp')), may hold values from 0.5 to 2
- shift_first: float32 [768], P(('batch', 'fsdp')), may hold values from -3 to 3
- gain_second: float32 [384], P(('batch', 'fsdp')), may hold values from 0.5 to 2
- shift_second: float32 [384], P(('batch', 'fsdp')), may hold values from -3 to 3
- out_grad: bfloat16 [64, 1024, 768], P(('batch', 'fsdp'), 'bins'), may hold values from -8 to 8
Outputs:
- block_out: bfloat16 [64, 1024, 768], P(('batch', 'fsdp'), 'bins')
- input_grad: bfloat16 [64, 1024, 768], P(('batch', 'fsdp'), 'bins')
- dilated_grad: float32 [2304, 384], P(('batch', 'fsdp'))
- point_grad: float32 [384, 768], P(('batch', 'fsdp'))
- bias_grad: float32 [768], P(('batch', 'fsdp'))
- gain_first_grad: float32 [768], P(('batch', 'fsdp'))
- shift_first_grad: float32 [768], P(('batch', 'fsdp'))
- gain_second_grad: float32 [384], P(('batch', 'fsdp'))
- shift_second_grad: float32 [384], P(('batch', 'fsdp'))
All inputs are finite; a program needn't handle non-finite values. No bound on the sum of `black_mask` or of `unmap_mask` on one device may be relied on, other than what follows from the above.
Results may differ from a plain program's by a relative error of at most 0.0074.
Values may be sent and summed in bfloat16 or wider, within the bound.
A program may use at most 128 MiB of HBM per device.

v0:
```python
import jax
import jax.numpy as jnp
from jax import lax
from jax.sharding import PartitionSpec as P

DILATION_STEP = 26


norm_eps = 1e-05


def extended(block, sides, width):
    for axis, dim in sides:
        count = lax.axis_size(axis)
        forward = [(i, i + 1) for i in range(count - 1)]
        backward = [(target, source) for source, target in forward]
        low = lax.ppermute(
            lax.slice_in_dim(block, block.shape[dim] - width, None, axis=dim), axis, forward
        )
        high = lax.ppermute(lax.slice_in_dim(block, 0, width, axis=dim), axis, backward)
        block = jnp.concatenate([low, block, high], axis=dim)
    return block


def activate(values):
    return values * jax.nn.sigmoid(1.702 * values)


def slope(values):
    sigma = jax.nn.sigmoid(1.702 * values)
    return sigma + 1.702 * values * sigma * (1.0 - sigma)


def moments(values, valid, local_count):
    total, count = lax.psum(
        (jnp.sum(values * valid, axis=0), local_count), ("bins", "batch", "fsdp")
    )
    mean = total / count
    centred = values - mean
    spread = lax.psum(jnp.sum(centred * centred * valid, axis=0), ("bins", "batch", "fsdp"))
    variance = spread / count
    scale = lax.rsqrt(variance + norm_eps)
    return (centred * scale, scale, count)


def norm_back(grad_out, normed, scale, gain, valid, count):
    total, cross = lax.psum(
        (jnp.sum(grad_out, axis=0), jnp.sum(grad_out * normed, axis=0)), ("bins", "batch", "fsdp")
    )
    grad_in = scale * gain * (grad_out - valid * (total + normed * cross) / count)
    return (grad_in, total, cross)


def contract_rows(left, right):
    return lax.dot_general(
        left, right, (((0,), (0,)), ((), ())), preferred_element_type=jnp.float32
    )


def local(
    track_in,
    black_mask,
    unmap_mask,
    seq_valid,
    dilated_weight,
    point_weight,
    point_bias,
    gain_first,
    shift_first,
    gain_second,
    shift_second,
    out_grad,
):
    sequence_count, count_of_bins, channel_count = track_in.shape
    row_count = sequence_count * count_of_bins
    bf = jnp.bfloat16
    gathered_taps = (
        lax.all_gather(dilated_weight.astype(bf), ("batch", "fsdp"), axis=0, tiled=True),
        lax.all_gather(point_weight.astype(bf), ("batch", "fsdp"), axis=0, tiled=True),
        lax.all_gather(point_bias.astype(bf), ("batch", "fsdp"), axis=0, tiled=True),
        lax.all_gather(gain_first.astype(bf), ("batch", "fsdp"), axis=0, tiled=True),
        lax.all_gather(shift_first.astype(bf), ("batch", "fsdp"), axis=0, tiled=True),
        lax.all_gather(gain_second.astype(bf), ("batch", "fsdp"), axis=0, tiled=True),
        lax.all_gather(shift_second.astype(bf), ("batch", "fsdp"), axis=0, tiled=True),
    )
    dilation_weight = gathered_taps[0]
    pointwise_weight = gathered_taps[1]
    hidden_state = pointwise_weight.shape[0]
    bias_vector = gathered_taps[2].astype(jnp.float32)
    first_gain = gathered_taps[3].astype(jnp.float32)
    first_offset = gathered_taps[4].astype(jnp.float32)
    second_gain = gathered_taps[5].astype(jnp.float32)
    second_offset = gathered_taps[6].astype(jnp.float32)
    place = lax.axis_index("bins") * count_of_bins + lax.broadcasted_iota(
        jnp.int32, (sequence_count, count_of_bins), 1
    )
    keep = (black_mask == 0) & (unmap_mask == 0) & (place < seq_valid[:, None])
    valid = keep.astype(jnp.float32).reshape(row_count, 1)
    local_count = jnp.sum(valid)
    input_signal = track_in.reshape(row_count, channel_count).astype(jnp.float32)
    normed_one, scale_one, count = moments(input_signal, valid, local_count)
    pre_one = normed_one * first_gain + first_offset
    first_hidden = activate(pre_one).astype(bf)
    first_padded = extended(
        first_hidden.reshape(sequence_count, count_of_bins, channel_count),
        (("bins", 1),),
        DILATION_STEP,
    )
    kernel_taps = jnp.concatenate(
        [
            first_padded[
                :,
                kernel_tap_index * DILATION_STEP : kernel_tap_index * DILATION_STEP + count_of_bins,
                :,
            ]
            for kernel_tap_index in range(3)
        ],
        axis=2,
    ).reshape(row_count, 3 * channel_count)
    convolution_output = jnp.dot(kernel_taps, dilation_weight, preferred_element_type=jnp.float32)
    normed_two, scale_two, count_again = moments(convolution_output, valid, local_count)
    pre_two = normed_two * second_gain + second_offset
    hidden_two = activate(pre_two).astype(bf)
    branch = jnp.dot(hidden_two, pointwise_weight, preferred_element_type=jnp.float32)
    block_out = (
        (input_signal + branch + bias_vector)
        .astype(bf)
        .reshape(sequence_count, count_of_bins, channel_count)
    )
    grad = out_grad.reshape(row_count, channel_count) * keep.reshape(row_count, 1).astype(bf)
    point_local = contract_rows(hidden_two, grad)
    bias_local = jnp.sum(grad, axis=0, dtype=jnp.float32)
    grad_two = jnp.dot(grad, pointwise_weight.T, preferred_element_type=jnp.float32) * slope(
        pre_two
    )
    convolution_gradient, shift_two_total, gain_two_total = norm_back(
        grad_two, normed_two, scale_two, second_gain, valid, count
    )
    convolution_gradient = convolution_gradient.astype(bf)
    dilated_local = contract_rows(kernel_taps, convolution_gradient)
    padded_gradient = extended(
        convolution_gradient.reshape(sequence_count, count_of_bins, hidden_state),
        (("bins", 1),),
        DILATION_STEP,
    )
    back_taps = jnp.concatenate(
        [
            padded_gradient[
                :,
                (2 - kernel_tap_index) * DILATION_STEP : (2 - kernel_tap_index) * DILATION_STEP
                + count_of_bins,
                :,
            ]
            for kernel_tap_index in range(3)
        ],
        axis=2,
    ).reshape(row_count, 3 * hidden_state)
    weight_backward = jnp.transpose(
        dilation_weight.reshape(3, channel_count, hidden_state), (0, 2, 1)
    ).reshape(3 * hidden_state, channel_count)
    grad_one = jnp.dot(back_taps, weight_backward, preferred_element_type=jnp.float32) * slope(
        pre_one
    )
    input_part, shift_one_total, gain_one_total = norm_back(
        grad_one, normed_one, scale_one, first_gain, valid, count
    )
    input_grad = (
        (grad.astype(jnp.float32) + input_part)
        .astype(bf)
        .reshape(sequence_count, count_of_bins, channel_count)
    )
    local_grads = (dilated_local, point_local, bias_local)
    summed = lax.psum((local_grads[0], local_grads[1], local_grads[2]), "bins")
    shares = (
        lax.psum_scatter(summed[0], ("batch", "fsdp"), scatter_dimension=0, tiled=True),
        lax.psum_scatter(summed[1], ("batch", "fsdp"), scatter_dimension=0, tiled=True),
        lax.psum_scatter(summed[2], ("batch", "fsdp"), scatter_dimension=0, tiled=True),
    )
    owner = lax.axis_index(("batch", "fsdp"))
    group_size = lax.axis_size(("batch", "fsdp"))
    wide_share = channel_count // group_size
    narrow_share = hidden_state // group_size
    gain_first_grad = lax.dynamic_slice_in_dim(gain_one_total, owner * wide_share, wide_share)
    shift_first_grad = lax.dynamic_slice_in_dim(shift_one_total, owner * wide_share, wide_share)
    gain_second_grad = lax.dynamic_slice_in_dim(gain_two_total, owner * narrow_share, narrow_share)
    shift_second_grad = lax.dynamic_slice_in_dim(
        shift_two_total, owner * narrow_share, narrow_share
    )
    return (
        block_out,
        input_grad,
        shares[0],
        shares[1],
        shares[2],
        gain_first_grad,
        shift_first_grad,
        gain_second_grad,
        shift_second_grad,
    )


def solution(mesh):
    return jax.shard_map(
        local,
        mesh=mesh,
        in_specs=(
            P(("batch", "fsdp"), "bins", None),
            P(("batch", "fsdp"), "bins"),
            P(("batch", "fsdp"), "bins"),
            P(("batch", "fsdp")),
            P(("batch", "fsdp"), None),
            P(("batch", "fsdp"), None),
            P(("batch", "fsdp")),
            P(("batch", "fsdp")),
            P(("batch", "fsdp")),
            P(("batch", "fsdp")),
            P(("batch", "fsdp")),
            P(("batch", "fsdp"), "bins", None),
        ),
        out_specs=(
            P(("batch", "fsdp"), "bins", None),
            P(("batch", "fsdp"), "bins", None),
            P(("batch", "fsdp"), None),
            P(("batch", "fsdp"), None),
            P(("batch", "fsdp")),
            P(("batch", "fsdp")),
            P(("batch", "fsdp")),
            P(("batch", "fsdp")),
            P(("batch", "fsdp")),
        ),
        check_vma=False,
    )
```

profile of v0, /device:TPU:0, one launch (start us, length us, event | category | flops | bytes accessed | tf_op | source)
XLA Modules:
  0.0 466.3 jit_solution(5711937940642805629)
XLA Ops:
  7.2 1.9 convert_element_type.96
  9.1 0.0 reduce-scatter.5.cloned.1.call-start
  9.2 0.8 fusion.46
  10.0 0.6 convert_reduce_fusion.1
  10.6 1.3 fusion.49
  13.2 0.7 convert_element_type.103
  13.9 0.7 convert_element_type.91
  14.6 0.7 convert_element_type.93
  15.2 0.7 convert_element_type.97
  15.9 0.7 convert_element_type.99
  16.5 0.2 dynamic-update-slice.3
  16.7 0.2 dynamic-update-slice.2
  16.9 0.2 dynamic-update-slice.1
  17.2 0.2 dynamic-update-slice.4
  17.4 0.2 dynamic-update-slice
  17.6 19.0 %all-reduce.10 = (bf16[768]{0:T(1024)(128)(2,1)S(1)}, bf16[768]{0:T(1024)(128)(2,1)S(1)}, bf16[768]{0:T(1024)(128)(2,1)S(1)}, bf16[384]{0:T(512)(128)(2,1)S(1)}, bf16[384]{0:T(512)(128)(2,1)S(1)}) all-reduce(bf16[768]{0:T(1024)(128)(2,1)S(1)} %dynamic-update-slice.4, ...), channel_id=1, replica_groups=mesh['bins'=4,'batch'=4,'fsdp'=2] {'batch','fsdp'}, use_global_device_ids=true, to_apply=%add.4 | all-reduce | flops 3072 | bytes 12288
  36.7 2.6 fusion.13
  39.3 38.0 %all-reduce.8 = (f32[768]{0:T(1024)S(1)}, f32[]{:T(128)}) all-reduce(f32[768]{0:T(1024)S(1)} %fusion.13, f32[]{:T(128)} %convert_reduce_fusion.1), channel_id=1, replica_groups=mesh['bins'=4,'batch'=4,'fsdp'=2] {'bins','batch','fsdp'}, use_global_device_ids=true, to_apply=%region_1.0 | all-reduce | flops 769 | bytes 6152 | tf_op jit(solution)/shard_map/psum | solution.py:35
  77.3 0.6 broadcast_divide_fusion
  77.9 1.1 fusion.3
  79.0 41.7 %psum.89 = f32[768]{0:T(1024)S(1)} all-reduce(f32[768]{0:T(1024)S(1)} %fusion.3), channel_id=1, replica_groups=mesh['bins'=4,'batch'=4,'fsdp'=2] {'bins','batch','fsdp'}, use_global_device_ids=true, to_apply=%region_5.0 | all-reduce | flops 768 | bytes 6144 | tf_op jit(solution)/shard_map/psum | solution.py:40
  120.6 1.2 convert_multiply_fusion.1
  121.9 2.4 fusion.12
  124.4 0.1 fusion.47
  124.5 4.2 collective-permute-start
  128.7 1.3 collective-permute-start.1
  130.0 2.3 bitcast_multiply_fusion
  132.3 15.8 %all_gather.26 = bf16[384,768]{1,0:T(8,128)(2,1)} all-gather(bf16[48,768]{1,0:T(8,128)(2,1)S(1)} %convert_element_type.102), channel_id=1, replica_groups=mesh['bins'=4,'batch'=4,'fsdp'=2] {'batch','fsdp'}, dimensions={0}, use_global_device_ids=true | all-gather | bytes 663552 | tf_op jit(solution)/shard_map/all_gather | solution.py:79
  148.2 3.6 pad_maximum_fusion.4
  151.8 9.3 %multiply_reduce_fusion.2 = (f32[384]{0:T(512)S(1)}, f32[2048,384]{1,0:T(8,128)}) fusion(f32[2048]{0:T(1024)S(1)} %bitcast.82, bf16[2304,384]{1,0:T(8,128)(2,1)} %all-gather.2.cloned.1.call-done, bf16[2048,768]{1,0:T(8,128)(2,1)} %bitcast.75, bf16[2048,768]{1,0:T(8,128)(2,1)} %bitcast.69, bf16[2048,768]{1,0:T(8,128)(2,1)} %bitcast.73), kind=kOutput, calls=%fused_computation.55 | convolution fusion | flops 3653762560 | bytes 14362112 | tf_op jit(solution)/shard_map/dot_general | solution.py:120
  161.0 39.7 %psum.90 = f32[384]{0:T(512)S(1)} all-reduce(f32[384]{0:T(512)S(1)} %get-tuple-element.45), channel_id=1, replica_groups=mesh['bins'=4,'batch'=4,'fsdp'=2] {'bins','batch','fsdp'}, use_global_device_ids=true, to_apply=%region_7.0 | all-reduce | flops 384 | bytes 3072 | tf_op jit(solution)/shard_map/psum | solution.py:35
  200.7 0.6 broadcast_divide_fusion.1
  201.4 2.3 multiply_reduce_fusion.1
  203.7 41.8 %psum.91 = f32[384]{0:T(512)S(1)} all-reduce(f32[384]{0:T(512)S(1)} %multiply_reduce_fusion.1), channel_id=1, replica_groups=mesh['bins'=4,'batch'=4,'fsdp'=2] {'bins','batch','fsdp'}, use_global_device_ids=true, to_apply=%region_9.0 | all-reduce | flops 384 | bytes 3072 | tf_op jit(solution)/shard_map/psum | solution.py:40
  245.6 0.7 convert_multiply_fusion.2
  246.2 5.5 %fusion.43 = f32[384,768]{1,0:T(8,128)} fusion(bf16[2048,768]{1,0:T(8,128)(2,1)} %bitcast_multiply_fusion, f32[2048,384]{1,0:T(8,128)} %get-tuple-element.46, f32[384]{0:T(512)S(1)} %convert_element_type.100, f32[384]{0:T(512)S(1)} %convert_element_type.98, f32[384]{0:T(512)S(1)} %get-tuple-element.31, f32[384]{0:T(512)S(1)} %broadcast_divide_fusion.1), kind=kOutput, calls=%fused_computation.73 | convolution fusion | flops 1215823872 | bytes 7477248 | tf_op jit(solution)/shard_map/dot_general | solution.py:55
  251.7 0.0 reduce-scatter.3.cloned.1.call-start
  251.8 7.8 %fusion.45 = (f32[384]{0:T(512)S(1)}, f32[384]{0:T(512)S(1)}, f32[2048,384]{1,0:T(8,128)}) fusion(f32[384]{0:T(512)S(1)} %get-tuple-element.31, f32[2048,384]{1,0:T(8,128)} %get-tuple-element.46, f32[384]{0:T(512)S(1)} %broadcast_divide_fusion.1, f32[384]{0:T(512)S(1)} %convert_element_type.100, f32[384]{0:T(512)S(1)} %convert_element_type.98, ...), kind=kOutput, calls=%fused_computation.75 | convolution fusion | flops 1220541696 | bytes 10036224 | tf_op jit(solution)/shard_map/dot_general | solution.py:133
  259.6 38.6 %all-reduce.7 = (f32[384]{0:T(512)S(1)}, f32[384]{0:T(512)S(1)}) all-reduce(f32[384]{0:T(512)S(1)} %get-tuple-element.12, f32[384]{0:T(512)S(1)} %get-tuple-element.11), channel_id=1, replica_groups=mesh['bins'=4,'batch'=4,'fsdp'=2] {'bins','batch','fsdp'}, use_global_device_ids=true, to_apply=%region_13.0 | all-reduce | flops 768 | bytes 6144 | tf_op jit(solution)/shard_map/psum | solution.py:47
  298.3 4.5 multiply_convert_fusion
  302.8 1.1 copy-done.4
  303.9 6.8 %fusion.36 = f32[2304,384]{1,0:T(8,128)} fusion(bf16[2048,384]{1,0:T(8,128)(2,1)S(1)} %multiply_convert_fusion, bf16[2048,768]{1,0:T(8,128)(2,1)} %bitcast.76, bf16[2048,768]{1,0:T(8,128)(2,1)S(1)} %bitcast.70, bf16[2048,768]{1,0:T(8,128)(2,1)S(1)} %bitcast.74), kind=kOutput, calls=%fused_computation.43 | convolution fusion | flops 3652190208 | bytes 14548992 | tf_op jit(solution)/shard_map/dot_general | solution.py:55
  310.7 0.0 all-reduce.13.cloned.1.call-start
  310.8 0.6 convert_element_type.104
  312.1 2.6 convert_reduce_fusion
  314.6 14.9 %all-reduce.5 = f32[768]{0:T(1024)S(1)} all-reduce(f32[768]{0:T(1024)S(1)} %convert_reduce_fusion), channel_id=4, replica_groups=mesh['bins'=4,'batch'=4,'fsdp'=2] {'batch','fsdp'}, use_global_device_ids=true, to_apply=%region_24.0.clone | all-reduce | flops 768 | bytes 6144
  329.5 0.1 dynamic-slice.6
  329.6 10.6 %psum.101 = f32[96]{0:T(128)} all-reduce(f32[96]{0:T(128)S(1)} %dynamic-slice.6), channel_id=1, replica_groups=mesh['bins'=4,'batch'=4,'fsdp'=2] {'bins'}, use_global_device_ids=true, to_apply=%region_23.0 | all-reduce | flops 96 | bytes 768 | tf_op jit(solution)/shard_map/psum | solution.py:173
  340.2 1.8 fusion.48
  342.0 1.3 collective-permute-start.2
  343.3 4.8 %collective-permute-start.3 = (bf16[8,26,384]{2,1,0:T(8,128)(2,1)}, bf16[8,26,384]{2,1,0:T(8,128)(2,1)S(1)}, u32[]{:S(2)}, u32[]{:S(2)}) collective-permute-start(bf16[8,26,384]{2,1,0:T(8,128)(2,1)} %get-tuple-element.39), channel_id=1, source_target_pairs={{0,8},{8,16},{16,24},{1,9},{9,17},{17,25},{2,10},{10,18},{18,26},{... | collective-permute-start | bytes 479240 | tf_op jit(solution)/shard_map/ppermute | solution.py:17
  348.1 6.4 %fusion.15 = bf16[2048,768]{1,0:T(8,128)(2,1)} fusion(bf16[8,256,768]{2,1,0:T(8,128)(2,1)S(1)} %copy-done, bf16[384,768]{1,0:T(8,128)(2,1)} %all_gather.26, f32[768]{0:T(1024)} %convert_element_type.104, f32[2048,384]{1,0:T(8,128)} %get-tuple-element.46, f32[384]{0:T(512)} %copy-done.20, f32[384]{0:T(512)} %copy-done.21, f32[384]{0:T(512)} %copy-done.17, ...), kind=kOutput, calls=%fused_computation.20 | convolution fusion | flops 1222115328 | bytes 10036224 | tf_op jit(solution)/shard_map/dot_general | solution.py:124
  354.5 1.2 dynamic_slice.15
  355.7 1.3 dynamic_slice.14
  356.9 3.8 copy.22
  360.8 3.1 pad_maximum_fusion.6
  364.0 8.4 %fusion.44 = (f32[768]{0:T(1024)S(1)}, f32[768]{0:T(1024)S(1)}, f32[2048,768]{1,0:T(8,128)}) fusion(f32[768]{0:T(1024)S(1)} %get-tuple-element.29, f32[768]{0:T(1024)S(1)} %broadcast_divide_fusion, bf16[8,256,768]{2,1,0:T(8,128)(2,1)S(1)} %copy-done, f32[768]{0:T(1024)S(1)} %copy-done.13, f32[768]{0:T(1024)S(1)} %copy-done.15, ...), kind=kOutput, calls=%fused_computation.74 | convolution fusion | flops 3664771584 | bytes 15943680 | tf_op jit(solution)/shard_map/dot_general | solution.py:161
  372.3 37.0 %all-reduce.6 = (f32[768]{0:T(1024)S(1)}, f32[768]{0:T(1024)S(1)}) all-reduce(f32[768]{0:T(1024)S(1)} %get-tuple-element.10, f32[768]{0:T(1024)S(1)} %get-tuple-element.9), channel_id=1, replica_groups=mesh['bins'=4,'batch'=4,'fsdp'=2] {'bins','batch','fsdp'}, use_global_device_ids=true, to_apply=%region_17.0 | all-reduce | flops 1536 | bytes 12288 | tf_op jit(solution)/shard_map/psum | solution.py:47
  409.4 6.9 %fusion.29 = bf16[2048,768]{1,0:T(8,128)(2,1)} fusion(f32[2048,768]{1,0:T(8,128)} %get-tuple-element.48, bf16[8,256,768]{2,1,0:T(8,128)(2,1)S(1)} %copy-done, f32[]{:T(128)} %get-tuple-element.18, f32[768]{0:T(1024)S(1)} %get-tuple-element.13, f32[768]{0:T(1024)S(1)} %get-tuple-element.14, f32[2048]{0:T(1024)S(1)} %bitcast.85, ...), kind=kLoop, calls=%fused_computation.36 | loop fusion | flops 20447232 | bytes 15756292 | tf_op jit(solution)/shard_map/convert_element_type | solution.py:169
  416.2 0.6 dynamic_slice.13
  416.8 0.6 dynamic_slice.12
  417.4 39.0 %all-reduce.13.cloned.1.call-done = (f32[288,384]{1,0:T(8,128)}, f32[48,768]{1,0:T(8,128)}) async-done(((f32[288,384]{1,0:T(8,128)}, f32[48,768]{1,0:T(8,128)}), (f32[288,384]{1,0:T(8,128)}, f32[48,768]{1,0:T(8,128)})) %all-reduce.13.cloned.1.call-update) | async-done | bytes 589840 | tf_op jit(solution)/shard_map/psum | solution.py:173
  456.4 1.8 copy.32
  458.2 1.6 copy.33
  (69 shorter events, 0.3 us)
Async XLA Ops:
  7.2 70.7 %copy-start = (bf16[8,256,768]{2,1,0:T(8,128)(2,1)S(1)}, bf16[8,256,768]{2,1,0:T(8,128)(2,1)}, u32[]{:S(2)}) copy-start(bf16[8,256,768]{2,1,0:T(8,128)(2,1)} %param.12) | copy-start | bytes 9437188
  7.2 144.6 %all-gather.2.cloned.1.call-start = ((), (), s32[]{:S(2)}) async-start(), calls=%async_computation.2 | async-start | bytes 1990656 | tf_op jit(solution)/shard_map/all_gather | solution.py:78
  9.1 400.2 %reduce-scatter.5.cloned.1.call-start = ((), (), s32[]{:S(2)}) async-start(), calls=%async_computation.4 | async-start | bytes 1327104 | tf_op jit(solution)/shard_map/reduce_scatter | solution.py:176
  36.6 85.3 %copy-start.12 = (f32[768]{0:T(1024)}, f32[768]{0:T(1024)S(1)}, u32[]{:S(2)}) copy-start(f32[768]{0:T(1024)S(1)} %convert_element_type.94) | copy-start | bytes 9220
  36.6 85.3 %copy-start.14 = (f32[768]{0:T(1024)}, f32[768]{0:T(1024)S(1)}, u32[]{:S(2)}) copy-start(f32[768]{0:T(1024)S(1)} %convert_element_type.92) | copy-start | bytes 9220
  121.9 8.1 %copy-start.1 = (bf16[8,256,768]{2,1,0:T(8,128)(2,1)S(1)}, bf16[8,256,768]{2,1,0:T(8,128)(2,1)}, u32[]{:S(2)}) copy-start(bf16[8,256,768]{2,1,0:T(8,128)(2,1)} %param.23) | copy-start | bytes 9437188
  124.3 23.8 %copy-start.2 = (bf16[8,256,768]{2,1,0:T(8,128)(2,1)}, bf16[8,256,768]{2,1,0:T(8,128)(2,1)S(1)}, u32[]{:S(2)}) copy-start(bf16[8,256,768]{2,1,0:T(8,128)(2,1)S(1)} %fusion.12) | copy-start | bytes 9437188
  124.5 23.7 %collective-permute-start = (bf16[8,26,768]{2,1,0:T(8,128)(2,1)S(1)}, bf16[8,26,768]{2,1,0:T(8,128)(2,1)S(1)}, u32[]{:S(2)}, u32[]{:S(2)}) collective-permute-start(bf16[8,26,768]{2,1,0:T(8,128)(2,1)S(1)} %get-tuple-element.34), channel_id=1, source_target_pairs={{0,8},{8,16},{16,24},{1,9},{9,17},{17,25},{2,10},{10,18},{18,26},{... | collective-permute-start | bytes 958472 | tf_op jit(solution)/shard_map/ppermute | solution.py:17
  128.7 19.5 %collective-permute-start.1 = (bf16[8,26,768]{2,1,0:T(8,128)(2,1)S(1)}, bf16[8,26,768]{2,1,0:T(8,128)(2,1)S(1)}, u32[]{:S(2)}, u32[]{:S(2)}) collective-permute-start(bf16[8,26,768]{2,1,0:T(8,128)(2,1)S(1)} %get-tuple-element.35), channel_id=1, source_target_pairs={{8,0},{16,8},{24,16},{9,1},{17,9},{25,17},{10,2},{18,10},{26,18},{... | collective-permute-start | bytes 958472 | tf_op jit(solution)/shard_map/ppermute | solution.py:20
  130.0 2.3 copy-start.9
  130.0 2.3 copy-start.8
  132.3 119.5 %copy-start.20 = (f32[384]{0:T(512)}, f32[384]{0:T(512)S(1)}, u32[]{:S(2)}) copy-start(f32[384]{0:T(512)S(1)} %convert_element_type.100) | copy-start | bytes 4612
  132.3 119.5 %copy-start.21 = (f32[384]{0:T(512)}, f32[384]{0:T(512)S(1)}, u32[]{:S(2)}) copy-start(f32[384]{0:T(512)S(1)} %convert_element_type.98) | copy-start | bytes 4612
  201.4 96.8 %copy-start.11 = (f32[384]{0:T(512)}, f32[384]{0:T(512)S(1)}, u32[]{:S(2)}) copy-start(f32[384]{0:T(512)S(1)} %broadcast_divide_fusion.1) | copy-start | bytes 4612
  246.2 52.0 %copy-start.17 = (f32[384]{0:T(512)}, f32[384]{0:T(512)S(1)}, u32[]{:S(2)}) copy-start(f32[384]{0:T(512)S(1)} %get-tuple-element.31) | copy-start | bytes 4612
  251.7 157.6 %reduce-scatter.3.cloned.1.call-start = ((), (), s32[]{:S(2)}) async-start(), calls=%async_computation.3 | async-start | bytes 3981312 | tf_op jit(solution)/shard_map/reduce_scatter | solution.py:175
  298.2 4.6 copy-start.18
  298.2 4.6 copy-start.19
  298.2 5.7 %copy-start.3 = (bf16[8,256,768]{2,1,0:T(8,128)(2,1)S(1)}, bf16[8,256,768]{2,1,0:T(8,128)(2,1)}, u32[]{:S(2)}) copy-start(bf16[8,256,768]{2,1,0:T(8,128)(2,1)} %copy-done.2) | copy-start | bytes 9437188
  298.2 5.7 %copy-start.6 = (bf16[8,256,768]{2,1,0:T(8,128)(2,1)S(1)}, bf16[8,256,768]{2,1,0:T(8,128)(2,1)}, u32[]{:S(2)}) copy-start(bf16[8,256,768]{2,1,0:T(8,128)(2,1)} %get-tuple-element.32) | copy-start | bytes 9437188
  302.8 1.1 copy-start.4
  310.7 145.6 %all-reduce.13.cloned.1.call-start = ((), (), s32[]{:S(2)}) async-start(), calls=%async_computation.5 | async-start | bytes 1179648 | tf_op jit(solution)/shard_map/psum | solution.py:173
  342.0 18.8 %collective-permute-start.2 = (bf16[8,26,384]{2,1,0:T(8,128)(2,1)}, bf16[8,26,384]{2,1,0:T(8,128)(2,1)S(1)}, u32[]{:S(2)}, u32[]{:S(2)}) collective-permute-start(bf16[8,26,384]{2,1,0:T(8,128)(2,1)} %get-tuple-element.38), channel_id=1, source_target_pairs={{8,0},{16,8},{24,16},{9,1},{17,9},{25,17},{10,2},{18,10},{26,18},{... | collective-permute-start | bytes 479240 | tf_op jit(solution)/shard_map/ppermute | solution.py:20
  343.3 17.5 %collective-permute-start.3 = (bf16[8,26,384]{2,1,0:T(8,128)(2,1)}, bf16[8,26,384]{2,1,0:T(8,128)(2,1)S(1)}, u32[]{:S(2)}, u32[]{:S(2)}) collective-permute-start(bf16[8,26,384]{2,1,0:T(8,128)(2,1)} %get-tuple-element.39), channel_id=1, source_target_pairs={{0,8},{8,16},{16,24},{1,9},{9,17},{17,25},{2,10},{10,18},{18,26},{... | collective-permute-start | bytes 479240 | tf_op jit(solution)/shard_map/ppermute | solution.py:17
  360.8 3.1 copy-start.5
  360.8 3.1 copy-start.7
  360.8 3.2 copy-start.13
  360.8 3.2 copy-start.15
  363.9 45.4 %copy-start.10 = (bf16[1,2,8,128]{3,1,2,0:T(2,128)(2,1)S(1)}, bf16[1,2,8,128]{3,1,2,0:T(2,128)(2,1)}, u32[]{:S(2)}) copy-start(bf16[1,2,8,128]{3,1,2,0:T(2,128)(2,1)} %copy-done.9) | copy-start | bytes 12292
  363.9 45.4 %copy-start.16 = (f32[768]{0:T(1024)S(1)}, f32[768]{0:T(1024)}, u32[]{:S(2)}) copy-start(f32[768]{0:T(1024)} %get-tuple-element.28) | copy-start | bytes 9220
Sparse Core Ops, SparseCore 0:
  10.2 29.7 all-gather.1
  251.9 31.9 reduce-scatter.4
  310.9 44.6 reduce-scatter.2
  409.5 46.8 all-reduce.12
where the time goes:
time: 468 us; the launch traced here: 466 us
  blocking collectives  297 us (63%)
  matrix products  44.1 us (9%)
  other arithmetic  41.7 us (9%)
  waiting for transfers between devices  39.1 us (8%)
  local copies, waits for them, and re-layouts  16.4 us (4%)
  between operations  16.2 us (3%)
  starting transfers between devices  11.7 us (2%)
    psum x2, blocking collectives, moments(): lax.psum(jnp.sum(centred * centred * valid, axis=0), ('bins', 'batch', 'f...  83.5 us
    psum x2, blocking collectives, moments(): lax.psum((jnp.sum(values * valid, axis=0), local_count), ('bins', 'batch'...  77.7 us
    psum x2, blocking collectives, norm_back(): lax.psum((jnp.sum(grad_out, axis=0), jnp.sum(grad_out * normed, axis=0)),...  75.6 us
    psum x1, waiting for transfers between devices, local(): summed = lax.psum((local_grads[0], local_grads[1], local_grads[2]), 'bins')  39 us
    unnamed x2, blocking collectives  33.9 us
    all_gather x1, blocking collectives, local(): lax.all_gather(point_weight.astype(bf), ('batch', 'fsdp'), axis=0, tiled=...  15.8 us
    dot_general x2, matrix products, contract_rows(): lax.dot_general(left, right, (((0,), (0,)), ((), ())), preferred_element_...  12.3 us
    psum x1, blocking collectives, local(): summed = lax.psum((local_grads[0], local_grads[1], local_grads[2]), 'bins')  10.6 us
  transfers between devices with their start and end apart: 8, of which 1 were waited for; matrix products, arithmetic and copies ran while one was open for 17% of the time, Pallas kernels for 0%

commit v1 on v0

v1 whole, which is shorter than its diff:
```python
import functools

import jax
import jax.numpy as jnp
from jax import lax
from jax.experimental import pallas as pl
from jax.experimental.pallas import tpu as pltpu
from jax.sharding import PartitionSpec as P

STEP = 26
EPS = 1e-5
PAD = 32
CHUNK = 32
MESH = pl.DeviceIdType.MESH
BF = jnp.bfloat16
F32 = jnp.float32


def dot(a, b, ca, cb):
    return lax.dot_general(a, b, (((ca,), (cb,)), ((), ())), preferred_element_type=F32)


def fold(v):
    rows, width = v.shape
    return jnp.sum(v.reshape(rows // 8, 8, width), axis=0)


def merge(entries):
    total = functools.reduce(jnp.add, [e[0] for e in entries])
    count = functools.reduce(jnp.add, [e[2] for e in entries])
    mean = total / jnp.maximum(count, 1.0)
    square = functools.reduce(jnp.add, [e[1] for e in entries])
    for s, _, n in entries:
        gap = s / jnp.maximum(n, 1.0) - mean
        square = square + n * gap * gap
    return total, square, count


def block(
    sizes,
    x_hbm, og_hbm, black, unmap, limit, wd, wp, par,
    out_hbm, gin_hbm, dwd, dwp, small,
    xpad, grad, vm, h1, z1, gw, h2, dz, taps, dg, stage,
    fs1, fr1, cs1, cr1, fs2, fr2, cs2, cr2, fs3, fr3, cs3, cr3, fs4, fr4, cs4, cr4,
    xsem, gsem, osem, isem, hsem, hrem, zsem, zrem, fss, frs, css, crs,
):
    nb, nz, nf = sizes
    seqs, bins, chans = grad.shape
    hid = z1.shape[2]
    wide, narrow = chans // 128, hid // 128
    pieces = bins // CHUNK
    bi, zi, fi = lax.axis_index("bins"), lax.axis_index("batch"), lax.axis_index("fsdp")

    def load_x(s):
        return pltpu.make_async_copy(x_hbm.at[s], xpad.at[s, pl.ds(PAD, bins), :], xsem.at[s])

    def load_g(s):
        return pltpu.make_async_copy(og_hbm.at[s], grad.at[s], gsem.at[s])

    for s in range(seqs):
        load_x(s).start()
    for s in range(seqs):
        load_g(s).start()

    mates = [(k,) for k in range(1, nf)]
    chips = [(b, z) for z in range(nz) for b in range(nb) if (b, z) != (0, 0)]

    def mate(k):
        return {"fsdp": lax.rem(fi + k, nf)}

    def chip(b, z):
        return {"bins": lax.rem(bi + b, nb), "batch": lax.rem(zi + z, nz)}

    barrier = pltpu.get_barrier_semaphore()
    for (k,) in mates:
        pl.semaphore_signal(barrier, inc=1, device_id=mate(k), device_id_type=MESH)
    for b, z in chips:
        pl.semaphore_signal(barrier, inc=1, device_id=chip(b, z), device_id_type=MESH)

    place = bi * bins + lax.broadcasted_iota(jnp.int32, (seqs, bins), 1)
    keep = (black[...] == 0) & (unmap[...] == 0) & (place < limit[...])
    columns = jnp.transpose(keep.astype(F32))
    tally = jnp.zeros((8, 128), F32)
    for s in range(seqs):
        lanes = jnp.broadcast_to(columns[:, s : s + 1], (bins, 128))
        vm[s] = lanes
        tally = tally + fold(lanes)
    own_count = jnp.sum(tally, axis=0, keepdims=True)

    def mask(s, r, copies):
        m = vm[s, r * CHUNK : (r + 1) * CHUNK, :]
        return jnp.concatenate([m] * copies, axis=1)

    pl.semaphore_wait(barrier, len(mates) + len(chips))

    low, high = lax.rem(bi + nb - 1, nb), lax.rem(bi + 1, nb)

    def edge_copies(src, dst, send, recv):
        to_low = pltpu.make_async_remote_copy(
            src_ref=src(0), dst_ref=dst(PAD + bins), send_sem=send.at[0], recv_sem=recv.at[0],
            device_id={"bins": low}, device_id_type=MESH,
        )
        to_high = pltpu.make_async_remote_copy(
            src_ref=src(bins - PAD), dst_ref=dst(0), send_sem=send.at[1], recv_sem=recv.at[1],
            device_id={"bins": high}, device_id_type=MESH,
        )
        return to_low, to_high

    x_low, x_high = edge_copies(
        lambda r: x_hbm.at[:, pl.ds(r, PAD), :], lambda r: xpad.at[:, pl.ds(r, PAD), :], hsem, hrem
    )

    def edge_start(to_low, to_high):
        @pl.when(bi > 0)
        def _():
            to_low.start()

        @pl.when(bi < nb - 1)
        def _():
            to_high.start()

    def edge_wait(to_low, to_high):
        @pl.when(bi < nb - 1)
        def _():
            to_low.wait_recv()
            to_high.wait_send()

        @pl.when(bi > 0)
        def _():
            to_high.wait_recv()
            to_low.wait_send()

    edge_start(x_low, x_high)

    def mate_copies(i, src, dst):
        return [
            pltpu.make_async_remote_copy(
                src_ref=src, dst_ref=dst.at[j], send_sem=fss.at[i, j], recv_sem=frs.at[i, j],
                device_id=mate(k), device_id_type=MESH,
            )
            for j, (k,) in enumerate(mates)
        ]

    def chip_copies(i, src, dst):
        return [
            pltpu.make_async_remote_copy(
                src_ref=src, dst_ref=dst.at[j], send_sem=css.at[i, j], recv_sem=crs.at[i, j],
                device_id=chip(b, z), device_id_type=MESH,
            )
            for j, (b, z) in enumerate(chips)
        ]

    def start(copies):
        for c in copies:
            c.start()

    def wait(copies):
        for c in copies:
            c.wait_recv()
        for c in copies:
            c.wait_send()

    def plain_sum(i, fs, fr, cs, cr, rows, filler):
        mine = mate_copies(i, fs, fr)
        start(mine)
        wait(mine)
        both = fs[...]
        for j in range(len(mates)):
            both = both + fr[j]
        cs[...] = both
        far = chip_copies(i, cs, cr)
        start(far)
        filler()
        wait(far)
        total = cs[...]
        for j in range(len(chips)):
            total = total + cr[j]
        return total

    def sums_x(s, acc):
        load_x(s).wait()
        for r in range(pieces):
            xx = xpad[s, PAD + r * CHUNK : PAD + (r + 1) * CHUNK, :].astype(F32)
            acc = acc + fold(xx * mask(s, r, wide))
        return acc

    acc = lax.fori_loop(0, seqs, sums_x, jnp.zeros((8, chans), F32))
    count_wide = jnp.concatenate([own_count] * wide, axis=1)
    count_narrow = jnp.concatenate([own_count] * narrow, axis=1)
    sum_one = jnp.sum(acc, axis=0, keepdims=True)
    local_one = sum_one / jnp.maximum(count_wide, 1.0)

    def squares_x(s, acc):
        for r in range(pieces):
            xx = xpad[s, PAD + r * CHUNK : PAD + (r + 1) * CHUNK, :].astype(F32) - local_one
            acc = acc + fold(xx * xx * mask(s, r, wide))
        return acc

    acc = lax.fori_loop(0, seqs, squares_x, jnp.zeros((8, chans), F32))
    fs1[0:1, :] = sum_one
    fs1[1:2, :] = jnp.sum(acc, axis=0, keepdims=True)
    fs1[2:3, :] = count_wide
    fs1[3:4, :] = count_wide

    def triple(ref):
        return ref[0:1, :], ref[1:2, :], ref[2:3, :]

    mine = mate_copies(0, fs1, fr1)
    start(mine)
    wait(mine)
    s_, q_, n_ = merge([triple(fs1)] + [triple(fr1.at[j]) for j in range(len(mates))])
    cs1[0:1, :] = s_
    cs1[1:2, :] = q_
    cs1[2:3, :] = n_
    cs1[3:4, :] = n_
    far = chip_copies(0, cs1, cr1)
    start(far)

    def mask_grad(s, acc):
        load_g(s).wait()
        for r in range(pieces):
            rows = slice(r * CHUNK, (r + 1) * CHUNK)
            g = grad[s, rows, :].astype(F32) * mask(s, r, wide)
            acc = acc + fold(g)
            grad[s, rows, :] = g.astype(BF)
        return acc

    acc = lax.fori_loop(0, seqs, mask_grad, jnp.zeros((8, chans), F32))
    own_bias = jnp.sum(acc, axis=0, keepdims=True)

    wait(far)
    s_, q_, count = merge([triple(cs1)] + [triple(cr1.at[j]) for j in range(len(chips))])
    mean_one = s_ / count
    scale_one = lax.rsqrt(q_ / count + EPS)
    gain_one = par[1:2, :] * scale_one
    shift_one = par[2:3, :]

    edge_wait(x_low, x_high)

    def first_act(s, _):
        for r in range(pieces + 2 * PAD // CHUNK):
            rows = slice(r * CHUNK, (r + 1) * CHUNK)
            v = (xpad[s, rows, :].astype(F32) - mean_one) * gain_one + shift_one
            v = 0.5 * v + (0.5 * v) * jnp.tanh(0.851 * v)
            if r * CHUNK < PAD:
                v = jnp.where(bi > 0, v, 0.0)
            if r * CHUNK >= PAD + bins:
                v = jnp.where(bi < nb - 1, v, 0.0)
            h1[s, rows, :] = v.astype(BF)
        return 0

    lax.fori_loop(0, seqs, first_act, 0)

    def conv(s, acc):
        z = None
        for k in range(3):
            first = PAD + (k - 1) * STEP
            part = dot(h1[s, first : first + bins, :], wd[k * chans : (k + 1) * chans, :], 1, 0)
            z = part if z is None else z + part
        z1[s] = z
        for r in range(pieces):
            acc = acc + fold(z1[s, r * CHUNK : (r + 1) * CHUNK, :] * mask(s, r, narrow))
        return acc

    acc = lax.fori_loop(0, seqs, conv, jnp.zeros((8, hid), F32))
    sum_two = jnp.sum(acc, axis=0, keepdims=True)
    local_two = sum_two / jnp.maximum(count_narrow, 1.0)

    def squares_z(s, acc):
        for r in range(pieces):
            z = z1[s, r * CHUNK : (r + 1) * CHUNK, :] - local_two
            acc = acc + fold(z * z * mask(s, r, narrow))
        return acc

    acc = lax.fori_loop(0, seqs, squares_z, jnp.zeros((8, hid), F32))
    fs2[0:1, :] = sum_two
    fs2[1:2, :] = jnp.sum(acc, axis=0, keepdims=True)
    fs2[2:3, :] = own_bias[:, :hid]
    fs2[3:4, :] = own_bias[:, hid:]

    def pair(ref, n):
        return ref[0:1, :], ref[1:2, :], n[2:3, :hid]

    mine = mate_copies(1, fs2, fr2)
    start(mine)
    wait(mine)
    entries = [pair(fs2, fs1)] + [pair(fr2.at[j], fr1.at[j]) for j in range(len(mates))]
    s_, q_, _ = merge(entries)
    bias_part = fs2[2:4, :]
    for j in range(len(mates)):
        bias_part = bias_part + fr2[j, 2:4, :]
    cs2[0:1, :] = s_
    cs2[1:2, :] = q_
    cs2[2:4, :] = bias_part
    far = chip_copies(1, cs2, cr2)
    start(far)

    def grad_point(s, _):
        gw[s] = dot(grad[s], wp[...], 1, 1)
        return 0

    lax.fori_loop(0, seqs, grad_point, 0)

    wait(far)
    entries = [pair(cs2, cs1)] + [pair(cr2.at[j], cr1.at[j]) for j in range(len(chips))]
    s_, q_, _ = merge(entries)
    for j in range(len(chips)):
        bias_part = bias_part + cr2[j, 2:4, :]
    small[0:1, :hid] = bias_part[0:1, :]
    small[0:1, hid:] = bias_part[1:2, :]
    mean_two = s_ / count[:, :hid]
    scale_two = lax.rsqrt(q_ / count[:, :hid] + EPS)
    gain_two = par[3:4, :hid]
    shift_two = par[3:4, hid:]

    def second_act(s, acc):
        a, b = acc
        for r in range(pieces):
            rows = slice(r * CHUNK, (r + 1) * CHUNK)
            xh = (z1[s, rows, :] - mean_two) * scale_two
            v = xh * gain_two + shift_two
            t = jnp.tanh(0.851 * v)
            h2[s, rows, :] = (0.5 * v + (0.5 * v) * t).astype(BF)
            d = gw[s, rows, :] * (0.5 + 0.5 * t + (0.4255 * v) * (1.0 - t * t))
            z1[s, rows, :] = xh
            gw[s, rows, :] = d
            a = a + fold(d)
            b = b + fold(d * xh)
        return a, b

    zero = jnp.zeros((8, hid), F32)
    a, b = lax.fori_loop(0, seqs, second_act, (zero, zero))
    fs3[0:1, :] = jnp.sum(a, axis=0, keepdims=True)
    fs3[1:2, :] = jnp.sum(b, axis=0, keepdims=True)

    def store_out(s):
        return pltpu.make_async_copy(stage.at[s], out_hbm.at[s], osem.at[s])

    def point_work():
        def branch(s, _):
            stage[s] = (
                xpad[s, PAD : PAD + bins, :].astype(F32) + dot(h2[s], wp[...], 1, 0) + par[0:1, :]
            ).astype(BF)
            store_out(s).start()
            return 0

        lax.fori_loop(0, seqs, branch, 0)
        flat = grad[...].reshape(seqs * bins, chans)
        dwp[...] = dot(h2[...].reshape(seqs * bins, hid), flat, 0, 0)

    both = plain_sum(2, fs3, fr3, cs3, cr3, 2, point_work)
    shift_total, gain_total = both[0:1, :], both[1:2, :]
    small[3:4, :hid] = gain_total
    small[3:4, hid:] = shift_total
    outer = scale_two * gain_two
    level = shift_total / count[:, :hid]
    slant = gain_total / count[:, :hid]

    def conv_grad(s, _):
        for r in range(pieces):
            rows = slice(r * CHUNK, (r + 1) * CHUNK)
            d = gw[s, rows, :] - mask(s, r, narrow) * (level + z1[s, rows, :] * slant)
            dz[s, PAD + r * CHUNK : PAD + (r + 1) * CHUNK, :] = (outer * d).astype(BF)
        return 0

    lax.fori_loop(0, seqs, conv_grad, 0)
    z_low, z_high = edge_copies(
        lambda r: dz.at[:, pl.ds(PAD + r, PAD), :], lambda r: dz.at[:, pl.ds(r, PAD), :], zsem, zrem
    )
    edge_start(z_low, z_high)

    @pl.when(bi == 0)
    def _():
        dz[:, 0:PAD, :] = jnp.zeros((seqs, PAD, hid), BF)

    @pl.when(bi == nb - 1)
    def _():
        dz[:, PAD + bins : PAD + bins + PAD, :] = jnp.zeros((seqs, PAD, hid), BF)

    edge_wait(z_low, z_high)

    def shift_taps(s, _):
        for k in range(3):
            first = PAD - (k - 1) * STEP
            taps[s, :, k * hid : (k + 1) * hid] = dz[s, first : first + bins, :]
        return 0

    lax.fori_loop(0, seqs, shift_taps, 0)

    def kernel_grad(m, _):
        cols = pl.ds(pl.multiple_of(m * 256, 256), 256)
        left = h1[:, PAD : PAD + bins, cols].reshape(seqs * bins, 256)
        for k in range(3):
            right = taps[:, :, k * hid : (k + 1) * hid].reshape(seqs * bins, hid)
            dwd[pl.ds(pl.multiple_of(k * chans + m * 256, 256), 256), :] = dot(left, right, 0, 0)
        return 0

    lax.fori_loop(0, chans // 256, kernel_grad, 0)

    def input_side(s, acc):
        a, b = acc
        d = None
        for k in range(3):
            part = dot(taps[s, :, k * hid : (k + 1) * hid], wd[k * chans : (k + 1) * chans, :], 1, 1)
            d = part if d is None else d + part
        dg[s] = d
        for r in range(pieces):
            rows = slice(r * CHUNK, (r + 1) * CHUNK)
            xc = xpad[s, PAD + r * CHUNK : PAD + (r + 1) * CHUNK, :].astype(F32) - mean_one
            v = xc * gain_one + shift_one
            t = jnp.tanh(0.851 * v)
            d = dg[s, rows, :] * (0.5 + 0.5 * t + (0.4255 * v) * (1.0 - t * t))
            dg[s, rows, :] = d
            a = a + fold(d)
            b = b + fold(d * (xc * scale_one))
        return a, b

    zero = jnp.zeros((8, chans), F32)
    a, b = lax.fori_loop(0, seqs, input_side, (zero, zero))
    fs4[0:1, :] = jnp.sum(a, axis=0, keepdims=True)
    fs4[1:2, :] = jnp.sum(b, axis=0, keepdims=True)
    both = plain_sum(3, fs4, fr4, cs4, cr4, 2, lambda: None)
    shift_total, gain_total = both[0:1, :], both[1:2, :]
    small[1:2, :] = gain_total
    small[2:3, :] = shift_total
    level = shift_total / count
    slant = gain_total / count

    def store_in(s):
        return pltpu.make_async_copy(grad.at[s], gin_hbm.at[s], isem.at[s])

    def input_grad(s, _):
        for r in range(pieces):
            rows = slice(r * CHUNK, (r + 1) * CHUNK)
            xc = xpad[s, PAD + r * CHUNK : PAD + (r + 1) * CHUNK, :].astype(F32) - mean_one
            d = dg[s, rows, :] - mask(s, r, wide) * (level + (xc * scale_one) * slant)
            grad[s, rows, :] = (grad[s, rows, :].astype(F32) + gain_one * d).astype(BF)
        store_in(s).start()
        return 0

    lax.fori_loop(0, seqs, input_grad, 0)

    def drain(s, _):
        store_out(s).wait()
        store_in(s).wait()
        return 0

    lax.fori_loop(0, seqs, drain, 0)


def local(sizes, x, black, unmap, limit, wd, wp, bias, g1, s1, g2, s2, og):
    nb, nz, nf = sizes
    seqs, bins, chans = x.shape
    hid = wd.shape[1]
    groups = ("batch", "fsdp")
    wd_all = lax.all_gather(wd.astype(BF), groups, axis=0, tiled=True)
    wp_all = lax.all_gather(wp.astype(BF), groups, axis=0, tiled=True)
    packed = jnp.concatenate([bias, g1, s1, g2, s2]).astype(BF)
    spread = lax.all_gather(packed, groups, axis=0).astype(F32)
    wide, narrow = bias.shape[0], g2.shape[0]
    rows = [spread[:, k * wide : (k + 1) * wide].reshape(1, chans) for k in range(3)]
    rest = [
        spread[:, 3 * wide + k * narrow : 3 * wide + (k + 1) * narrow].reshape(1, hid)
        for k in range(2)
    ]
    par = jnp.concatenate(rows + [jnp.concatenate(rest, axis=1)] * 5, axis=0)
    near, far = nf - 1, nb * nz - 1
    vmem = pl.BlockSpec(memory_space=pltpu.VMEM)
    hbm = pl.BlockSpec(memory_space=pl.ANY)
    dma = pltpu.SemaphoreType.DMA

    def sums(rows, width):
        return [
            pltpu.VMEM((rows, width), F32),
            pltpu.VMEM((near, rows, width), F32),
            pltpu.VMEM((rows, width), F32),
            pltpu.VMEM((far, rows, width), F32),
        ]

    tall = bins + 2 * PAD
    out, gin, dwd, dwp, small = pl.pallas_call(
        functools.partial(block, sizes),
        out_shape=(
            jax.ShapeDtypeStruct(x.shape, BF),
            jax.ShapeDtypeStruct(x.shape, BF),
            jax.ShapeDtypeStruct((3 * chans, hid), F32),
            jax.ShapeDtypeStruct((hid, chans), F32),
            jax.ShapeDtypeStruct((8, chans), F32),
        ),
        in_specs=[hbm, hbm] + [vmem] * 6,
        out_specs=(hbm, hbm, vmem, vmem, vmem),
        scratch_shapes=[
            pltpu.VMEM((seqs, tall, chans), BF),
            pltpu.VMEM((seqs, bins, chans), BF),
            pltpu.VMEM((seqs, bins, 128), F32),
            pltpu.VMEM((seqs, tall, chans), BF),
            pltpu.VMEM((seqs, bins, hid), F32),
            pltpu.VMEM((seqs, bins, hid), F32),
            pltpu.VMEM((seqs, bins, hid), BF),
            pltpu.VMEM((seqs, tall, hid), BF),
            pltpu.VMEM((seqs, bins, 3 * hid), BF),
            pltpu.VMEM((seqs, bins, chans), F32),
            pltpu.VMEM((seqs, bins, chans), BF),
        ]
        + sums(4, chans) + sums(4, hid) + sums(2, hid) + sums(2, chans)
        + [
            dma((seqs,)), dma((seqs,)), dma((seqs,)), dma((seqs,)),
            dma((2,)), dma((2,)), dma((2,)), dma((2,)),
            dma((4, near)), dma((4, near)), dma((4, far)), dma((4, far)),
        ],
        compiler_params=pltpu.CompilerParams(
            collective_id=0, has_side_effects=True, vmem_limit_bytes=60 * 2**20
        ),
    )(x, og, black, unmap, limit.reshape(seqs, 1), wd_all, wp_all, par)
    summed = lax.psum((dwd, dwp), "bins")
    owner = lax.axis_index(groups)

    def own(row, width):
        return lax.dynamic_slice_in_dim(row, owner * width, width)

    return (
        out,
        gin,
        lax.psum_scatter(summed[0], groups, scatter_dimension=0, tiled=True),
        lax.psum_scatter(summed[1], groups, scatter_dimension=0, tiled=True),
        own(small[0], wide),
        own(small[1], wide),
        own(small[2], wide),
        own(small[3, :hid], narrow),
        own(small[3, hid:], narrow),
    )


def solution(mesh):
    sizes = (mesh.shape["bins"], mesh.shape["batch"], mesh.shape["fsdp"])
    rows = P(("batch", "fsdp"))
    track = P(("batch", "fsdp"), "bins", None)
    table = P(("batch", "fsdp"), None)
    return jax.shard_map(
        functools.partial(local, sizes),
        mesh=mesh,
        in_specs=(track, P(("batch", "fsdp"), "bins"), P(("batch", "fsdp"), "bins"), rows,
                  table, table, rows, rows, rows, rows, rows, track),
        out_specs=(track, track, table, table, rows, rows, rows, rows, rows),
        check_vma=False,
    )
```

time: 468 us -> 272 us (0.58)
  blocking collectives: 297 us -> 32.3 us
  Pallas kernels: 0 us -> 88.5 us
  waiting for transfers between devices: 39.1 us -> 121 us
  matrix products: 44.1 us -> 0 us
  other arithmetic: 41.7 us -> 4.67 us
  starting transfers between devices: 11.7 us -> 0.16 us
  local copies, waits for them, and re-layouts: 16.4 us -> 11.7 us
    psum x7 -> x0, blocking collectives: 247 us -> none  [the longest x2 83.5 us: moments(): lax.psum(jnp.sum(centred * centred * valid, axis=0), ('bins', 'batch', 'f...]
    pallas_call x0 -> x1, Pallas kernels: none -> 88.5 us  [local(): pl.pallas_call(functools.partial(block, sizes), out_shape=(jax.ShapeDtype...]
    reduce_scatter x2, waiting for transfers between devices: 0.01 us -> 74.8 us  [the longest x1 44.5 us: local(): lax.psum_scatter(summed[0], groups, scatter_dimension=0, tiled=True)]
    dot_general x6 -> x0, matrix products: 44.1 us -> none  [the longest x2 12.3 us: contract_rows(): lax.dot_general(left, right, (((0,), (0,)), ((), ())), preferred_element_...]
    unnamed x2 -> x0, blocking collectives: 33.9 us -> none
    convert_element_type x16 -> x2, other arithmetic: 20.4 us -> 2.65 us  [the longest x1 1.72 us: local(): wd_all = lax.all_gather(wd.astype(BF), groups, axis=0, tiled=True)]
    all_gather x1 -> x2, blocking collectives: 15.8 us -> 32.3 us  [the longest x1 17.8 us: local(): wp_all = lax.all_gather(wp.astype(BF), groups, axis=0, tiled=True)]
    ppermute x4 -> x0, starting transfers between devices: 11.6 us -> none  [the longest x2 8.98 us: extended(): lax.ppermute(lax.slice_in_dim(block, block.shape[dim] - width, None, axis...]
  transfers between devices with their start and end apart: 8 -> 4, of which waited for: 1 -> 3; matrix products, arithmetic and copies ran while one was open for 17% -> 3% of each run, Pallas kernels for 0% -> 0%
where the time goes in v1:
time: 272 us
  waiting for transfers between devices  121 us (44%)
  Pallas kernels  88.5 us (33%)
  blocking collectives  32.3 us (12%)
  between operations  13.8 us (5%)
  local copies, waits for them, and re-layouts  11.7 us (4%)
  other arithmetic  4.67 us (2%)
    pallas_call x1, Pallas kernels, local(): pl.pallas_call(functools.partial(block, sizes), out_shape=(jax.ShapeDtype...  88.5 us
    psum x1, waiting for transfers between devices, local(): summed = lax.psum((dwd, dwp), 'bins')  45.5 us
    reduce_scatter x1, waiting for transfers between devices, local(): lax.psum_scatter(summed[0], groups, scatter_dimension=0, tiled=True)  44.5 us
    reduce_scatter x1, waiting for transfers between devices, local(): lax.psum_scatter(summed[1], groups, scatter_dimension=0, tiled=True)  30.3 us
    all_gather x1, blocking collectives, local(): wp_all = lax.all_gather(wp.astype(BF), groups, axis=0, tiled=True)  17.8 us
    all_gather x1, blocking collectives, local(): spread = lax.all_gather(packed, groups, axis=0).astype(F32)  14.5 us
    unnamed x15, local copies, waits for them, and re-layouts  6.13 us
  transfers between devices with their start and end apart: 4, of which 3 were waited for; matrix products, arithmetic and copies ran while one was open for 3% of the time, Pallas kernels for 0%

profile of v1, /device:TPU:0, one launch (start us, length us, event | category | flops | bytes accessed | tf_op | source)
XLA Modules:
  0.0 272.1 jit_solution(15503263213466903153)
XLA Ops:
  7.2 0.0 all-gather.3.cloned.1.call-start
  7.2 1.7 convert_element_type.17
  8.9 0.0 all-gather.3.cloned.1.call-update
  9.0 0.0 reduce-scatter.5.cloned.1.call-start
  9.0 0.7 convert_bitcast_fusion.4
  9.7 0.7 convert_bitcast_fusion
  10.4 0.7 convert_bitcast_fusion.2
  11.0 0.1 concatenate.32
  11.1 14.5 %all-gather = bf16[8,1,384]{2,1,0:T(2,128)(2,1)S(1)} all-gather(bf16[1,1,384]{2,1,0:T(2,128)(2,1)S(1)} %bitcast.27), channel_id=1, replica_groups=mesh['bins'=4,'batch'=4,'fsdp'=2] {'batch','fsdp'}, dimensions={0}, use_global_device_ids=true | all-gather | bytes 6912 | tf_op jit(solution)/shard_map/all_gather | solution.py:459
  25.6 0.1 fusion.7
  25.7 0.1 reshape.118
  25.7 0.1 reshape.119
  25.8 0.1 fusion.8
  25.9 0.1 reshape.115
  26.0 0.1 reshape.116
  26.1 0.1 reshape.117
  26.1 0.9 convert_element_type.18
  27.1 1.3 copy.22.limit
  28.4 0.7 concatenate.34.par
  29.1 17.8 %all_gather.11.wp = bf16[384,768]{1,0:T(8,128)(2,1)} all-gather(bf16[48,768]{1,0:T(8,128)(2,1)S(1)} %convert_element_type.18), channel_id=1, replica_groups=mesh['bins'=4,'batch'=4,'fsdp'=2] {'batch','fsdp'}, dimensions={0}, use_global_device_ids=true | all-gather | bytes 663552 | tf_op jit(solution)/shard_map/all_gather | solution.py:457
  46.9 0.0 all-gather.3.cloned.1.call-done.wd
  46.9 88.5 %shard_map.187 = (bf16[8,256,768]{2,1,0:T(8,128)(2,1)}, bf16[8,256,768]{2,1,0:T(8,128)(2,1)}, f32[2304,384]{1,0:T(8,128)}, f32[384,768]{1,0:T(8,128)}, f32[8,768]{1,0:T(8,128)}) custom-call(bf16[8,256,768]{2,1,0:T(8,128)(2,1)} %x_hbm.1, bf16[8,256,768]{2,1,0:T(8,128)(2,1)} %og_hbm.1, s32[8,256]{1,0:T(8,128)} %black.1, s32[8,256]{1,0:T(8,128)} %unmap.1, ...), custom_call_target="tpu_custom_call" | custom-call | tf_op jit(solution)/shard_map/pallas_call | solution.py:481
  135.3 0.0 copy-start.4
  135.4 0.0 copy-start.1
  135.4 0.0 reduce-scatter.5.cloned.1.call-update
  135.4 0.0 reduce-scatter.3.cloned.1.call-start
  135.4 0.7 reduce-scatter.3.cloned.1.call-update
  136.1 0.0 all-reduce.3.cloned.1.call-start
  136.2 0.0 copy-done.4
  136.2 0.6 fusion
  136.8 30.3 %reduce-scatter.5.cloned.1.call-done = f32[48,768]{1,0:T(8,128)} async-done(((f32[384,768]{1,0:T(8,128)}), f32[48,768]{1,0:T(8,128)}) %reduce-scatter.5.cloned.1.call-update) | async-done | bytes 147472 | tf_op jit(solution)/shard_map/reduce_scatter | solution.py:525
  167.1 44.5 %reduce-scatter.3.cloned.1.call-done = f32[288,384]{1,0:T(8,128)} async-done(((f32[2304,384]{1,0:T(8,128)}), f32[288,384]{1,0:T(8,128)}) %reduce-scatter.3.cloned.1.call-update) | async-done | bytes 442384 | tf_op jit(solution)/shard_map/reduce_scatter | solution.py:524
  211.6 0.0 all-reduce.3.cloned.1.call-update
  211.6 0.6 fusion.1
  212.2 0.6 fusion.2
  212.8 0.6 fusion.3
  213.3 0.6 fusion.4
  213.9 45.5 %all-reduce.3.cloned.1.call-done = (f32[288,384]{1,0:T(8,128)}, f32[48,768]{1,0:T(8,128)}) async-done(((f32[288,384]{1,0:T(8,128)}, f32[48,768]{1,0:T(8,128)}), (f32[288,384]{1,0:T(8,128)}, f32[48,768]{1,0:T(8,128)})) %all-reduce.3.cloned.1.call-update) | async-done | bytes 589840 | tf_op jit(solution)/shard_map/psum | solution.py:515
  259.5 0.0 copy-done.1
  259.5 0.0 copy-start
  259.5 1.7 copy.30
  261.1 1.4 copy-done
  262.5 0.0 copy-start.2
  262.5 0.0 copy-start.3
  262.5 1.7 copy.31
  264.2 0.0 copy-done.2
  264.2 0.8 copy.32
  264.9 0.0 copy-done.3
  264.9 0.7 copy.33
  (4 shorter events, 0.0 us)
Async XLA Ops:
  7.2 39.7 %all-gather.3.cloned.1.call-start = ((), (), s32[]{:S(2)}) async-start(), calls=%async_computation.2 | async-start | bytes 1990656 | tf_op jit(solution)/shard_map/all_gather | solution.py:456
  9.0 158.1 %reduce-scatter.5.cloned.1.call-start = ((), (), s32[]{:S(2)}) async-start(), calls=%async_computation.4 | async-start | bytes 1327104 | tf_op jit(solution)/shard_map/reduce_scatter | solution.py:525
  135.3 0.8 copy-start.4
  135.4 124.1 %copy-start.1 = (bf16[8,256,768]{2,1,0:T(8,128)(2,1)S(1)}, bf16[8,256,768]{2,1,0:T(8,128)(2,1)}, u32[]{:S(2)}) copy-start(bf16[8,256,768]{2,1,0:T(8,128)(2,1)} %get-tuple-element.44) | copy-start | bytes 9437188
  135.4 76.2 %reduce-scatter.3.cloned.1.call-start = ((), (), s32[]{:S(2)}) async-start(), calls=%async_computation.3 | async-start | bytes 3981312 | tf_op jit(solution)/shard_map/reduce_scatter | solution.py:524
  136.1 123.3 %all-reduce.3.cloned.1.call-start = ((), (), s32[]{:S(2)}) async-start(), calls=%async_computation.5 | async-start | bytes 1179648 | tf_op jit(solution)/shard_map/psum | solution.py:515
  259.5 3.0 %copy-start = (bf16[8,256,768]{2,1,0:T(8,128)(2,1)S(1)}, bf16[8,256,768]{2,1,0:T(8,128)(2,1)}, u32[]{:S(2)}) copy-start(bf16[8,256,768]{2,1,0:T(8,128)(2,1)} %get-tuple-element.45) | copy-start | bytes 9437188
  262.5 1.7 copy-start.2
  262.5 2.4 copy-start.3
Sparse Core Ops, SparseCore 0:
  10.2 32.9 all-gather.2
  135.5 31.5 reduce-scatter.4
  169.4 42.0 reduce-scatter.2
  214.7 44.6 all-reduce.2

commit v2 on v1

--- a/solution.py
+++ b/solution.py
@@ -38,13 +38,16 @@
 
 def block(
     sizes,
-    x_hbm, og_hbm, black, unmap, limit, wd, wp, par,
-    out_hbm, gin_hbm, dwd, dwp, small,
-    xpad, grad, vm, h1, z1, gw, h2, dz, taps, dg, stage,
+    x_hbm, og_hbm, black_hbm, unmap_hbm, limit, wd_hbm, wp_hbm, bias_in, g1_in, s1_in, g2_in, s2_in,
+    out_hbm, gin_hbm, dwd, dwp, bias_out, g1_out, s1_out, g2_out, s2_out,
+    xin, grad, vm, h1, z1, gw, h2, dz, taps, dg, stage,
     fs1, fr1, cs1, cr1, fs2, fr2, cs2, cr2, fs3, fr3, cs3, cr3, fs4, fr4, cs4, cr4,
-    xsem, gsem, osem, isem, hsem, hrem, zsem, zrem, fss, frs, css, crs,
+    black, unmap, wd_own, wp_own, wd, wp, wall, pall, par, es, er,
+    xsem, gsem, osem, isem, lsem, hsem, hrem, zsem, zrem, fss, frs, css, crs,
+    wzs, wzr, wcs, wcr, wfs, wfr, pzs, pzr, pfs, pfr,
 ):
     nb, nz, nf = sizes
+    inside = wall is not None
     seqs, bins, chans = grad.shape
     hid = z1.shape[2]
     wide, narrow = chans // 128, hid // 128
@@ -52,15 +55,17 @@
     bi, zi, fi = lax.axis_index("bins"), lax.axis_index("batch"), lax.axis_index("fsdp")
 
     def load_x(s):
-        return pltpu.make_async_copy(x_hbm.at[s], xpad.at[s, pl.ds(PAD, bins), :], xsem.at[s])
+        return pltpu.make_async_copy(x_hbm.at[s], xin.at[s], xsem.at[s])
 
     def load_g(s):
         return pltpu.make_async_copy(og_hbm.at[s], grad.at[s], gsem.at[s])
 
-    for s in range(seqs):
-        load_x(s).start()
-    for s in range(seqs):
-        load_g(s).start()
+    small_loads = [
+        pltpu.make_async_copy(src, dst, lsem.at[i])
+        for i, (src, dst) in enumerate(
+            [(black_hbm, black), (unmap_hbm, unmap), (wd_hbm, wd_own), (wp_hbm, wp_own)]
+        )
+    ]
 
     mates = [(k,) for k in range(1, nf)]
     chips = [(b, z) for z in range(nz) for b in range(nb) if (b, z) != (0, 0)]
@@ -77,8 +82,23 @@
     for b, z in chips:
         pl.semaphore_signal(barrier, inc=1, device_id=chip(b, z), device_id_type=MESH)
 
+    small_loads[0].start()
+    small_loads[1].start()
+    for s in range(seqs):
+        load_x(s).start()
+    small_loads[2].start()
+    small_loads[3].start()
+    for s in range(seqs):
+        load_g(s).start()
+
+    small_loads[0].wait()
+    small_loads[1].wait()
+    ends = jnp.zeros((seqs, bins), jnp.int32)
+    for s in range(seqs):
+        row = lax.broadcasted_iota(jnp.int32, (seqs, bins), 0)
+        ends = jnp.where(row == s, limit[s], ends)
     place = bi * bins + lax.broadcasted_iota(jnp.int32, (seqs, bins), 1)
-    keep = (black[...] == 0) & (unmap[...] == 0) & (place < limit[...])
+    keep = (black[...] == 0) & (unmap[...] == 0) & (place < ends)
     columns = jnp.transpose(keep.astype(F32))
     tally = jnp.zeros((8, 128), F32)
     for s in range(seqs):
@@ -91,24 +111,18 @@
         m = vm[s, r * CHUNK : (r + 1) * CHUNK, :]
         return jnp.concatenate([m] * copies, axis=1)
 
-    pl.semaphore_wait(barrier, len(mates) + len(chips))
-
     low, high = lax.rem(bi + nb - 1, nb), lax.rem(bi + 1, nb)
 
-    def edge_copies(src, dst, send, recv):
+    def edge_copies(low_src, low_dst, high_src, high_dst, send, recv):
         to_low = pltpu.make_async_remote_copy(
-            src_ref=src(0), dst_ref=dst(PAD + bins), send_sem=send.at[0], recv_sem=recv.at[0],
+            src_ref=low_src, dst_ref=low_dst, send_sem=send.at[0], recv_sem=recv.at[0],
             device_id={"bins": low}, device_id_type=MESH,
         )
         to_high = pltpu.make_async_remote_copy(
-            src_ref=src(bins - PAD), dst_ref=dst(0), send_sem=send.at[1], recv_sem=recv.at[1],
+            src_ref=high_src, dst_ref=high_dst, send_sem=send.at[1], recv_sem=recv.at[1],
             device_id={"bins": high}, device_id_type=MESH,
         )
         return to_low, to_high
-
-    x_low, x_high = edge_copies(
-        lambda r: x_hbm.at[:, pl.ds(r, PAD), :], lambda r: xpad.at[:, pl.ds(r, PAD), :], hsem, hrem
-    )
 
     def edge_start(to_low, to_high):
         @pl.when(bi > 0)
@@ -129,8 +143,6 @@
         def _():
             to_high.wait_recv()
             to_low.wait_send()
-
-    edge_start(x_low, x_high)
 
     def mate_copies(i, src, dst):
         return [
@@ -177,10 +189,74 @@
             total = total + cr[j]
         return total
 
+    own = zi * nf + fi
+    pall[own] = jnp.zeros((8, 128), F32)
+    for r, ref in enumerate((bias_in, g1_in, s1_in, g2_in, s2_in)):
+        n = ref.shape[0]
+        pall[own, r : r + 1, 0:n] = ref[...].astype(BF).astype(F32).reshape(1, n)
+    small_loads[2].wait()
+    small_loads[3].wait()
+    share = wp_own.shape[0]
+    if inside:
+        base = wd_own.shape[0]
+        piece = (base + 2 * share) // nb
+        wall[own, 0:base, :] = wd_own[...].astype(BF)
+        wall[own, base : base + share, :] = wp_own[:, 0:hid].astype(BF)
+        wall[own, base + share : base + 2 * share, :] = wp_own[:, hid:].astype(BF)
+
+    def before(i, k, n):
+        return lax.rem(i + n - k, n)
+
+    def send(ref, ssem, rsem, where):
+        return pltpu.make_async_remote_copy(
+            src_ref=ref, dst_ref=ref, send_sem=ssem, recv_sem=rsem,
+            device_id=where, device_id_type=MESH,
+        )
+
+    def along(k):
+        return {"batch": lax.rem(zi + k, nz)}
+
+    def slot(z, f):
+        return z * nf + f
+
+    par_far = [send(pall.at[own], pzs.at[k], pzr.at[k], along(k)) for k in range(1, nz)]
+    par_near = [
+        [
+            send(pall.at[slot(before(zi, k, nz), fi)], pfs.at[j, k], pfr.at[j, k], mate(m))
+            for j, (m,) in enumerate(mates)
+        ]
+        for k in range(nz)
+    ]
+
+    def part(k, b):
+        rows = pl.ds(pl.multiple_of(before(bi, b, nb) * piece, 16), piece)
+        return wall.at[slot(before(zi, k, nz), fi), rows, :]
+
+    if inside:
+        w_far = [send(part(0, 0), wzs.at[k], wzr.at[k], along(k)) for k in range(1, nz)]
+        w_side = [
+            [
+                send(part(k, 0), wcs.at[k, b], wcr.at[k, b], {"bins": lax.rem(bi + b, nb)})
+                for b in range(1, nb)
+            ]
+            for k in range(1, nz)
+        ]
+        w_own = [
+            send(wall.at[own], wfs.at[j, 0, 0], wfr.at[j, 0, 0], mate(m))
+            for j, (m,) in enumerate(mates)
+        ]
+        w_near = [
+            [
+                [send(part(k, b), wfs.at[j, k, b], wfr.at[j, k, b], mate(m)) for j, (m,) in enumerate(mates)]
+                for b in range(nb)
+            ]
+            for k in range(1, nz)
+        ]
+
     def sums_x(s, acc):
         load_x(s).wait()
         for r in range(pieces):
-            xx = xpad[s, PAD + r * CHUNK : PAD + (r + 1) * CHUNK, :].astype(F32)
+            xx = xin[s, r * CHUNK : (r + 1) * CHUNK, :].astype(F32)
             acc = acc + fold(xx * mask(s, r, wide))
         return acc
 
@@ -192,7 +268,7 @@
 
     def squares_x(s, acc):
         for r in range(pieces):
-            xx = xpad[s, PAD + r * CHUNK : PAD + (r + 1) * CHUNK, :].astype(F32) - local_one
+            xx = xin[s, r * CHUNK : (r + 1) * CHUNK, :].astype(F32) - local_one
             acc = acc + fold(xx * xx * mask(s, r, wide))
         return acc
 
@@ -205,8 +281,14 @@
     def triple(ref):
         return ref[0:1, :], ref[1:2, :], ref[2:3, :]
 
+    pl.semaphore_wait(barrier, len(mates) + len(chips))
     mine = mate_copies(0, fs1, fr1)
     start(mine)
+    start(par_far)
+    start(par_near[0])
+    if inside:
+        start(w_far)
+        start(w_own)
     wait(mine)
     s_, q_, n_ = merge([triple(fs1)] + [triple(fr1.at[j]) for j in range(len(mates))])
     cs1[0:1, :] = s_
@@ -228,6 +310,36 @@
     acc = lax.fori_loop(0, seqs, mask_grad, jnp.zeros((8, chans), F32))
     own_bias = jnp.sum(acc, axis=0, keepdims=True)
 
+    for k in range(1, nz):
+        par_far[k - 1].wait_recv()
+        start(par_near[k])
+        if inside:
+            w_far[k - 1].wait_recv()
+            start(w_side[k - 1])
+            start(w_near[k - 1][0])
+    for k in range(nz):
+        for c in par_near[k]:
+            c.wait_recv()
+
+    rows = jnp.zeros((8, chans + 256), F32)
+    cols = jnp.zeros((8, hid + 256), F32)
+
+    def laid(into, tile, width, index):
+        at = index * width
+        first, turn = at // 128 * 128, at % 128
+        tile = jnp.concatenate([tile, jnp.zeros((8, 128), F32)], axis=1)
+        tile = pltpu.roll(tile, turn, 1) if turn else tile
+        return jnp.concatenate(
+            [t for t in (into[:, :first], into[:, first : first + 256] + tile, into[:, first + 256 :]) if t.shape[1]],
+            axis=1,
+        )
+
+    for c in range(nz * nf):
+        rows = laid(rows, pall[c], bias_in.shape[0], c)
+        cols = laid(cols, pall[c], g2_in.shape[0], c)
+    par[0:3, :] = rows[0:3, :chans]
+    par[3:5, 0:hid] = cols[3:5, :hid]
+
     wait(far)
     s_, q_, count = merge([triple(cs1)] + [triple(cr1.at[j]) for j in range(len(chips))])
     mean_one = s_ / count
@@ -235,34 +347,70 @@
     gain_one = par[1:2, :] * scale_one
     shift_one = par[2:3, :]
 
-    edge_wait(x_low, x_high)
+    h1[:, 0:PAD, :] = jnp.zeros((seqs, PAD, chans), BF)
+    h1[:, PAD + bins : PAD + bins + PAD, :] = jnp.zeros((seqs, PAD, chans), BF)
 
     def first_act(s, _):
-        for r in range(pieces + 2 * PAD // CHUNK):
-            rows = slice(r * CHUNK, (r + 1) * CHUNK)
-            v = (xpad[s, rows, :].astype(F32) - mean_one) * gain_one + shift_one
-            v = 0.5 * v + (0.5 * v) * jnp.tanh(0.851 * v)
-            if r * CHUNK < PAD:
-                v = jnp.where(bi > 0, v, 0.0)
-            if r * CHUNK >= PAD + bins:
-                v = jnp.where(bi < nb - 1, v, 0.0)
-            h1[s, rows, :] = v.astype(BF)
+        for r in range(pieces):
+            rows = slice(PAD + r * CHUNK, PAD + (r + 1) * CHUNK)
+            v = (xin[s, r * CHUNK : (r + 1) * CHUNK, :].astype(F32) - mean_one) * gain_one + shift_one
+            h1[s, rows, :] = (0.5 * v + (0.5 * v) * jnp.tanh(0.851 * v)).astype(BF)
         return 0
 
     lax.fori_loop(0, seqs, first_act, 0)
 
-    def conv(s, acc):
+    if inside:
+        for k in range(1, nz):
+            for b in range(1, nb):
+                w_side[k - 1][b - 1].wait_recv()
+                start(w_near[k - 1][b])
+        for c in w_own:
+            c.wait_recv()
+        for k in range(1, nz):
+            for b in range(nb):
+                for c in w_near[k - 1][b]:
+                    c.wait_recv()
+        for c in range(nz * nf):
+            wd[c * base : (c + 1) * base, :] = wall[c, 0:base, :]
+            wp[c * share : (c + 1) * share, 0:hid] = wall[c, base : base + share, :]
+            wp[c * share : (c + 1) * share, hid:] = wall[c, base + share : base + 2 * share, :]
+
+    def tap(k):
+        return wd[k * chans : (k + 1) * chans, :]
+
+    over = h1[:, PAD + bins - STEP : PAD + bins - STEP + PAD, :].reshape(seqs * PAD, chans)
+    es[1] = dot(over, tap(0), 1, 0).astype(BF).reshape(seqs, PAD, hid)
+    under = h1[:, STEP : STEP + PAD, :].reshape(seqs * PAD, chans)
+    es[0] = dot(under, tap(2), 1, 0).astype(BF).reshape(seqs, PAD, hid)
+    e_low, e_high = edge_copies(es.at[0], er.at[0], es.at[1], er.at[1], hsem, hrem)
+    edge_start(e_low, e_high)
+
+    def conv(s, _):
         z = None
         for k in range(3):
             first = PAD + (k - 1) * STEP
-            part = dot(h1[s, first : first + bins, :], wd[k * chans : (k + 1) * chans, :], 1, 0)
+            part = dot(h1[s, first : first + bins, :], tap(k), 1, 0)
             z = part if z is None else z + part
         z1[s] = z
+        return 0
+
+    lax.fori_loop(0, seqs, conv, 0)
+    edge_wait(e_low, e_high)
+
+    @pl.when(bi > 0)
+    def _():
+        z1[:, 0:PAD, :] = z1[:, 0:PAD, :] + er[1].astype(F32)
+
+    @pl.when(bi < nb - 1)
+    def _():
+        z1[:, bins - PAD :, :] = z1[:, bins - PAD :, :] + er[0].astype(F32)
+
+    def sums_z(s, acc):
         for r in range(pieces):
             acc = acc + fold(z1[s, r * CHUNK : (r + 1) * CHUNK, :] * mask(s, r, narrow))
         return acc
 
-    acc = lax.fori_loop(0, seqs, conv, jnp.zeros((8, hid), F32))
+    acc = lax.fori_loop(0, seqs, sums_z, jnp.zeros((8, hid), F32))
     sum_two = jnp.sum(acc, axis=0, keepdims=True)
     local_two = sum_two / jnp.maximum(count_narrow, 1.0)
 
@@ -306,12 +454,25 @@
     s_, q_, _ = merge(entries)
     for j in range(len(chips)):
         bias_part = bias_part + cr2[j, 2:4, :]
-    small[0:1, :hid] = bias_part[0:1, :]
-    small[0:1, hid:] = bias_part[1:2, :]
+    bias_total = jnp.concatenate([bias_part[0:1, :], bias_part[1:2, :]], axis=1)
+
+    def owned(out, row):
+        n = out.shape[0]
+        row = jnp.concatenate([row, jnp.zeros((1, 256), F32)], axis=1)
+        row = jnp.broadcast_to(row, (8, row.shape[1]))
+        mine = jnp.zeros((8, 128), F32)
+        for c in range(nz * nf):
+            first, turn = c * n // 128 * 128, c * n % 128
+            tile = row[:, first : first + 256]
+            tile = (pltpu.roll(tile, 256 - turn, 1) if turn else tile)[:, :128]
+            mine = jnp.where(own == c, tile, mine)
+        out[...] = mine[0:1, 0:n].reshape(n)
+
+    owned(bias_out, bias_total)
     mean_two = s_ / count[:, :hid]
     scale_two = lax.rsqrt(q_ / count[:, :hid] + EPS)
     gain_two = par[3:4, :hid]
-    shift_two = par[3:4, hid:]
+    shift_two = par[4:5, :hid]
 
     def second_act(s, acc):
         a, b = acc
@@ -339,7 +500,7 @@
     def point_work():
         def branch(s, _):
             stage[s] = (
-                xpad[s, PAD : PAD + bins, :].astype(F32) + dot(h2[s], wp[...], 1, 0) + par[0:1, :]
+                xin[s].astype(F32) + dot(h2[s], wp[...], 1, 0) + par[0:1, :]
             ).astype(BF)
             store_out(s).start()
             return 0
@@ -350,8 +511,8 @@
 
     both = plain_sum(2, fs3, fr3, cs3, cr3, 2, point_work)
     shift_total, gain_total = both[0:1, :], both[1:2, :]
-    small[3:4, :hid] = gain_total
-    small[3:4, hid:] = shift_total
+    owned(g2_out, gain_total)
+    owned(s2_out, shift_total)
     outer = scale_two * gain_two
     level = shift_total / count[:, :hid]
     slant = gain_total / count[:, :hid]
@@ -365,7 +526,8 @@
 
     lax.fori_loop(0, seqs, conv_grad, 0)
     z_low, z_high = edge_copies(
-        lambda r: dz.at[:, pl.ds(PAD + r, PAD), :], lambda r: dz.at[:, pl.ds(r, PAD), :], zsem, zrem
+        dz.at[:, pl.ds(PAD, PAD), :], dz.at[:, pl.ds(PAD + bins, PAD), :],
+        dz.at[:, pl.ds(bins, PAD), :], dz.at[:, pl.ds(0, PAD), :], zsem, zrem,
     )
     edge_start(z_low, z_high)
 
@@ -406,7 +568,7 @@
         dg[s] = d
         for r in range(pieces):
             rows = slice(r * CHUNK, (r + 1) * CHUNK)
-            xc = xpad[s, PAD + r * CHUNK : PAD + (r + 1) * CHUNK, :].astype(F32) - mean_one
+            xc = xin[s, r * CHUNK : (r + 1) * CHUNK, :].astype(F32) - mean_one
             v = xc * gain_one + shift_one
             t = jnp.tanh(0.851 * v)
             d = dg[s, rows, :] * (0.5 + 0.5 * t + (0.4255 * v) * (1.0 - t * t))
@@ -421,8 +583,8 @@
     fs4[1:2, :] = jnp.sum(b, axis=0, keepdims=True)
     both = plain_sum(3, fs4, fr4, cs4, cr4, 2, lambda: None)
     shift_total, gain_total = both[0:1, :], both[1:2, :]
-    small[1:2, :] = gain_total
-    small[2:3, :] = shift_total
+    owned(g1_out, gain_total)
+    owned(s1_out, shift_total)
     level = shift_total / count
     slant = gain_total / count
 
@@ -432,7 +594,7 @@
     def input_grad(s, _):
         for r in range(pieces):
             rows = slice(r * CHUNK, (r + 1) * CHUNK)
-            xc = xpad[s, PAD + r * CHUNK : PAD + (r + 1) * CHUNK, :].astype(F32) - mean_one
+            xc = xin[s, r * CHUNK : (r + 1) * CHUNK, :].astype(F32) - mean_one
             d = dg[s, rows, :] - mask(s, r, wide) * (level + (xc * scale_one) * slant)
             grad[s, rows, :] = (grad[s, rows, :].astype(F32) + gain_one * d).astype(BF)
         store_in(s).start()
@@ -446,6 +608,28 @@
         return 0
 
     lax.fori_loop(0, seqs, drain, 0)
+    for c in par_far:
+        c.wait_send()
+    for k in range(nz):
+        for c in par_near[k]:
+            c.wait_send()
+    if inside:
+        for c in w_far + w_own:
+            c.wait_send()
+        for k in range(1, nz):
+            for c in w_side[k - 1]:
+                c.wait_send()
+            for b in range(nb):
+                for c in w_near[k - 1][b]:
+                    c.wait_send()
+
+
+def call(sizes, inside, *refs):
+    refs = list(refs)
+    if not inside:
+        first = 21 + 11 + 16 + 2
+        refs[first + 2 : first + 2] = [refs[first], refs[first + 1], None]
+    block(sizes, *refs)
 
 
 def local(sizes, x, black, unmap, limit, wd, wp, bias, g1, s1, g2, s2, og):
@@ -453,17 +637,15 @@
     seqs, bins, chans = x.shape
     hid = wd.shape[1]
     groups = ("batch", "fsdp")
-    wd_all = lax.all_gather(wd.astype(BF), groups, axis=0, tiled=True)
-    wp_all = lax.all_gather(wp.astype(BF), groups, axis=0, tiled=True)
-    packed = jnp.concatenate([bias, g1, s1, g2, s2]).astype(BF)
-    spread = lax.all_gather(packed, groups, axis=0).astype(F32)
-    wide, narrow = bias.shape[0], g2.shape[0]
-    rows = [spread[:, k * wide : (k + 1) * wide].reshape(1, chans) for k in range(3)]
-    rest = [
-        spread[:, 3 * wide + k * narrow : 3 * wide + (k + 1) * narrow].reshape(1, hid)
-        for k in range(2)
-    ]
-    par = jnp.concatenate(rows + [jnp.concatenate(rest, axis=1)] * 5, axis=0)
+    inside = (
+        wd.shape[0] % 16 == 0
+        and wp.shape[0] % 16 == 0
+        and (wd.shape[0] + 2 * wp.shape[0]) % (16 * nb) == 0
+        and chans == 2 * hid
+    )
+    if not inside:
+        wd = lax.all_gather(wd.astype(BF), groups, axis=0, tiled=True)
+        wp = lax.all_gather(wp.astype(BF), groups, axis=0, tiled=True)
     near, far = nf - 1, nb * nz - 1
     vmem = pl.BlockSpec(memory_space=pltpu.VMEM)
     hbm = pl.BlockSpec(memory_space=pl.ANY)
@@ -478,19 +660,36 @@
         ]
 
     tall = bins + 2 * PAD
-    out, gin, dwd, dwp, small = pl.pallas_call(
-        functools.partial(block, sizes),
+    scratch = [
+        pltpu.VMEM(black.shape, jnp.int32),
+        pltpu.VMEM(black.shape, jnp.int32),
+        pltpu.VMEM(wd.shape, wd.dtype),
+        pltpu.VMEM(wp.shape, wp.dtype),
+        pltpu.VMEM((3 * chans, hid), BF) if inside else None,
+        pltpu.VMEM((hid, chans), BF) if inside else None,
+        pltpu.VMEM((nz * nf, wd.shape[0] + 2 * wp.shape[0], hid), BF) if inside else None,
+        pltpu.VMEM((nz * nf, 8, 128), F32),
+        pltpu.VMEM((8, chans), F32),
+        pltpu.VMEM((2, seqs, PAD, hid), BF),
+        pltpu.VMEM((2, seqs, PAD, hid), BF),
+    ]
+    out, gin, dwd, dwp, bias_grad, g1_grad, s1_grad, g2_grad, s2_grad = pl.pallas_call(
+        functools.partial(call, sizes, inside),
         out_shape=(
             jax.ShapeDtypeStruct(x.shape, BF),
             jax.ShapeDtypeStruct(x.shape, BF),
             jax.ShapeDtypeStruct((3 * chans, hid), F32),
             jax.ShapeDtypeStruct((hid, chans), F32),
-            jax.ShapeDtypeStruct((8, chans), F32),
+            jax.ShapeDtypeStruct(bias.shape, F32),
+            jax.ShapeDtypeStruct(bias.shape, F32),
+            jax.ShapeDtypeStruct(bias.shape, F32),
+            jax.ShapeDtypeStruct(g2.shape, F32),
+            jax.ShapeDtypeStruct(g2.shape, F32),
         ),
-        in_specs=[hbm, hbm] + [vmem] * 6,
-        out_specs=(hbm, hbm, vmem, vmem, vmem),
+        in_specs=[hbm] * 4 + [pl.BlockSpec(memory_space=pltpu.SMEM)] + [hbm] * 2 + [vmem] * 5,
+        out_specs=(hbm, hbm) + (vmem,) * 7,
         scratch_shapes=[
-            pltpu.VMEM((seqs, tall, chans), BF),
+            pltpu.VMEM((seqs, bins, chans), BF),
             pltpu.VMEM((seqs, bins, chans), BF),
             pltpu.VMEM((seqs, bins, 128), F32),
             pltpu.VMEM((seqs, tall, chans), BF),
@@ -503,31 +702,30 @@
             pltpu.VMEM((seqs, bins, chans), BF),
         ]
         + sums(4, chans) + sums(4, hid) + sums(2, hid) + sums(2, chans)
+        + [m for m in scratch if m is not None]
         + [
-            dma((seqs,)), dma((seqs,)), dma((seqs,)), dma((seqs,)),
+            dma((seqs,)), dma((seqs,)), dma((seqs,)), dma((seqs,)), dma((4,)),
             dma((2,)), dma((2,)), dma((2,)), dma((2,)),
             dma((4, near)), dma((4, near)), dma((4, far)), dma((4, far)),
+            dma((nz,)), dma((nz,)), dma((nz, nb)), dma((nz, nb)),
+            dma((near, nz, nb)), dma((near, nz, nb)),
+            dma((nz,)), dma((nz,)), dma((near, nz)), dma((near, nz)),
         ],
         compiler_params=pltpu.CompilerParams(
             collective_id=0, has_side_effects=True, vmem_limit_bytes=60 * 2**20
         ),
-    )(x, og, black, unmap, limit.reshape(seqs, 1), wd_all, wp_all, par)
+    )(x, og, black, unmap, limit, wd, wp, bias, g1, s1, g2, s2)
     summed = lax.psum((dwd, dwp), "bins")
-    owner = lax.axis_index(groups)
-
-    def own(row, width):
-        return lax.dynamic_slice_in_dim(row, owner * width, width)
-
     return (
         out,
         gin,
         lax.psum_scatter(summed[0], groups, scatter_dimension=0, tiled=True),
         lax.psum_scatter(summed[1], groups, scatter_dimension=0, tiled=True),
-        own(small[0], wide),
-        own(small[1], wide),
-        own(small[2], wide),
-        own(small[3, :hid], narrow),
-        own(small[3, hid:], narrow),
+        bias_grad,
+        g1_grad,
+        s1_grad,
+        g2_grad,
+        s2_grad,
     )
 
 

time: 272 us -> 239 us (0.88)
  blocking collectives: 32.3 us -> 0 us
  other arithmetic: 4.67 us -> 0 us
  Pallas kernels: 88.5 us -> 92.2 us
  local copies, waits for them, and re-layouts: 11.7 us -> 8.7 us
  waiting for transfers between devices: 121 us -> 124 us
    all_gather x2 -> x0, blocking collectives: 32.3 us -> none  [the longest x1 17.8 us: local(): wp_all = lax.all_gather(wp.astype(BF), groups, axis=0, tiled=True)]
    pallas_call x1, Pallas kernels: 88.5 us -> 92.2 us  [local(): pl.pallas_call(functools.partial(call, sizes, inside), out_shape=(jax.Sha...]
    dynamic_slice x5 -> x0, local copies, waits for them, and re-layouts: 2.92 us -> none  [own(): return lax.dynamic_slice_in_dim(row, owner * width, width)]
    unnamed x15 -> x27, local copies, waits for them, and re-layouts: 6.13 us -> 8.7 us
  transfers between devices with their start and end apart: 4 -> 3, of which waited for: 3 -> 3; matrix products, arithmetic and copies ran while one was open for 3% -> 0% of each run, Pallas kernels for 0% -> 0%
where the time goes in v2:
time: 239 us
  waiting for transfers between devices  124 us (52%)
  Pallas kernels  92.2 us (39%)
  between operations  13.8 us (6%)
  local copies, waits for them, and re-layouts  8.7 us (4%)
    pallas_call x1, Pallas kernels, local(): pl.pallas_call(functools.partial(call, sizes, inside), out_shape=(jax.Sha...  92.2 us
    psum x1, waiting for transfers between devices, local(): summed = lax.psum((dwd, dwp), 'bins')  48 us
    reduce_scatter x1, waiting for transfers between devices, local(): lax.psum_scatter(summed[0], groups, scatter_dimension=0, tiled=True)  44.5 us
    reduce_scatter x1, waiting for transfers between devices, local(): lax.psum_scatter(summed[1], groups, scatter_dimension=0, tiled=True)  30.8 us
    unnamed x27, local copies, waits for them, and re-layouts  8.7 us
  transfers between devices with their start and end apart: 3, of which 3 were waited for; matrix products, arithmetic and copies ran while one was open for 0% of the time, Pallas kernels for 0%

profile of v2, /device:TPU:0, one launch (start us, length us, event | category | flops | bytes accessed | tf_op | source)
XLA Modules:
  0.0 239.0 jit_solution(9245267782395987490)
XLA Ops:
  7.2 0.0 reduce-scatter.5.cloned.1.call-start
  7.2 92.2 %shard_map.187 = (bf16[8,256,768]{2,1,0:T(8,128)(2,1)}, bf16[8,256,768]{2,1,0:T(8,128)(2,1)}, f32[2304,384]{1,0:T(8,128)}, f32[384,768]{1,0:T(8,128)}, f32[96]{0...) custom-call(bf16[8,256,768]{2,1,0:T(8,128)(2,1)} %refs_0_.1, bf16[8,256,768]{2,1,0:T(8,128)(2,1)} %refs_1_.1, ...), custom_call_target="tpu_custom_call" | custom-call | tf_op jit(solution)/shard_map/pallas_call | solution.py:676
  99.5 0.0 copy-start.1
  99.5 0.0 reduce-scatter.5.cloned.1.call-update
  99.5 0.0 reduce-scatter.3.cloned.1.call-start
  99.6 0.7 reduce-scatter.3.cloned.1.call-update
  100.3 0.0 all-reduce.3.cloned.1.call-start
  100.3 30.8 %reduce-scatter.5.cloned.1.call-done = f32[48,768]{1,0:T(8,128)} async-done(((f32[384,768]{1,0:T(8,128)}), f32[48,768]{1,0:T(8,128)}) %reduce-scatter.5.cloned.1.call-update) | async-done | bytes 147472 | tf_op jit(solution)/shard_map/reduce_scatter | solution.py:723
  131.1 44.5 %reduce-scatter.3.cloned.1.call-done = f32[288,384]{1,0:T(8,128)} async-done(((f32[2304,384]{1,0:T(8,128)}), f32[288,384]{1,0:T(8,128)}) %reduce-scatter.3.cloned.1.call-update) | async-done | bytes 442384 | tf_op jit(solution)/shard_map/reduce_scatter | solution.py:722
  175.7 0.0 all-reduce.3.cloned.1.call-update
  175.7 48.0 %all-reduce.3.cloned.1.call-done = (f32[288,384]{1,0:T(8,128)}, f32[48,768]{1,0:T(8,128)}) async-done(((f32[288,384]{1,0:T(8,128)}, f32[48,768]{1,0:T(8,128)}), (f32[288,384]{1,0:T(8,128)}, f32[48,768]{1,0:T(8,128)})) %all-reduce.3.cloned.1.call-update) | async-done | bytes 589840 | tf_op jit(solution)/shard_map/psum | solution.py:718
  223.7 0.0 copy-done.1
  223.7 0.0 copy-start
  223.7 1.7 copy.30
  225.4 1.4 copy-done
  226.7 0.0 copy-start.2
  226.8 0.0 copy-start.3
  226.8 0.0 copy-start.8
  226.8 0.0 copy-start.7
  226.8 0.0 copy-start.6
  226.8 0.0 copy-start.5
  226.8 0.0 copy-start.4
  226.8 1.7 copy.31
  228.5 0.0 copy-done.2
  228.5 0.8 copy.32
  229.2 0.0 copy-done.3
  229.2 0.7 copy.33
  229.9 0.0 copy-done.8
  229.9 0.5 copy.34
  230.4 0.0 copy-done.7
  230.4 0.5 copy.35
  230.9 0.0 copy-done.6
  230.9 0.5 copy.36
  231.4 0.0 copy-done.5
  231.4 0.5 copy.37
  231.9 0.0 copy-done.4
  231.9 0.5 copy.38
Async XLA Ops:
  7.2 123.9 %reduce-scatter.5.cloned.1.call-start = ((), (), s32[]{:S(2)}) async-start(), calls=%async_computation.3 | async-start | bytes 1327104 | tf_op jit(solution)/shard_map/reduce_scatter | solution.py:723
  99.5 124.2 %copy-start.1 = (bf16[8,256,768]{2,1,0:T(8,128)(2,1)S(1)}, bf16[8,256,768]{2,1,0:T(8,128)(2,1)}, u32[]{:S(2)}) copy-start(bf16[8,256,768]{2,1,0:T(8,128)(2,1)} %get-tuple-element.38) | copy-start | bytes 9437188
  99.5 76.1 %reduce-scatter.3.cloned.1.call-start = ((), (), s32[]{:S(2)}) async-start(), calls=%async_computation.2 | async-start | bytes 3981312 | tf_op jit(solution)/shard_map/reduce_scatter | solution.py:722
  100.3 123.4 %all-reduce.3.cloned.1.call-start = ((), (), s32[]{:S(2)}) async-start(), calls=%async_computation.4 | async-start | bytes 1179648 | tf_op jit(solution)/shard_map/psum | solution.py:718
  223.7 3.0 %copy-start = (bf16[8,256,768]{2,1,0:T(8,128)(2,1)S(1)}, bf16[8,256,768]{2,1,0:T(8,128)(2,1)}, u32[]{:S(2)}) copy-start(bf16[8,256,768]{2,1,0:T(8,128)(2,1)} %get-tuple-element.39) | copy-start | bytes 9437188
  226.7 1.7 copy-start.2
  226.8 2.5 %copy-start.3 = (f32[48,768]{1,0:T(8,128)S(1)}, f32[48,768]{1,0:T(8,128)}, u32[]{:S(2)}) copy-start(f32[48,768]{1,0:T(8,128)} %get-tuple-element.41) | copy-start | bytes 442372
  226.8 3.1 %copy-start.8 = (f32[96]{0:T(128)S(1)}, f32[96]{0:T(128)}, u32[]{:S(2)}) copy-start(f32[96]{0:T(128)} %get-tuple-element.42) | copy-start | bytes 1156
  226.8 3.6 %copy-start.7 = (f32[96]{0:T(128)S(1)}, f32[96]{0:T(128)}, u32[]{:S(2)}) copy-start(f32[96]{0:T(128)} %get-tuple-element.43) | copy-start | bytes 1156
  226.8 4.2 %copy-start.6 = (f32[96]{0:T(128)S(1)}, f32[96]{0:T(128)}, u32[]{:S(2)}) copy-start(f32[96]{0:T(128)} %get-tuple-element.44) | copy-start | bytes 1156
  226.8 4.7 %copy-start.5 = (f32[48]{0:T(128)S(1)}, f32[48]{0:T(128)}, u32[]{:S(2)}) copy-start(f32[48]{0:T(128)} %get-tuple-element.45) | copy-start | bytes 580
  226.8 5.2 %copy-start.4 = (f32[48]{0:T(128)S(1)}, f32[48]{0:T(128)}, u32[]{:S(2)}) copy-start(f32[48]{0:T(128)} %get-tuple-element.46) | copy-start | bytes 580
Sparse Core Ops, SparseCore 0:
  99.6 31.4 reduce-scatter.4
  133.5 42.1 reduce-scatter.2
  179.0 44.7 all-reduce.2

commit v3 on v2

--- a/solution.py
+++ b/solution.py
@@ -39,12 +39,14 @@
 def block(
     sizes,
     x_hbm, og_hbm, black_hbm, unmap_hbm, limit, wd_hbm, wp_hbm, bias_in, g1_in, s1_in, g2_in, s2_in,
-    out_hbm, gin_hbm, dwd, dwp, bias_out, g1_out, s1_out, g2_out, s2_out,
-    xin, grad, vm, h1, z1, gw, h2, dz, taps, dg, stage,
+    out_hbm, gin_hbm, dwd_out, dwp_out, bias_out, g1_out, s1_out, g2_out, s2_out,
+    xin, grad, vm, h1, z1, gw, h2, dz, taps, dg, stage, upper, lower, mcol,
     fs1, fr1, cs1, cr1, fs2, fr2, cs2, cr2, fs3, fr3, cs3, cr3, fs4, fr4, cs4, cr4,
-    black, unmap, wd_own, wp_own, wd, wp, wall, pall, par, es, er,
+    black, unmap, wd_own, wp_own, pall, par, es, er,
+    wd, wp, wall, dwd, dwp, dwd_red, dwp_red,
     xsem, gsem, osem, isem, lsem, hsem, hrem, zsem, zrem, fss, frs, css, crs,
     wzs, wzr, wcs, wcr, wfs, wfr, pzs, pzr, pfs, pfr,
+    rfs, rfr, rxs, rxr, rzs, rzr, ras, rar,
 ):
     nb, nz, nf = sizes
     inside = wall is not None
@@ -76,6 +78,10 @@
     def chip(b, z):
         return {"bins": lax.rem(bi + b, nb), "batch": lax.rem(zi + z, nz)}
 
+    upper[...] = jnp.zeros_like(upper)
+    lower[...] = jnp.zeros_like(lower)
+    dz[:, 0:PAD, :] = jnp.zeros((seqs, PAD, hid), BF)
+    dz[:, PAD + bins : PAD + bins + PAD, :] = jnp.zeros((seqs, PAD, hid), BF)
     barrier = pltpu.get_barrier_semaphore()
     for (k,) in mates:
         pl.semaphore_signal(barrier, inc=1, device_id=mate(k), device_id_type=MESH)
@@ -172,7 +178,7 @@
         for c in copies:
             c.wait_send()
 
-    def plain_sum(i, fs, fr, cs, cr, rows, filler):
+    def plain_sum(i, fs, fr, cs, cr, filler):
         mine = mate_copies(i, fs, fr)
         start(mine)
         wait(mine)
@@ -207,11 +213,14 @@
     def before(i, k, n):
         return lax.rem(i + n - k, n)
 
-    def send(ref, ssem, rsem, where):
+    def send_to(src, dst, ssem, rsem, where):
         return pltpu.make_async_remote_copy(
-            src_ref=ref, dst_ref=ref, send_sem=ssem, recv_sem=rsem,
+            src_ref=src, dst_ref=dst, send_sem=ssem, recv_sem=rsem,
             device_id=where, device_id_type=MESH,
         )
+
+    def send(ref, ssem, rsem, where):
+        return send_to(ref, ref, ssem, rsem, where)
 
     def along(k):
         return {"batch": lax.rem(zi + k, nz)}
@@ -253,6 +262,94 @@
             for k in range(1, nz)
         ]
 
+    def reduction(i, bufs, get):
+        fs, fr, xs, xr, acc, zs, zr, ga = bufs
+        other = lax.rem(fi + 1, 2)
+
+        def f_copy(d):
+            return send_to(fs.at[d], fr.at[d], rfs.at[i, d], rfr.at[i, d], mate(1))
+
+        def x_copy(d, b):
+            j = lax.rem(bi + b, nb)
+            return send_to(
+                xs.at[d, j], xr.at[b - 1, d], rxs.at[i, b - 1, d], rxr.at[i, b - 1, d], {"bins": j}
+            )
+
+        def z_copy(d):
+            return send_to(zs.at[d - 1], zr.at[d - 1], rzs.at[i, d], rzr.at[i, d], along(d))
+
+        def a_copy(b):
+            return send_to(
+                ga.at[bi], ga.at[bi], ras.at[i, b], rar.at[i, b], {"bins": lax.rem(bi + b, nb)}
+            )
+
+        def f_send(d):
+            z = lax.rem(zi + d, nz)
+            for j in range(nb):
+                fs[d, j] = get(slot(z, other), j).astype(BF)
+            f_copy(d).start()
+
+        def x_send(d):
+            z = lax.rem(zi + d, nz)
+            f_copy(d).wait_recv()
+            for j in range(nb):
+                xs[d, j] = (get(slot(z, fi), j) + fr[d, j].astype(F32)).astype(BF)
+            acc[d] = get(slot(z, fi), bi) + fr[d, bi].astype(F32)
+            for b in range(1, nb):
+                x_copy(d, b).start()
+
+        def z_send(d):
+            total = acc[d]
+            for b in range(1, nb):
+                x_copy(d, b).wait_recv()
+                total = total + xr[b - 1, d].astype(F32)
+            if d:
+                zs[d - 1] = total.astype(BF)
+                z_copy(d).start()
+            else:
+                acc[0] = total
+
+        def a_send(more=None):
+            total = acc[0] if more is None else acc[0] + more
+            for d in range(1, nz):
+                z_copy(d).wait_recv()
+                total = total + zr[d - 1].astype(F32)
+            ga[bi] = total.astype(BF)
+            for b in range(1, nb):
+                a_copy(b).start()
+
+        def finish(put):
+            for b in range(1, nb):
+                a_copy(b).wait_recv()
+            for j in range(nb):
+                put(j, ga[j].astype(F32))
+            for d in range(nz):
+                f_copy(d).wait_send()
+                for b in range(1, nb):
+                    x_copy(d, b).wait_send()
+                if d:
+                    z_copy(d).wait_send()
+            for b in range(1, nb):
+                a_copy(b).wait_send()
+
+        return f_send, x_send, z_send, a_send, finish
+
+    far_first = list(range(1, nz)) + [0]
+    if inside:
+        tall, small = base // nb, 2 * share // nb
+
+        def dwd_get(c, j):
+            return dwd[pl.ds(pl.multiple_of(c * base + j * tall, 8), tall), :]
+
+        def dwp_get(c, j):
+            rows = pl.ds(pl.multiple_of(c * share + lax.rem(j, 2) * small, 8), small)
+            if isinstance(j, int):
+                return dwp[rows, j // 2 * hid : (j // 2 + 1) * hid]
+            return dwp[rows, pl.ds(pl.multiple_of(j // 2 * hid, 128), hid)]
+
+        wide_f, wide_x, wide_z, wide_a, wide_end = reduction(0, dwd_red, dwd_get)
+        point_f, point_x, point_z, point_a, point_end = reduction(1, dwp_red, dwp_get)
+
     def sums_x(s, acc):
         load_x(s).wait()
         for r in range(pieces):
@@ -350,14 +447,17 @@
     h1[:, 0:PAD, :] = jnp.zeros((seqs, PAD, chans), BF)
     h1[:, PAD + bins : PAD + bins + PAD, :] = jnp.zeros((seqs, PAD, chans), BF)
 
-    def first_act(s, _):
+    def first_act(s, acc):
         for r in range(pieces):
             rows = slice(PAD + r * CHUNK, PAD + (r + 1) * CHUNK)
             v = (xin[s, r * CHUNK : (r + 1) * CHUNK, :].astype(F32) - mean_one) * gain_one + shift_one
-            h1[s, rows, :] = (0.5 * v + (0.5 * v) * jnp.tanh(0.851 * v)).astype(BF)
-        return 0
-
-    lax.fori_loop(0, seqs, first_act, 0)
+            v = 0.5 * v + (0.5 * v) * jnp.tanh(0.851 * v)
+            h1[s, rows, :] = v.astype(BF)
+            acc = acc + fold(v)
+        return acc
+
+    acc = lax.fori_loop(0, seqs, first_act, jnp.zeros((8, chans), F32))
+    act_sum = jnp.sum(acc, axis=0, keepdims=True)
 
     if inside:
         for k in range(1, nz):
@@ -493,6 +593,8 @@
     a, b = lax.fori_loop(0, seqs, second_act, (zero, zero))
     fs3[0:1, :] = jnp.sum(a, axis=0, keepdims=True)
     fs3[1:2, :] = jnp.sum(b, axis=0, keepdims=True)
+    fs3[2:3, :] = act_sum[:, :hid]
+    fs3[3:4, :] = act_sum[:, hid:]
 
     def store_out(s):
         return pltpu.make_async_copy(stage.at[s], out_hbm.at[s], osem.at[s])
@@ -509,37 +611,46 @@
         flat = grad[...].reshape(seqs * bins, chans)
         dwp[...] = dot(h2[...].reshape(seqs * bins, hid), flat, 0, 0)
 
-    both = plain_sum(2, fs3, fr3, cs3, cr3, 2, point_work)
+    both = plain_sum(2, fs3, fr3, cs3, cr3, point_work)
     shift_total, gain_total = both[0:1, :], both[1:2, :]
     owned(g2_out, gain_total)
     owned(s2_out, shift_total)
+    if inside:
+        for d in far_first:
+            point_f(d)
     outer = scale_two * gain_two
     level = shift_total / count[:, :hid]
     slant = gain_total / count[:, :hid]
 
-    def conv_grad(s, _):
+    typical = jnp.concatenate([both[2:3, :], both[3:4, :]], axis=1) / (nb * nz * nf * seqs * bins)
+    typical = jnp.concatenate([typical, jnp.zeros((7, chans), F32)], axis=0)
+    middle_act = lax.dot_general(
+        typical, jnp.ones((8, 128), F32), (((0,), (0,)), ((), ())),
+        precision=lax.Precision.HIGHEST, preferred_element_type=F32,
+    )
+    for k in range(3):
+        mcol[k * chans : (k + 1) * chans, :] = middle_act
+
+    def conv_grad(s, acc):
         for r in range(pieces):
             rows = slice(r * CHUNK, (r + 1) * CHUNK)
-            d = gw[s, rows, :] - mask(s, r, narrow) * (level + z1[s, rows, :] * slant)
-            dz[s, PAD + r * CHUNK : PAD + (r + 1) * CHUNK, :] = (outer * d).astype(BF)
-        return 0
-
-    lax.fori_loop(0, seqs, conv_grad, 0)
+            d = outer * (gw[s, rows, :] - mask(s, r, narrow) * (level + z1[s, rows, :] * slant))
+            dz[s, PAD + r * CHUNK : PAD + (r + 1) * CHUNK, :] = d.astype(BF)
+            acc = acc + fold(d)
+        return acc
+
+    acc = lax.fori_loop(0, seqs, conv_grad, jnp.zeros((8, hid), F32))
+    dz_sum = jnp.sum(acc, axis=0, keepdims=True)
+
+    def rank_one(first, count, row):
+        m = mcol[pl.ds(pl.multiple_of(first, 8), count), :]
+        return jnp.concatenate([m] * narrow, axis=1) * row
+
     z_low, z_high = edge_copies(
-        dz.at[:, pl.ds(PAD, PAD), :], dz.at[:, pl.ds(PAD + bins, PAD), :],
-        dz.at[:, pl.ds(bins, PAD), :], dz.at[:, pl.ds(0, PAD), :], zsem, zrem,
+        dz.at[:, pl.ds(PAD, PAD), :], upper.at[:, pl.ds(PAD, PAD), :],
+        dz.at[:, pl.ds(bins, PAD), :], lower.at[:, pl.ds(0, PAD), :], zsem, zrem,
     )
     edge_start(z_low, z_high)
-
-    @pl.when(bi == 0)
-    def _():
-        dz[:, 0:PAD, :] = jnp.zeros((seqs, PAD, hid), BF)
-
-    @pl.when(bi == nb - 1)
-    def _():
-        dz[:, PAD + bins : PAD + bins + PAD, :] = jnp.zeros((seqs, PAD, hid), BF)
-
-    edge_wait(z_low, z_high)
 
     def shift_taps(s, _):
         for k in range(3):
@@ -548,23 +659,57 @@
         return 0
 
     lax.fori_loop(0, seqs, shift_taps, 0)
+    if inside:
+        for d in far_first:
+            point_x(d)
 
     def kernel_grad(m, _):
         cols = pl.ds(pl.multiple_of(m * 256, 256), 256)
         left = h1[:, PAD : PAD + bins, cols].reshape(seqs * bins, 256)
         for k in range(3):
             right = taps[:, :, k * hid : (k + 1) * hid].reshape(seqs * bins, hid)
-            dwd[pl.ds(pl.multiple_of(k * chans + m * 256, 256), 256), :] = dot(left, right, 0, 0)
+            g = dot(left, right, 0, 0)
+            if inside:
+                g = g - rank_one(m * 256, 256, dz_sum)
+            dwd[pl.ds(pl.multiple_of(k * chans + m * 256, 256), 256), :] = g
         return 0
 
     lax.fori_loop(0, chans // 256, kernel_grad, 0)
+
+    def middle(s, _):
+        dg[s] = dot(taps[s, :, hid : 2 * hid], tap(1), 1, 1)
+        return 0
+
+    lax.fori_loop(0, seqs, middle, 0)
+
+    edge_wait(z_low, z_high)
+    after = upper[:, STEP : STEP + PAD, :]
+    ahead = lower[:, PAD - STEP : 2 * PAD - STEP, :]
+    taps[:, bins - PAD :, 0:hid] = taps[:, bins - PAD :, 0:hid] + after
+    taps[:, 0:PAD, 2 * hid :] = taps[:, 0:PAD, 2 * hid :] + ahead
+    after = after.reshape(seqs * PAD, hid)
+    ahead = ahead.reshape(seqs * PAD, hid)
+
+    def kernel_edge(m, _):
+        cols = pl.ds(pl.multiple_of(m * 256, 256), 256)
+        for k, rows, right in ((0, bins, after), (2, PAD, ahead)):
+            left = h1[:, rows : rows + PAD, cols].reshape(seqs * PAD, 256)
+            where = pl.ds(pl.multiple_of(k * chans + m * 256, 256), 256)
+            dwd[where, :] = dwd[where, :] + dot(left, right, 0, 0)
+        return 0
+
+    lax.fori_loop(0, chans // 256, kernel_edge, 0)
+    if inside:
+        for d in far_first:
+            wide_f(d)
+        for d in far_first:
+            point_z(d)
 
     def input_side(s, acc):
         a, b = acc
-        d = None
-        for k in range(3):
-            part = dot(taps[s, :, k * hid : (k + 1) * hid], wd[k * chans : (k + 1) * chans, :], 1, 1)
-            d = part if d is None else d + part
+        d = dg[s]
+        for k in (0, 2):
+            d = d + dot(taps[s, :, k * hid : (k + 1) * hid], tap(k), 1, 1)
         dg[s] = d
         for r in range(pieces):
             rows = slice(r * CHUNK, (r + 1) * CHUNK)
@@ -578,10 +723,25 @@
         return a, b
 
     zero = jnp.zeros((8, chans), F32)
-    a, b = lax.fori_loop(0, seqs, input_side, (zero, zero))
+    a, b = lax.fori_loop(0, seqs // 2, input_side, (zero, zero))
+    if inside:
+        for d in far_first:
+            wide_x(d)
+    a, b = lax.fori_loop(seqs // 2, seqs, input_side, (a, b))
     fs4[0:1, :] = jnp.sum(a, axis=0, keepdims=True)
     fs4[1:2, :] = jnp.sum(b, axis=0, keepdims=True)
-    both = plain_sum(3, fs4, fr4, cs4, cr4, 2, lambda: None)
+    fs4[2:3, :] = jnp.concatenate([dz_sum, dz_sum], axis=1)
+    fs4[3:4, :] = fs4[2:3, :]
+
+    def weight_work():
+        if inside:
+            point_a()
+            for d in far_first:
+                wide_z(d)
+
+    both = plain_sum(3, fs4, fr4, cs4, cr4, weight_work)
+    if inside:
+        wide_a(rank_one(own * base + bi * tall, tall, both[2:3, :hid]))
     shift_total, gain_total = both[0:1, :], both[1:2, :]
     owned(g1_out, gain_total)
     owned(s1_out, shift_total)
@@ -608,6 +768,16 @@
         return 0
 
     lax.fori_loop(0, seqs, drain, 0)
+    if inside:
+
+        def put_wide(j, v):
+            dwd_out[j * tall : (j + 1) * tall, :] = v
+
+        def put_point(j, v):
+            dwp_out[j % 2 * small : (j % 2 + 1) * small, j // 2 * hid : (j // 2 + 1) * hid] = v
+
+        point_end(put_point)
+        wide_end(put_wide)
     for c in par_far:
         c.wait_send()
     for k in range(nz):
@@ -626,9 +796,12 @@
 
 def call(sizes, inside, *refs):
     refs = list(refs)
-    if not inside:
-        first = 21 + 11 + 16 + 2
-        refs[first + 2 : first + 2] = [refs[first], refs[first + 1], None]
+    first = 21 + 14 + 16 + 8
+    if inside:
+        red = first + 5
+        refs[red : red + 16] = [refs[red : red + 8], refs[red + 8 : red + 16]]
+    else:
+        refs[first:first] = [refs[first - 6], refs[first - 5], None, refs[14], refs[15], None, None]
     block(sizes, *refs)
 
 
@@ -638,7 +811,9 @@
     hid = wd.shape[1]
     groups = ("batch", "fsdp")
     inside = (
-        wd.shape[0] % 16 == 0
+        nf == 2
+        and nb == 4
+        and wd.shape[0] % (8 * nb) == 0
         and wp.shape[0] % 16 == 0
         and (wd.shape[0] + 2 * wp.shape[0]) % (16 * nb) == 0
         and chans == 2 * hid
@@ -665,21 +840,37 @@
         pltpu.VMEM(black.shape, jnp.int32),
         pltpu.VMEM(wd.shape, wd.dtype),
         pltpu.VMEM(wp.shape, wp.dtype),
-        pltpu.VMEM((3 * chans, hid), BF) if inside else None,
-        pltpu.VMEM((hid, chans), BF) if inside else None,
-        pltpu.VMEM((nz * nf, wd.shape[0] + 2 * wp.shape[0], hid), BF) if inside else None,
         pltpu.VMEM((nz * nf, 8, 128), F32),
         pltpu.VMEM((8, chans), F32),
         pltpu.VMEM((2, seqs, PAD, hid), BF),
         pltpu.VMEM((2, seqs, PAD, hid), BF),
     ]
+    if inside:
+        scratch += [
+            pltpu.VMEM((3 * chans, hid), BF),
+            pltpu.VMEM((hid, chans), BF),
+            pltpu.VMEM((nz * nf, wd.shape[0] + 2 * wp.shape[0], hid), BF),
+            pltpu.VMEM((3 * chans, hid), F32),
+            pltpu.VMEM((hid, chans), F32),
+        ]
+        for p in (wd.shape[0] // nb, 2 * wp.shape[0] // nb):
+            scratch += [
+                pltpu.VMEM((nz, nb, p, hid), BF),
+                pltpu.VMEM((nz, nb, p, hid), BF),
+                pltpu.VMEM((nz, nb, p, hid), BF),
+                pltpu.VMEM((nb - 1, nz, p, hid), BF),
+                pltpu.VMEM((nz, p, hid), F32),
+                pltpu.VMEM((nz - 1, p, hid), BF),
+                pltpu.VMEM((nz - 1, p, hid), BF),
+                pltpu.VMEM((nb, p, hid), BF),
+            ]
     out, gin, dwd, dwp, bias_grad, g1_grad, s1_grad, g2_grad, s2_grad = pl.pallas_call(
         functools.partial(call, sizes, inside),
         out_shape=(
             jax.ShapeDtypeStruct(x.shape, BF),
             jax.ShapeDtypeStruct(x.shape, BF),
-            jax.ShapeDtypeStruct((3 * chans, hid), F32),
-            jax.ShapeDtypeStruct((hid, chans), F32),
+            jax.ShapeDtypeStruct(wd.shape if inside else (3 * chans, hid), F32),
+            jax.ShapeDtypeStruct(wp.shape if inside else (hid, chans), F32),
             jax.ShapeDtypeStruct(bias.shape, F32),
             jax.ShapeDtypeStruct(bias.shape, F32),
             jax.ShapeDtypeStruct(bias.shape, F32),
@@ -700,9 +891,12 @@
             pltpu.VMEM((seqs, bins, 3 * hid), BF),
             pltpu.VMEM((seqs, bins, chans), F32),
             pltpu.VMEM((seqs, bins, chans), BF),
+            pltpu.VMEM((seqs, 2 * PAD, hid), BF),
+            pltpu.VMEM((seqs, 2 * PAD, hid), BF),
+            pltpu.VMEM((3 * chans, 128), F32),
         ]
-        + sums(4, chans) + sums(4, hid) + sums(2, hid) + sums(2, chans)
-        + [m for m in scratch if m is not None]
+        + sums(4, chans) + sums(4, hid) + sums(4, hid) + sums(4, chans)
+        + scratch
         + [
             dma((seqs,)), dma((seqs,)), dma((seqs,)), dma((seqs,)), dma((4,)),
             dma((2,)), dma((2,)), dma((2,)), dma((2,)),
@@ -710,17 +904,22 @@
             dma((nz,)), dma((nz,)), dma((nz, nb)), dma((nz, nb)),
             dma((near, nz, nb)), dma((near, nz, nb)),
             dma((nz,)), dma((nz,)), dma((near, nz)), dma((near, nz)),
+            dma((2, nz)), dma((2, nz)), dma((2, nb, nz)), dma((2, nb, nz)),
+            dma((2, nz)), dma((2, nz)), dma((2, nb)), dma((2, nb)),
         ],
         compiler_params=pltpu.CompilerParams(
             collective_id=0, has_side_effects=True, vmem_limit_bytes=60 * 2**20
         ),
     )(x, og, black, unmap, limit, wd, wp, bias, g1, s1, g2, s2)
-    summed = lax.psum((dwd, dwp), "bins")
+    if not inside:
+        dwd, dwp = lax.psum((dwd, dwp), "bins")
+        dwd = lax.psum_scatter(dwd, groups, scatter_dimension=0, tiled=True)
+        dwp = lax.psum_scatter(dwp, groups, scatter_dimension=0, tiled=True)
     return (
         out,
         gin,
-        lax.psum_scatter(summed[0], groups, scatter_dimension=0, tiled=True),
-        lax.psum_scatter(summed[1], groups, scatter_dimension=0, tiled=True),
+        dwd,
+        dwp,
         bias_grad,
         g1_grad,
         s1_grad,

time: 239 us -> 106 us (0.44)
  waiting for transfers between devices: 124 us -> 0 us
  between operations: 13.8 us -> 0.71 us
  Pallas kernels: 92.2 us -> 95.3 us
    reduce_scatter x2 -> x0, waiting for transfers between devices: 75.3 us -> none  [the longest x1 44.5 us: local(): lax.psum_scatter(summed[0], groups, scatter_dimension=0, tiled=True)]
    psum x1 -> x0, waiting for transfers between devices: 48 us -> none  [local(): summed = lax.psum((dwd, dwp), 'bins')]
    pallas_call x1, Pallas kernels: 92.2 us -> 95.3 us  [local(): pl.pallas_call(functools.partial(call, sizes, inside), out_shape=(jax.Sha...]
    unnamed x27 -> x25, local copies, waits for them, and re-layouts: 8.7 us -> 9.59 us
  transfers between devices with their start and end apart: 3 -> 0, of which waited for: 3 -> 0; matrix products, arithmetic and copies ran while one was open for 0% -> 0% of each run, Pallas kernels for 0% -> 0%
where the time goes in v3:
time: 106 us
  Pallas kernels  95.3 us (90%)
  local copies, waits for them, and re-layouts  9.59 us (9%)
    pallas_call x1, Pallas kernels, local(): pl.pallas_call(functools.partial(call, sizes, inside), out_shape=(jax.Sha...  95.3 us
    unnamed x25, local copies, waits for them, and re-layouts  9.59 us

profile of v3, /device:TPU:0, one launch (start us, length us, event | category | flops | bytes accessed | tf_op | source)
XLA Modules:
  0.0 105.6 jit_solution(9046187168659021182)
XLA Ops:
  0.6 95.3 %shard_map.187 = (bf16[8,256,768]{2,1,0:T(8,128)(2,1)}, bf16[8,256,768]{2,1,0:T(8,128)(2,1)}, f32[288,384]{1,0:T(8,128)}, f32[48,768]{1,0:T(8,128)}, f32[96]{0:T...) custom-call(bf16[8,256,768]{2,1,0:T(8,128)(2,1)} %refs_0_.1, bf16[8,256,768]{2,1,0:T(8,128)(2,1)} %refs_1_.1, ...), custom_call_target="tpu_custom_call" | custom-call | tf_op jit(solution)/shard_map/pallas_call | solution.py:867
  95.9 0.0 copy-start
  96.0 3.9 %copy.30 = bf16[8,256,768]{2,1,0:T(8,128)(2,1)} copy(bf16[8,256,768]{2,1,0:T(8,128)(2,1)} %get-tuple-element.18) | data formatting | bytes 6291456
  99.9 0.0 copy-done
  99.9 0.0 copy-start.1
  99.9 0.0 copy-start.2
  99.9 0.0 copy-start.7
  99.9 0.0 copy-start.6
  99.9 0.0 copy-start.5
  99.9 0.0 copy-start.4
  99.9 0.0 copy-start.3
  99.9 1.7 %copy.31 = bf16[8,256,768]{2,1,0:T(8,128)(2,1)} copy(bf16[8,256,768]{2,1,0:T(8,128)(2,1)S(1)} %copy-done) | data formatting | bytes 6291456
  101.6 0.0 copy-done.1
  101.6 0.8 copy.32
  102.3 0.0 copy-done.2
  102.3 0.7 copy.33
  103.0 0.0 copy-done.7
  103.0 0.5 copy.34
  103.5 0.0 copy-done.6
  103.5 0.5 copy.35
  104.0 0.0 copy-done.5
  104.0 0.5 copy.36
  104.5 0.0 copy-done.4
  104.6 0.5 copy.37
  105.1 0.0 copy-done.3
  105.1 0.5 copy.38
Async XLA Ops:
  95.9 3.9 %copy-start = (bf16[8,256,768]{2,1,0:T(8,128)(2,1)S(1)}, bf16[8,256,768]{2,1,0:T(8,128)(2,1)}, u32[]{:S(2)}) copy-start(bf16[8,256,768]{2,1,0:T(8,128)(2,1)} %get-tuple-element.19) | copy-start | bytes 9437188
  99.9 1.7 %copy-start.1 = (f32[288,384]{1,0:T(8,128)S(1)}, f32[288,384]{1,0:T(8,128)}, u32[]{:S(2)}) copy-start(f32[288,384]{1,0:T(8,128)} %get-tuple-element.20) | copy-start | bytes 1327108
  99.9 2.5 %copy-start.2 = (f32[48,768]{1,0:T(8,128)S(1)}, f32[48,768]{1,0:T(8,128)}, u32[]{:S(2)}) copy-start(f32[48,768]{1,0:T(8,128)} %get-tuple-element.21) | copy-start | bytes 442372
  99.9 3.1 %copy-start.7 = (f32[96]{0:T(128)S(1)}, f32[96]{0:T(128)}, u32[]{:S(2)}) copy-start(f32[96]{0:T(128)} %get-tuple-element.22) | copy-start | bytes 1156
  99.9 3.7 %copy-start.6 = (f32[96]{0:T(128)S(1)}, f32[96]{0:T(128)}, u32[]{:S(2)}) copy-start(f32[96]{0:T(128)} %get-tuple-element.23) | copy-start | bytes 1156
  99.9 4.2 %copy-start.5 = (f32[96]{0:T(128)S(1)}, f32[96]{0:T(128)}, u32[]{:S(2)}) copy-start(f32[96]{0:T(128)} %get-tuple-element.24) | copy-start | bytes 1156
  99.9 4.7 %copy-start.4 = (f32[48]{0:T(128)S(1)}, f32[48]{0:T(128)}, u32[]{:S(2)}) copy-start(f32[48]{0:T(128)} %get-tuple-element.25) | copy-start | bytes 580
  99.9 5.2 %copy-start.3 = (f32[48]{0:T(128)S(1)}, f32[48]{0:T(128)}, u32[]{:S(2)}) copy-start(f32[48]{0:T(128)} %get-tuple-element.26) | copy-start | bytes 580

commit v4 on v3

--- a/solution.py
+++ b/solution.py
@@ -39,12 +39,12 @@
 def block(
     sizes,
     x_hbm, og_hbm, black_hbm, unmap_hbm, limit, wd_hbm, wp_hbm, bias_in, g1_in, s1_in, g2_in, s2_in,
-    out_hbm, gin_hbm, dwd_out, dwp_out, bias_out, g1_out, s1_out, g2_out, s2_out,
-    xin, grad, vm, h1, z1, gw, h2, dz, taps, dg, stage, upper, lower, mcol,
+    out, gin, dwd_out, dwp_out, tile_out,
+    xin, grad, vm, h1, z1, gw, h2, dz, taps, dg, zs_out, zs_in, mid_e, mid_z, upper, lower, mcol,
     fs1, fr1, cs1, cr1, fs2, fr2, cs2, cr2, fs3, fr3, cs3, cr3, fs4, fr4, cs4, cr4,
     black, unmap, wd_own, wp_own, pall, par, es, er,
-    wd, wp, wall, dwd, dwp, dwd_red, dwp_red,
-    xsem, gsem, osem, isem, lsem, hsem, hrem, zsem, zrem, fss, frs, css, crs,
+    wt, wd, wp, wall, dwd, dwp, dwd_red, dwp_red,
+    xsem, gsem, lsem, hsem, zsem, fss, frs, css, crs,
     wzs, wzr, wcs, wcr, wfs, wfr, pzs, pzr, pfs, pfr,
     rfs, rfr, rxs, rxr, rzs, rzr, ras, rar,
 ):
@@ -69,6 +69,13 @@
         )
     ]
 
+    for c in small_loads:
+        c.start()
+    for s in range(seqs):
+        load_x(s).start()
+    for s in range(seqs):
+        load_g(s).start()
+
     mates = [(k,) for k in range(1, nf)]
     chips = [(b, z) for z in range(nz) for b in range(nb) if (b, z) != (0, 0)]
 
@@ -88,14 +95,97 @@
     for b, z in chips:
         pl.semaphore_signal(barrier, inc=1, device_id=chip(b, z), device_id_type=MESH)
 
-    small_loads[0].start()
-    small_loads[1].start()
-    for s in range(seqs):
-        load_x(s).start()
-    small_loads[2].start()
-    small_loads[3].start()
-    for s in range(seqs):
-        load_g(s).start()
+    def start(copies):
+        for c in copies:
+            c.start()
+
+    def wait(copies):
+        for c in copies:
+            c.wait_recv()
+        for c in copies:
+            c.wait_send()
+
+    own = zi * nf + fi
+    pall[own] = jnp.zeros((8, 128), F32)
+    for r, ref in enumerate((bias_in, g1_in, s1_in, g2_in, s2_in)):
+        n = ref.shape[0]
+        pall[own, r : r + 1, 0:n] = ref[...].astype(BF).astype(F32).reshape(1, n)
+    small_loads[2].wait()
+    small_loads[3].wait()
+    share = wp_own.shape[0]
+    if inside:
+        base = wd_own.shape[0]
+        piece = (base + 2 * share) // nb
+        wall[own, 0:base, :] = wd_own[...].astype(BF)
+        wall[own, base : base + share, :] = wp_own[:, 0:hid].astype(BF)
+        wall[own, base + share : base + 2 * share, :] = wp_own[:, hid:].astype(BF)
+
+    def before(i, k, n):
+        return lax.rem(i + n - k, n)
+
+    hops = [h for k in range(1, nz) for h in (k, -k)]
+
+    def sends(h):
+        return (zi + h >= 0) & (zi + h < nz)
+
+    def receives(h):
+        return (zi - h >= 0) & (zi - h < nz)
+
+    def send_to(src, dst, ssem, rsem, where):
+        return pltpu.make_async_remote_copy(
+            src_ref=src, dst_ref=dst, send_sem=ssem, recv_sem=rsem,
+            device_id=where, device_id_type=MESH,
+        )
+
+    def send(ref, ssem, rsem, where):
+        return send_to(ref, ref, ssem, rsem, where)
+
+    def along(k):
+        return {"batch": lax.rem(zi + k, nz)}
+
+    def slot(z, f):
+        return z * nf + f
+
+    par_far = [send(pall.at[own], pzs.at[k], pzr.at[k], along(k)) for k in range(1, nz)]
+    par_near = [
+        [
+            send(pall.at[slot(before(zi, k, nz), fi)], pfs.at[j, k], pfr.at[j, k], mate(m))
+            for j, (m,) in enumerate(mates)
+        ]
+        for k in range(nz)
+    ]
+
+    def part(h, b):
+        rows = pl.ds(pl.multiple_of(before(bi, b, nb) * piece, 16), piece)
+        return wall.at[slot(zi - h, fi), rows, :]
+
+    if inside:
+        w_far = {
+            h: send(part(0, 0), wzs.at[i], wzr.at[i], {"batch": zi + h}) for i, h in enumerate(hops)
+        }
+        w_side = {
+            h: [
+                send(part(h, 0), wcs.at[i, b], wcr.at[i, b], {"bins": lax.rem(bi + b, nb)})
+                for b in range(1, nb)
+            ]
+            for i, h in enumerate(hops)
+        }
+        w_own = [send(wall.at[own], wfs.at[len(hops), 0], wfr.at[len(hops), 0], mate(1))]
+        w_near = {
+            h: [send(part(h, b), wfs.at[i, b], wfr.at[i, b], mate(1)) for b in range(nb)]
+            for i, h in enumerate(hops)
+        }
+
+    def for_hops(test, do):
+        for h in hops if inside else ():
+            pl.when(test(h))(functools.partial(do, h))
+
+    pl.semaphore_wait(barrier, len(mates) + len(chips))
+    for_hops(sends, lambda h: w_far[h].start())
+    if inside:
+        start(w_own)
+    start(par_far)
+    start(par_near[0])
 
     small_loads[0].wait()
     small_loads[1].wait()
@@ -119,36 +209,81 @@
 
     low, high = lax.rem(bi + nb - 1, nb), lax.rem(bi + 1, nb)
 
-    def edge_copies(low_src, low_dst, high_src, high_dst, send, recv):
-        to_low = pltpu.make_async_remote_copy(
-            src_ref=low_src, dst_ref=low_dst, send_sem=send.at[0], recv_sem=recv.at[0],
-            device_id={"bins": low}, device_id_type=MESH,
+    relay = nb == 4
+    half = seqs // 2
+
+    def edge_copy(src, dst, sems, i, where):
+        return pltpu.make_async_remote_copy(
+            src_ref=src, dst_ref=dst, send_sem=sems.at[0, i], recv_sem=sems.at[1, i],
+            device_id={"bins": where}, device_id_type=MESH,
         )
-        to_high = pltpu.make_async_remote_copy(
-            src_ref=high_src, dst_ref=high_dst, send_sem=send.at[1], recv_sem=recv.at[1],
-            device_id={"bins": high}, device_id_type=MESH,
-        )
-        return to_low, to_high
-
-    def edge_start(to_low, to_high):
-        @pl.when(bi > 0)
-        def _():
-            to_low.start()
-
-        @pl.when(bi < nb - 1)
-        def _():
-            to_high.start()
-
-    def edge_wait(to_low, to_high):
-        @pl.when(bi < nb - 1)
-        def _():
-            to_low.wait_recv()
-            to_high.wait_send()
-
-        @pl.when(bi > 0)
-        def _():
-            to_high.wait_recv()
-            to_low.wait_send()
+
+    def edges(src, dst, mid, sems):
+        to_low = [edge_copy(src.at[0, i], dst.at[0, i], sems, i, low) for i in range(2)]
+        to_high = [edge_copy(src.at[1, i], dst.at[1, i], sems, 2 + i, high) for i in range(2)]
+        by_0 = [edge_copy(src.at[0, 1], mid, sems, 4, 0), edge_copy(mid, dst.at[0, 1], sems, 1, 1)]
+        by_3 = [edge_copy(src.at[1, 1], mid, sems, 4, nb - 1), edge_copy(mid, dst.at[1, 1], sems, 3, nb - 2)]
+
+        def sides(do_low, do_high):
+            pl.when(bi > 0)(do_low)
+            pl.when(bi < nb - 1)(do_high)
+
+        def first():
+            def _low():
+                to_low[0].start()
+                if not relay:
+                    to_low[1].start()
+
+            def _high():
+                to_high[0].start()
+                if not relay:
+                    to_high[1].start()
+
+            sides(_low, _high)
+            if relay:
+                pl.when((bi == 1) | (bi == 3))(to_low[1].start)
+                pl.when((bi == 0) | (bi == 2))(to_high[1].start)
+                pl.when(bi == 2)(by_0[0].start)
+                pl.when(bi == 1)(by_3[0].start)
+
+        def onward():
+            def _pass(copies):
+                copies[0].wait_recv()
+                copies[1].start()
+
+            if relay:
+                pl.when(bi == 0)(functools.partial(_pass, by_0))
+                pl.when(bi == nb - 1)(functools.partial(_pass, by_3))
+
+        def last():
+            def _from_low():
+                for c in to_high:
+                    c.wait_recv()
+                to_low[0].wait_send()
+                if not relay:
+                    to_low[1].wait_send()
+
+            def _from_high():
+                for c in to_low:
+                    c.wait_recv()
+                to_high[0].wait_send()
+                if not relay:
+                    to_high[1].wait_send()
+
+            sides(_from_low, _from_high)
+            if relay:
+                pl.when((bi == 1) | (bi == 3))(to_low[1].wait_send)
+                pl.when((bi == 0) | (bi == 2))(to_high[1].wait_send)
+                pl.when(bi == 2)(by_0[0].wait_send)
+                pl.when(bi == 1)(by_3[0].wait_send)
+                pl.when(bi == 0)(by_0[1].wait_send)
+                pl.when(bi == nb - 1)(by_3[1].wait_send)
+
+        return first, onward, last
+
+    def packed(s):
+        first = s % half * STEP
+        return s // half, slice(first, first + STEP), slice(None)
 
     def mate_copies(i, src, dst):
         return [
@@ -167,16 +302,6 @@
             )
             for j, (b, z) in enumerate(chips)
         ]
-
-    def start(copies):
-        for c in copies:
-            c.start()
-
-    def wait(copies):
-        for c in copies:
-            c.wait_recv()
-        for c in copies:
-            c.wait_send()
 
     def plain_sum(i, fs, fr, cs, cr, filler):
         mine = mate_copies(i, fs, fr)
@@ -195,75 +320,9 @@
             total = total + cr[j]
         return total
 
-    own = zi * nf + fi
-    pall[own] = jnp.zeros((8, 128), F32)
-    for r, ref in enumerate((bias_in, g1_in, s1_in, g2_in, s2_in)):
-        n = ref.shape[0]
-        pall[own, r : r + 1, 0:n] = ref[...].astype(BF).astype(F32).reshape(1, n)
-    small_loads[2].wait()
-    small_loads[3].wait()
-    share = wp_own.shape[0]
-    if inside:
-        base = wd_own.shape[0]
-        piece = (base + 2 * share) // nb
-        wall[own, 0:base, :] = wd_own[...].astype(BF)
-        wall[own, base : base + share, :] = wp_own[:, 0:hid].astype(BF)
-        wall[own, base + share : base + 2 * share, :] = wp_own[:, hid:].astype(BF)
-
-    def before(i, k, n):
-        return lax.rem(i + n - k, n)
-
-    def send_to(src, dst, ssem, rsem, where):
-        return pltpu.make_async_remote_copy(
-            src_ref=src, dst_ref=dst, send_sem=ssem, recv_sem=rsem,
-            device_id=where, device_id_type=MESH,
-        )
-
-    def send(ref, ssem, rsem, where):
-        return send_to(ref, ref, ssem, rsem, where)
-
-    def along(k):
-        return {"batch": lax.rem(zi + k, nz)}
-
-    def slot(z, f):
-        return z * nf + f
-
-    par_far = [send(pall.at[own], pzs.at[k], pzr.at[k], along(k)) for k in range(1, nz)]
-    par_near = [
-        [
-            send(pall.at[slot(before(zi, k, nz), fi)], pfs.at[j, k], pfr.at[j, k], mate(m))
-            for j, (m,) in enumerate(mates)
-        ]
-        for k in range(nz)
-    ]
-
-    def part(k, b):
-        rows = pl.ds(pl.multiple_of(before(bi, b, nb) * piece, 16), piece)
-        return wall.at[slot(before(zi, k, nz), fi), rows, :]
-
-    if inside:
-        w_far = [send(part(0, 0), wzs.at[k], wzr.at[k], along(k)) for k in range(1, nz)]
-        w_side = [
-            [
-                send(part(k, 0), wcs.at[k, b], wcr.at[k, b], {"bins": lax.rem(bi + b, nb)})
-                for b in range(1, nb)
-            ]
-            for k in range(1, nz)
-        ]
-        w_own = [
-            send(wall.at[own], wfs.at[j, 0, 0], wfr.at[j, 0, 0], mate(m))
-            for j, (m,) in enumerate(mates)
-        ]
-        w_near = [
-            [
-                [send(part(k, b), wfs.at[j, k, b], wfr.at[j, k, b], mate(m)) for j, (m,) in enumerate(mates)]
-                for b in range(nb)
-            ]
-            for k in range(1, nz)
-        ]
-
     def reduction(i, bufs, get):
-        fs, fr, xs, xr, acc, zs, zr, ga = bufs
+        fs, fr, xr, acc, zs, zr, ga = bufs
+        xs = fs
         other = lax.rem(fi + 1, 2)
 
         def f_copy(d):
@@ -291,7 +350,7 @@
 
         def x_send(d):
             z = lax.rem(zi + d, nz)
-            f_copy(d).wait_recv()
+            f_copy(d).wait()
             for j in range(nb):
                 xs[d, j] = (get(slot(z, fi), j) + fr[d, j].astype(F32)).astype(BF)
             acc[d] = get(slot(z, fi), bi) + fr[d, bi].astype(F32)
@@ -309,8 +368,8 @@
             else:
                 acc[0] = total
 
-        def a_send(more=None):
-            total = acc[0] if more is None else acc[0] + more
+        def a_send():
+            total = acc[0]
             for d in range(1, nz):
                 z_copy(d).wait_recv()
                 total = total + zr[d - 1].astype(F32)
@@ -324,7 +383,6 @@
             for j in range(nb):
                 put(j, ga[j].astype(F32))
             for d in range(nz):
-                f_copy(d).wait_send()
                 for b in range(1, nb):
                     x_copy(d, b).wait_send()
                 if d:
@@ -378,14 +436,16 @@
     def triple(ref):
         return ref[0:1, :], ref[1:2, :], ref[2:3, :]
 
-    pl.semaphore_wait(barrier, len(mates) + len(chips))
     mine = mate_copies(0, fs1, fr1)
     start(mine)
-    start(par_far)
-    start(par_near[0])
-    if inside:
-        start(w_far)
-        start(w_own)
+
+    def side_work(h):
+        w_far[h].wait_recv()
+        start(w_side[h])
+        w_near[h][0].start()
+
+    for h in hops[:2] if inside else ():
+        pl.when(receives(h))(functools.partial(side_work, h))
     wait(mine)
     s_, q_, n_ = merge([triple(fs1)] + [triple(fr1.at[j]) for j in range(len(mates))])
     cs1[0:1, :] = s_
@@ -394,6 +454,8 @@
     cs1[3:4, :] = n_
     far = chip_copies(0, cs1, cr1)
     start(far)
+    for h in hops[2:] if inside else ():
+        pl.when(receives(h))(functools.partial(side_work, h))
 
     def mask_grad(s, acc):
         load_g(s).wait()
@@ -410,10 +472,6 @@
     for k in range(1, nz):
         par_far[k - 1].wait_recv()
         start(par_near[k])
-        if inside:
-            w_far[k - 1].wait_recv()
-            start(w_side[k - 1])
-            start(w_near[k - 1][0])
     for k in range(nz):
         for c in par_near[k]:
             c.wait_recv()
@@ -459,17 +517,20 @@
     acc = lax.fori_loop(0, seqs, first_act, jnp.zeros((8, chans), F32))
     act_sum = jnp.sum(acc, axis=0, keepdims=True)
 
-    if inside:
-        for k in range(1, nz):
-            for b in range(1, nb):
-                w_side[k - 1][b - 1].wait_recv()
-                start(w_near[k - 1][b])
+    def near_work(h):
+        for b in range(1, nb):
+            w_side[h][b - 1].wait_recv()
+            w_near[h][b].start()
+
+    def near_end(h):
+        for c in w_near[h]:
+            c.wait_recv()
+
+    for_hops(receives, near_work)
+    for_hops(receives, near_end)
+    if inside:
         for c in w_own:
             c.wait_recv()
-        for k in range(1, nz):
-            for b in range(nb):
-                for c in w_near[k - 1][b]:
-                    c.wait_recv()
         for c in range(nz * nf):
             wd[c * base : (c + 1) * base, :] = wall[c, 0:base, :]
             wp[c * share : (c + 1) * share, 0:hid] = wall[c, base : base + share, :]
@@ -479,31 +540,43 @@
         return wd[k * chans : (k + 1) * chans, :]
 
     over = h1[:, PAD + bins - STEP : PAD + bins - STEP + PAD, :].reshape(seqs * PAD, chans)
-    es[1] = dot(over, tap(0), 1, 0).astype(BF).reshape(seqs, PAD, hid)
+    over = dot(over, tap(0), 1, 0).astype(BF)
     under = h1[:, STEP : STEP + PAD, :].reshape(seqs * PAD, chans)
-    es[0] = dot(under, tap(2), 1, 0).astype(BF).reshape(seqs, PAD, hid)
-    e_low, e_high = edge_copies(es.at[0], er.at[0], es.at[1], er.at[1], hsem, hrem)
-    edge_start(e_low, e_high)
-
-    def conv(s, _):
+    under = dot(under, tap(2), 1, 0).astype(BF)
+    for s in range(seqs):
+        es[(1,) + packed(s)] = over[s * PAD : s * PAD + STEP, :]
+        es[(0,) + packed(s)] = under[s * PAD + PAD - STEP : s * PAD + PAD, :]
+    e_first, e_onward, e_last = edges(es, er, mid_e, hsem)
+    e_first()
+
+    group = seqs // 2
+
+    def conv(i, _):
+        some = pl.ds(i * group, group)
         z = None
         for k in range(3):
             first = PAD + (k - 1) * STEP
-            part = dot(h1[s, first : first + bins, :], tap(k), 1, 0)
+            left = h1[some, first : first + bins, :].reshape(group * bins, chans)
+            part = dot(left, tap(k), 1, 0)
             z = part if z is None else z + part
-        z1[s] = z
+        z1[some] = z.reshape(group, bins, hid)
         return 0
 
-    lax.fori_loop(0, seqs, conv, 0)
-    edge_wait(e_low, e_high)
+    lax.fori_loop(0, 1, conv, 0)
+    e_onward()
+    lax.fori_loop(1, 2, conv, 0)
+
+    e_last()
 
     @pl.when(bi > 0)
     def _():
-        z1[:, 0:PAD, :] = z1[:, 0:PAD, :] + er[1].astype(F32)
+        for s in range(seqs):
+            z1[s, 0:STEP, :] = z1[s, 0:STEP, :] + er[(1,) + packed(s)].astype(F32)
 
     @pl.when(bi < nb - 1)
     def _():
-        z1[:, bins - PAD :, :] = z1[:, bins - PAD :, :] + er[0].astype(F32)
+        for s in range(seqs):
+            z1[s, bins - STEP :, :] = z1[s, bins - STEP :, :] + er[(0,) + packed(s)].astype(F32)
 
     def sums_z(s, acc):
         for r in range(pieces):
@@ -543,11 +616,15 @@
     far = chip_copies(1, cs2, cr2)
     start(far)
 
-    def grad_point(s, _):
-        gw[s] = dot(grad[s], wp[...], 1, 1)
+    def grad_point(i, _):
+        some = pl.ds(i * group, group)
+        left = grad[some].reshape(group * bins, chans)
+        gw[some] = dot(left, wp[...], 1, 1).reshape(group, bins, hid)
         return 0
 
-    lax.fori_loop(0, seqs, grad_point, 0)
+    lax.fori_loop(0, 2, grad_point, 0)
+    for k in range(3):
+        wt[k * hid : (k + 1) * hid, :] = jnp.transpose(tap(k))
 
     wait(far)
     entries = [pair(cs2, cs1)] + [pair(cr2.at[j], cr1.at[j]) for j in range(len(chips))]
@@ -556,19 +633,19 @@
         bias_part = bias_part + cr2[j, 2:4, :]
     bias_total = jnp.concatenate([bias_part[0:1, :], bias_part[1:2, :]], axis=1)
 
-    def owned(out, row):
-        n = out.shape[0]
+    def owned(r, n, row):
         row = jnp.concatenate([row, jnp.zeros((1, 256), F32)], axis=1)
         row = jnp.broadcast_to(row, (8, row.shape[1]))
         mine = jnp.zeros((8, 128), F32)
         for c in range(nz * nf):
             first, turn = c * n // 128 * 128, c * n % 128
-            tile = row[:, first : first + 256]
-            tile = (pltpu.roll(tile, 256 - turn, 1) if turn else tile)[:, :128]
-            mine = jnp.where(own == c, tile, mine)
-        out[...] = mine[0:1, 0:n].reshape(n)
-
-    owned(bias_out, bias_total)
+            piece_ = row[:, first : first + 256]
+            piece_ = (pltpu.roll(piece_, 256 - turn, 1) if turn else piece_)[:, :128]
+            mine = jnp.where(own == c, piece_, mine)
+        tile_out[r : r + 1, :] = mine[0:1, :]
+
+    wide_row, narrow_row = bias_in.shape[0], g2_in.shape[0]
+    owned(0, wide_row, bias_total)
     mean_two = s_ / count[:, :hid]
     scale_two = lax.rsqrt(q_ / count[:, :hid] + EPS)
     gain_two = par[3:4, :hid]
@@ -596,15 +673,11 @@
     fs3[2:3, :] = act_sum[:, :hid]
     fs3[3:4, :] = act_sum[:, hid:]
 
-    def store_out(s):
-        return pltpu.make_async_copy(stage.at[s], out_hbm.at[s], osem.at[s])
-
     def point_work():
         def branch(s, _):
-            stage[s] = (
+            out[s] = (
                 xin[s].astype(F32) + dot(h2[s], wp[...], 1, 0) + par[0:1, :]
             ).astype(BF)
-            store_out(s).start()
             return 0
 
         lax.fori_loop(0, seqs, branch, 0)
@@ -613,8 +686,8 @@
 
     both = plain_sum(2, fs3, fr3, cs3, cr3, point_work)
     shift_total, gain_total = both[0:1, :], both[1:2, :]
-    owned(g2_out, gain_total)
-    owned(s2_out, shift_total)
+    owned(3, narrow_row, gain_total)
+    owned(4, narrow_row, shift_total)
     if inside:
         for d in far_first:
             point_f(d)
@@ -646,11 +719,11 @@
         m = mcol[pl.ds(pl.multiple_of(first, 8), count), :]
         return jnp.concatenate([m] * narrow, axis=1) * row
 
-    z_low, z_high = edge_copies(
-        dz.at[:, pl.ds(PAD, PAD), :], upper.at[:, pl.ds(PAD, PAD), :],
-        dz.at[:, pl.ds(bins, PAD), :], lower.at[:, pl.ds(0, PAD), :], zsem, zrem,
-    )
-    edge_start(z_low, z_high)
+    for s in range(seqs):
+        zs_out[(0,) + packed(s)] = dz[s, PAD : PAD + STEP, :]
+        zs_out[(1,) + packed(s)] = dz[s, PAD + bins - STEP : PAD + bins, :]
+    z_first, z_onward, z_last = edges(zs_out, zs_in, mid_z, zsem)
+    z_first()
 
     def shift_taps(s, _):
         for k in range(3):
@@ -664,27 +737,33 @@
             point_x(d)
 
     def kernel_grad(m, _):
-        cols = pl.ds(pl.multiple_of(m * 256, 256), 256)
-        left = h1[:, PAD : PAD + bins, cols].reshape(seqs * bins, 256)
+        cols = pl.ds(pl.multiple_of(m * hid, 128), hid)
+        left = h1[:, PAD : PAD + bins, cols].reshape(seqs * bins, hid)
+        g = dot(left, taps[...].reshape(seqs * bins, 3 * hid), 0, 0)
         for k in range(3):
-            right = taps[:, :, k * hid : (k + 1) * hid].reshape(seqs * bins, hid)
-            g = dot(left, right, 0, 0)
+            part = g[:, k * hid : (k + 1) * hid]
             if inside:
-                g = g - rank_one(m * 256, 256, dz_sum)
-            dwd[pl.ds(pl.multiple_of(k * chans + m * 256, 256), 256), :] = g
+                part = part - rank_one(m * hid, hid, dz_sum)
+            dwd[pl.ds(pl.multiple_of(k * chans + m * hid, 128), hid), :] = part
         return 0
 
-    lax.fori_loop(0, chans // 256, kernel_grad, 0)
-
-    def middle(s, _):
-        dg[s] = dot(taps[s, :, hid : 2 * hid], tap(1), 1, 1)
-        return 0
-
-    lax.fori_loop(0, seqs, middle, 0)
-
-    edge_wait(z_low, z_high)
-    after = upper[:, STEP : STEP + PAD, :]
-    ahead = lower[:, PAD - STEP : 2 * PAD - STEP, :]
+    lax.fori_loop(0, 1, kernel_grad, 0)
+    z_onward()
+    lax.fori_loop(1, chans // hid, kernel_grad, 0)
+
+    z_last()
+
+    @pl.when(bi < nb - 1)
+    def _():
+        for s in range(seqs):
+            upper[s, PAD - STEP :, :] = zs_in[(0,) + packed(s)]
+
+    @pl.when(bi > 0)
+    def _():
+        for s in range(seqs):
+            lower[s, 0:STEP, :] = zs_in[(1,) + packed(s)]
+
+    after, ahead = upper[...], lower[...]
     taps[:, bins - PAD :, 0:hid] = taps[:, bins - PAD :, 0:hid] + after
     taps[:, 0:PAD, 2 * hid :] = taps[:, 0:PAD, 2 * hid :] + ahead
     after = after.reshape(seqs * PAD, hid)
@@ -704,30 +783,42 @@
             wide_f(d)
         for d in far_first:
             point_z(d)
-
-    def input_side(s, acc):
+        wide_x(far_first[0])
+
+    def back_conv(i):
+        some = pl.ds(i * 2, 2)
+        left = taps[some].reshape(2 * bins, 3 * hid)
+        dg[some] = dot(left, wt[...], 1, 0).reshape(2, bins, chans)
+
+    def back_act(i, acc):
         a, b = acc
-        d = dg[s]
-        for k in (0, 2):
-            d = d + dot(taps[s, :, k * hid : (k + 1) * hid], tap(k), 1, 1)
-        dg[s] = d
-        for r in range(pieces):
-            rows = slice(r * CHUNK, (r + 1) * CHUNK)
-            xc = xin[s, r * CHUNK : (r + 1) * CHUNK, :].astype(F32) - mean_one
-            v = xc * gain_one + shift_one
-            t = jnp.tanh(0.851 * v)
-            d = dg[s, rows, :] * (0.5 + 0.5 * t + (0.4255 * v) * (1.0 - t * t))
-            dg[s, rows, :] = d
-            a = a + fold(d)
-            b = b + fold(d * (xc * scale_one))
+        for s in (2 * i, 2 * i + 1):
+            for r in range(pieces):
+                rows = slice(r * CHUNK, (r + 1) * CHUNK)
+                xc = xin[s, rows, :].astype(F32) - mean_one
+                v = xc * gain_one + shift_one
+                t = jnp.tanh(0.851 * v)
+                d = dg[s, rows, :] * (0.5 + 0.5 * t + (0.4255 * v) * (1.0 - t * t))
+                dg[s, rows, :] = d
+                a = a + fold(d)
+                b = b + fold(d * (xc * scale_one))
         return a, b
 
+    def input_side(i, acc):
+        acc = back_act(i - 1, acc)
+        back_conv(i)
+        return acc
+
     zero = jnp.zeros((8, chans), F32)
-    a, b = lax.fori_loop(0, seqs // 2, input_side, (zero, zero))
-    if inside:
-        for d in far_first:
+    back_conv(0)
+    if inside:
+        for d in far_first[1:]:
             wide_x(d)
-    a, b = lax.fori_loop(seqs // 2, seqs, input_side, (a, b))
+        point_a()
+    a, b = lax.fori_loop(1, seqs // 2, input_side, (zero, zero))
+    a, b = back_act(seqs // 2 - 1, (a, b))
+    if inside:
+        wide_z(far_first[0])
     fs4[0:1, :] = jnp.sum(a, axis=0, keepdims=True)
     fs4[1:2, :] = jnp.sum(b, axis=0, keepdims=True)
     fs4[2:3, :] = jnp.concatenate([dz_sum, dz_sum], axis=1)
@@ -735,43 +826,32 @@
 
     def weight_work():
         if inside:
-            point_a()
-            for d in far_first:
+            for d in far_first[1:]:
                 wide_z(d)
+            wide_a()
 
     both = plain_sum(3, fs4, fr4, cs4, cr4, weight_work)
-    if inside:
-        wide_a(rank_one(own * base + bi * tall, tall, both[2:3, :hid]))
     shift_total, gain_total = both[0:1, :], both[1:2, :]
-    owned(g1_out, gain_total)
-    owned(s1_out, shift_total)
+    owned(1, wide_row, gain_total)
+    owned(2, wide_row, shift_total)
     level = shift_total / count
     slant = gain_total / count
-
-    def store_in(s):
-        return pltpu.make_async_copy(grad.at[s], gin_hbm.at[s], isem.at[s])
 
     def input_grad(s, _):
         for r in range(pieces):
             rows = slice(r * CHUNK, (r + 1) * CHUNK)
             xc = xin[s, r * CHUNK : (r + 1) * CHUNK, :].astype(F32) - mean_one
             d = dg[s, rows, :] - mask(s, r, wide) * (level + (xc * scale_one) * slant)
-            grad[s, rows, :] = (grad[s, rows, :].astype(F32) + gain_one * d).astype(BF)
-        store_in(s).start()
+            gin[s, rows, :] = (grad[s, rows, :].astype(F32) + gain_one * d).astype(BF)
         return 0
 
     lax.fori_loop(0, seqs, input_grad, 0)
 
-    def drain(s, _):
-        store_out(s).wait()
-        store_in(s).wait()
-        return 0
-
-    lax.fori_loop(0, seqs, drain, 0)
     if inside:
 
         def put_wide(j, v):
-            dwd_out[j * tall : (j + 1) * tall, :] = v
+            more = rank_one(own * base + j * tall, tall, both[2:3, :hid])
+            dwd_out[j * tall : (j + 1) * tall, :] = v + more
 
         def put_point(j, v):
             dwp_out[j % 2 * small : (j % 2 + 1) * small, j // 2 * hid : (j // 2 + 1) * hid] = v
@@ -783,26 +863,42 @@
     for k in range(nz):
         for c in par_near[k]:
             c.wait_send()
-    if inside:
-        for c in w_far + w_own:
+
+    def sent(h):
+        for c in w_side[h] + w_near[h]:
             c.wait_send()
-        for k in range(1, nz):
-            for c in w_side[k - 1]:
-                c.wait_send()
-            for b in range(nb):
-                for c in w_near[k - 1][b]:
-                    c.wait_send()
+
+    for_hops(sends, lambda h: w_far[h].wait_send())
+    for_hops(receives, sent)
+    if inside:
+        for c in w_own:
+            c.wait_send()
 
 
 def call(sizes, inside, *refs):
     refs = list(refs)
-    first = 21 + 14 + 16 + 8
+    first = 17 + 17 + 16 + 9
     if inside:
         red = first + 5
-        refs[red : red + 16] = [refs[red : red + 8], refs[red + 8 : red + 16]]
+        refs[red : red + 14] = [refs[red : red + 7], refs[red + 7 : red + 14]]
     else:
-        refs[first:first] = [refs[first - 6], refs[first - 5], None, refs[14], refs[15], None, None]
+        refs[first:first] = [refs[first - 7], refs[first - 6], None, refs[14], refs[15], None, None]
     block(sizes, *refs)
+
+
+def write_out(out, gin, dwd, dwp, tile, *refs):
+    sem = refs[9]
+    copies = [
+        pltpu.make_async_copy(src, dst, sem.at[i])
+        for i, (src, dst) in enumerate(zip((out, gin, dwd, dwp), refs[:4]))
+    ]
+    for c in copies:
+        c.start()
+    for r, ref in enumerate(refs[4:9]):
+        n = ref.shape[0]
+        ref[...] = tile[r : r + 1, 0:n].reshape(n)
+    for c in copies:
+        c.wait()
 
 
 def local(sizes, x, black, unmap, limit, wd, wp, bias, g1, s1, g2, s2, og):
@@ -842,9 +938,10 @@
         pltpu.VMEM(wp.shape, wp.dtype),
         pltpu.VMEM((nz * nf, 8, 128), F32),
         pltpu.VMEM((8, chans), F32),
-        pltpu.VMEM((2, seqs, PAD, hid), BF),
-        pltpu.VMEM((2, seqs, PAD, hid), BF),
+        pltpu.VMEM((2, 2, seqs // 2 * STEP, hid), BF),
+        pltpu.VMEM((2, 2, seqs // 2 * STEP, hid), BF),
     ]
+    scratch.append(pltpu.VMEM((3 * hid, chans), BF))
     if inside:
         scratch += [
             pltpu.VMEM((3 * chans, hid), BF),
@@ -857,28 +954,23 @@
             scratch += [
                 pltpu.VMEM((nz, nb, p, hid), BF),
                 pltpu.VMEM((nz, nb, p, hid), BF),
-                pltpu.VMEM((nz, nb, p, hid), BF),
                 pltpu.VMEM((nb - 1, nz, p, hid), BF),
                 pltpu.VMEM((nz, p, hid), F32),
                 pltpu.VMEM((nz - 1, p, hid), BF),
                 pltpu.VMEM((nz - 1, p, hid), BF),
                 pltpu.VMEM((nb, p, hid), BF),
             ]
-    out, gin, dwd, dwp, bias_grad, g1_grad, s1_grad, g2_grad, s2_grad = pl.pallas_call(
+    out, gin, dwd, dwp, tile = pl.pallas_call(
         functools.partial(call, sizes, inside),
         out_shape=(
-            jax.ShapeDtypeStruct(x.shape, BF),
-            jax.ShapeDtypeStruct(x.shape, BF),
-            jax.ShapeDtypeStruct(wd.shape if inside else (3 * chans, hid), F32),
-            jax.ShapeDtypeStruct(wp.shape if inside else (hid, chans), F32),
-            jax.ShapeDtypeStruct(bias.shape, F32),
-            jax.ShapeDtypeStruct(bias.shape, F32),
-            jax.ShapeDtypeStruct(bias.shape, F32),
-            jax.ShapeDtypeStruct(g2.shape, F32),
-            jax.ShapeDtypeStruct(g2.shape, F32),
+            pltpu.VMEM(x.shape, BF),
+            pltpu.VMEM(x.shape, BF),
+            pltpu.VMEM(wd.shape if inside else (3 * chans, hid), F32),
+            pltpu.VMEM(wp.shape if inside else (hid, chans), F32),
+            pltpu.VMEM((8, 128), F32),
         ),
         in_specs=[hbm] * 4 + [pl.BlockSpec(memory_space=pltpu.SMEM)] + [hbm] * 2 + [vmem] * 5,
-        out_specs=(hbm, hbm) + (vmem,) * 7,
+        out_specs=(vmem,) * 5,
         scratch_shapes=[
             pltpu.VMEM((seqs, bins, chans), BF),
             pltpu.VMEM((seqs, bins, chans), BF),
@@ -890,42 +982,44 @@
             pltpu.VMEM((seqs, tall, hid), BF),
             pltpu.VMEM((seqs, bins, 3 * hid), BF),
             pltpu.VMEM((seqs, bins, chans), F32),
-            pltpu.VMEM((seqs, bins, chans), BF),
-            pltpu.VMEM((seqs, 2 * PAD, hid), BF),
-            pltpu.VMEM((seqs, 2 * PAD, hid), BF),
+            pltpu.VMEM((2, 2, seqs // 2 * STEP, hid), BF),
+            pltpu.VMEM((2, 2, seqs // 2 * STEP, hid), BF),
+            pltpu.VMEM((seqs // 2 * STEP, hid), BF),
+            pltpu.VMEM((seqs // 2 * STEP, hid), BF),
+            pltpu.VMEM((seqs, PAD, hid), BF),
+            pltpu.VMEM((seqs, PAD, hid), BF),
             pltpu.VMEM((3 * chans, 128), F32),
         ]
         + sums(4, chans) + sums(4, hid) + sums(4, hid) + sums(4, chans)
         + scratch
         + [
-            dma((seqs,)), dma((seqs,)), dma((seqs,)), dma((seqs,)), dma((4,)),
-            dma((2,)), dma((2,)), dma((2,)), dma((2,)),
+            dma((seqs,)), dma((seqs,)), dma((4,)),
+            dma((2, 5)), dma((2, 5)),
             dma((4, near)), dma((4, near)), dma((4, far)), dma((4, far)),
-            dma((nz,)), dma((nz,)), dma((nz, nb)), dma((nz, nb)),
-            dma((near, nz, nb)), dma((near, nz, nb)),
+            dma((2 * nz,)), dma((2 * nz,)), dma((2 * nz, nb)), dma((2 * nz, nb)),
+            dma((2 * nz, nb)), dma((2 * nz, nb)),
             dma((nz,)), dma((nz,)), dma((near, nz)), dma((near, nz)),
             dma((2, nz)), dma((2, nz)), dma((2, nb, nz)), dma((2, nb, nz)),
             dma((2, nz)), dma((2, nz)), dma((2, nb)), dma((2, nb)),
         ],
         compiler_params=pltpu.CompilerParams(
-            collective_id=0, has_side_effects=True, vmem_limit_bytes=60 * 2**20
+            collective_id=0, has_side_effects=True, vmem_limit_bytes=(54 if inside else 50) * 2**20
         ),
     )(x, og, black, unmap, limit, wd, wp, bias, g1, s1, g2, s2)
     if not inside:
         dwd, dwp = lax.psum((dwd, dwp), "bins")
         dwd = lax.psum_scatter(dwd, groups, scatter_dimension=0, tiled=True)
         dwp = lax.psum_scatter(dwp, groups, scatter_dimension=0, tiled=True)
-    return (
-        out,
-        gin,
-        dwd,
-        dwp,
-        bias_grad,
-        g1_grad,
-        s1_grad,
-        g2_grad,
-        s2_grad,
-    )
+    results = (x, x, dwd, dwp, bias, g1, s1, g2, s2)
+    kinds = (BF, BF) + (F32,) * 7
+    return pl.pallas_call(
+        write_out,
+        out_shape=tuple(jax.ShapeDtypeStruct(r.shape, t) for r, t in zip(results, kinds)),
+        in_specs=[vmem] * 5,
+        out_specs=(hbm,) * 4 + (vmem,) * 5,
+        scratch_shapes=[dma((4,))],
+        compiler_params=pltpu.CompilerParams(vmem_limit_bytes=2**20),
+    )(*(pltpu.with_memory_space_constraint(v, pltpu.VMEM) for v in (out, gin, dwd, dwp, tile)))
 
 
 def solution(mesh):

time: 106 us -> 95.1 us (0.90)
  local copies, waits for them, and re-layouts: 9.59 us -> 0 us
  Pallas kernels: 95.3 us -> 94.1 us
    unnamed x25 -> x0, local copies, waits for them, and re-layouts: 9.59 us -> none
    pallas_call x1 -> x2, Pallas kernels: 95.3 us -> 94.1 us  [the longest x1 90.7 us: local(): pl.pallas_call(functools.partial(call, sizes, inside), out_shape=(pltpu.V...]
where the time goes in v4:
time: 95.1 us; the launch traced here: 94.9 us
  Pallas kernels  94.1 us (99%)
    pallas_call x1, Pallas kernels, local(): pl.pallas_call(functools.partial(call, sizes, inside), out_shape=(pltpu.V...  90.7 us
    pallas_call x1, Pallas kernels, local(): pl.pallas_call(write_out, out_shape=tuple((jax.ShapeDtypeStruct(r.shape,...  3.43 us

profile of v4, /device:TPU:0, one launch (start us, length us, event | category | flops | bytes accessed | tf_op | source)
XLA Modules:
  0.0 94.9 jit_solution(12331097046015139586)
XLA Ops:
  0.6 90.7 %shard_map.187 = (bf16[8,256,768]{2,1,0:T(8,128)(2,1)S(1)}, bf16[8,256,768]{2,1,0:T(8,128)(2,1)S(1)}, f32[288,384]{1,0:T(8,128)S(1)}, f32[48,768]{1,0:T(8,128)S(1)}, f32[8,128]{1,0:T(8,128)S(1)}) custom-call(bf16[8,256,768]{2,1,0:T(8,128)(2,1)} %refs_0_.1, bf16[8,256,768]{2,1,0:T(8,128)(2,1)} %refs_1_.1, s32[8,256]{1,0:T(8,128)} %refs_2_.1, ...), custom_call_target="tpu_custom_call" | custom-call | tf_op jit(solution)/shard_map/pallas_call | solution.py:963
  91.3 3.4 %shard_map.188 = (bf16[8,256,768]{2,1,0:T(8,128)(2,1)}, bf16[8,256,768]{2,1,0:T(8,128)(2,1)}, f32[288,384]{1,0:T(8,128)}, f32[48,768]{1,0:T(8,128)}, f32[96]{0:T...) custom-call(bf16[8,256,768]{2,1,0:T(8,128)(2,1)S(1)} %get-tuple-element.14.out, ...), custom_call_target="tpu_custom_call" | custom-call | tf_op jit(solution)/shard_map/pallas_call | solution.py:1015

commit v5 on v4

--- a/solution.py
+++ b/solution.py
@@ -43,13 +43,13 @@
     xin, grad, vm, h1, z1, gw, h2, dz, taps, dg, zs_out, zs_in, mid_e, mid_z, upper, lower, mcol,
     fs1, fr1, cs1, cr1, fs2, fr2, cs2, cr2, fs3, fr3, cs3, cr3, fs4, fr4, cs4, cr4,
     black, unmap, wd_own, wp_own, pall, par, es, er,
-    wt, wd, wp, wall, dwd, dwp, dwd_red, dwp_red,
+    wt, wd, wp, wall_d, wall_p, dwd, dwp, dwd_red, dwp_red,
     xsem, gsem, lsem, hsem, zsem, fss, frs, css, crs,
     wzs, wzr, wcs, wcr, wfs, wfr, pzs, pzr, pfs, pfr,
     rfs, rfr, rxs, rxr, rzs, rzr, ras, rar,
 ):
     nb, nz, nf = sizes
-    inside = wall is not None
+    inside = wall_d is not None
     seqs, bins, chans = grad.shape
     hid = z1.shape[2]
     wide, narrow = chans // 128, hid // 128
@@ -115,10 +115,11 @@
     share = wp_own.shape[0]
     if inside:
         base = wd_own.shape[0]
-        piece = (base + 2 * share) // nb
-        wall[own, 0:base, :] = wd_own[...].astype(BF)
-        wall[own, base : base + share, :] = wp_own[:, 0:hid].astype(BF)
-        wall[own, base + share : base + 2 * share, :] = wp_own[:, hid:].astype(BF)
+        tall, small = base // nb, 2 * share // nb
+        for j in range(nb):
+            wall_d[own, j] = wd_own[j * tall : (j + 1) * tall, :].astype(BF)
+            first, col = j % 2 * small, j // 2 * hid
+            wall_p[own, j] = wp_own[first : first + small, col : col + hid].astype(BF)
 
     def before(i, k, n):
         return lax.rem(i + n - k, n)
@@ -155,35 +156,73 @@
         for k in range(nz)
     ]
 
-    def part(h, b):
-        rows = pl.ds(pl.multiple_of(before(bi, b, nb) * piece, 16), piece)
-        return wall.at[slot(zi - h, fi), rows, :]
-
-    if inside:
-        w_far = {
-            h: send(part(0, 0), wzs.at[i], wzr.at[i], {"batch": zi + h}) for i, h in enumerate(hops)
-        }
-        w_side = {
-            h: [
-                send(part(h, 0), wcs.at[i, b], wcr.at[i, b], {"bins": lax.rem(bi + b, nb)})
-                for b in range(1, nb)
-            ]
-            for i, h in enumerate(hops)
-        }
-        w_own = [send(wall.at[own], wfs.at[len(hops), 0], wfr.at[len(hops), 0], mate(1))]
-        w_near = {
-            h: [send(part(h, b), wfs.at[i, b], wfr.at[i, b], mate(1)) for b in range(nb)]
-            for i, h in enumerate(hops)
-        }
+    class Spread:
+        def __init__(self, i, ref):
+            def part(h, b):
+                return ref.at[slot(zi - h, fi), before(bi, b, nb)]
+
+            n = len(hops)
+            self.far = {
+                h: send(part(0, 0), wzs.at[i, k], wzr.at[i, k], {"batch": zi + h})
+                for k, h in enumerate(hops)
+            }
+            self.side = {
+                h: [
+                    send(part(h, 0), wcs.at[i, k, b], wcr.at[i, k, b], {"bins": lax.rem(bi + b, nb)})
+                    for b in range(1, nb)
+                ]
+                for k, h in enumerate(hops)
+            }
+            self.own = send(ref.at[own], wfs.at[i, n, 0], wfr.at[i, n, 0], mate(1))
+            self.near = {
+                h: [send(part(h, b), wfs.at[i, k, b], wfr.at[i, k, b], mate(1)) for b in range(nb)]
+                for k, h in enumerate(hops)
+            }
+
+        def begin(self):
+            for_hops(sends, lambda h: self.far[h].start())
+            self.own.start()
+
+        def arrive(self, h):
+            self.far[h].wait_recv()
+            self.near[h][0].start()
+
+        def across(self, h):
+            start(self.side[h])
+
+        def hand_on(self):
+            def near_work(h):
+                for b in range(1, nb):
+                    self.side[h][b - 1].wait_recv()
+                    self.near[h][b].start()
+
+            def near_end(h):
+                for c in self.near[h]:
+                    c.wait_recv()
+
+            for_hops(receives, near_work)
+            for_hops(receives, near_end)
+            self.own.wait_recv()
+
+        def end(self):
+            def sent(h):
+                for c in self.side[h] + self.near[h]:
+                    c.wait_send()
+
+            for_hops(sends, lambda h: self.far[h].wait_send())
+            for_hops(receives, sent)
+            self.own.wait_send()
+
+    if inside:
+        spread_d, spread_p = Spread(0, wall_d), Spread(1, wall_p)
 
     def for_hops(test, do):
         for h in hops if inside else ():
             pl.when(test(h))(functools.partial(do, h))
 
     pl.semaphore_wait(barrier, len(mates) + len(chips))
-    for_hops(sends, lambda h: w_far[h].start())
-    if inside:
-        start(w_own)
+    if inside:
+        spread_d.begin()
     start(par_far)
     start(par_near[0])
 
@@ -394,7 +433,6 @@
 
     far_first = list(range(1, nz)) + [0]
     if inside:
-        tall, small = base // nb, 2 * share // nb
 
         def dwd_get(c, j):
             return dwd[pl.ds(pl.multiple_of(c * base + j * tall, 8), tall), :]
@@ -428,33 +466,31 @@
         return acc
 
     acc = lax.fori_loop(0, seqs, squares_x, jnp.zeros((8, chans), F32))
-    fs1[0:1, :] = sum_one
-    fs1[1:2, :] = jnp.sum(acc, axis=0, keepdims=True)
-    fs1[2:3, :] = count_wide
-    fs1[3:4, :] = count_wide
+    fs1[0:1, :chans] = sum_one
+    fs1[1:2, :chans] = jnp.sum(acc, axis=0, keepdims=True)
+    fs1[0:1, chans:] = own_count
+    fs1[1:2, chans:] = own_count
 
     def triple(ref):
-        return ref[0:1, :], ref[1:2, :], ref[2:3, :]
+        n = jnp.concatenate([ref[0:1, chans:]] * wide, axis=1)
+        return ref[0:1, :chans], ref[1:2, :chans], n
 
     mine = mate_copies(0, fs1, fr1)
     start(mine)
 
     def side_work(h):
-        w_far[h].wait_recv()
-        start(w_side[h])
-        w_near[h][0].start()
-
-    for h in hops[:2] if inside else ():
-        pl.when(receives(h))(functools.partial(side_work, h))
+        spread_d.arrive(h)
+        spread_d.across(h)
+
     wait(mine)
     s_, q_, n_ = merge([triple(fs1)] + [triple(fr1.at[j]) for j in range(len(mates))])
-    cs1[0:1, :] = s_
-    cs1[1:2, :] = q_
-    cs1[2:3, :] = n_
-    cs1[3:4, :] = n_
+    cs1[0:1, :chans] = s_
+    cs1[1:2, :chans] = q_
+    cs1[0:1, chans:] = n_[:, :128]
+    cs1[1:2, chans:] = n_[:, :128]
     far = chip_copies(0, cs1, cr1)
     start(far)
-    for h in hops[2:] if inside else ():
+    for h in hops if inside else ():
         pl.when(receives(h))(functools.partial(side_work, h))
 
     def mask_grad(s, acc):
@@ -517,24 +553,15 @@
     acc = lax.fori_loop(0, seqs, first_act, jnp.zeros((8, chans), F32))
     act_sum = jnp.sum(acc, axis=0, keepdims=True)
 
-    def near_work(h):
-        for b in range(1, nb):
-            w_side[h][b - 1].wait_recv()
-            w_near[h][b].start()
-
-    def near_end(h):
-        for c in w_near[h]:
-            c.wait_recv()
-
-    for_hops(receives, near_work)
-    for_hops(receives, near_end)
-    if inside:
-        for c in w_own:
-            c.wait_recv()
+    if inside:
+        spread_p.begin()
+
+    if inside:
+        spread_d.hand_on()
         for c in range(nz * nf):
-            wd[c * base : (c + 1) * base, :] = wall[c, 0:base, :]
-            wp[c * share : (c + 1) * share, 0:hid] = wall[c, base : base + share, :]
-            wp[c * share : (c + 1) * share, hid:] = wall[c, base + share : base + 2 * share, :]
+            for j in range(nb):
+                first = c * base + j * tall
+                wd[first : first + tall, :] = wall_d[c, j]
 
     def tap(k):
         return wd[k * chans : (k + 1) * chans, :]
@@ -564,6 +591,9 @@
 
     lax.fori_loop(0, 1, conv, 0)
     e_onward()
+    if inside:
+        for_hops(receives, spread_p.arrive)
+        for_hops(receives, spread_p.across)
     lax.fori_loop(1, 2, conv, 0)
 
     e_last()
@@ -600,7 +630,7 @@
     fs2[3:4, :] = own_bias[:, hid:]
 
     def pair(ref, n):
-        return ref[0:1, :], ref[1:2, :], n[2:3, :hid]
+        return ref[0:1, :], ref[1:2, :], jnp.concatenate([n[0:1, chans:]] * narrow, axis=1)
 
     mine = mate_copies(1, fs2, fr2)
     start(mine)
@@ -622,9 +652,15 @@
         gw[some] = dot(left, wp[...], 1, 1).reshape(group, bins, hid)
         return 0
 
-    lax.fori_loop(0, 2, grad_point, 0)
     for k in range(3):
         wt[k * hid : (k + 1) * hid, :] = jnp.transpose(tap(k))
+    if inside:
+        spread_p.hand_on()
+        for c in range(nz * nf):
+            for j in range(nb):
+                first, col = c * share + j % 2 * small, j // 2 * hid
+                wp[first : first + small, col : col + hid] = wall_p[c, j]
+    lax.fori_loop(0, 2, grad_point, 0)
 
     wait(far)
     entries = [pair(cs2, cs1)] + [pair(cr2.at[j], cr1.at[j]) for j in range(len(chips))]
@@ -674,46 +710,50 @@
     fs3[3:4, :] = act_sum[:, hid:]
 
     def point_work():
-        def branch(s, _):
-            out[s] = (
-                xin[s].astype(F32) + dot(h2[s], wp[...], 1, 0) + par[0:1, :]
-            ).astype(BF)
-            return 0
-
-        lax.fori_loop(0, seqs, branch, 0)
         flat = grad[...].reshape(seqs * bins, chans)
         dwp[...] = dot(h2[...].reshape(seqs * bins, hid), flat, 0, 0)
+        if inside:
+            for d in far_first:
+                point_f(d)
+
+        def branch(i, _):
+            some = pl.ds(i * 2, 2)
+            more = dot(h2[some].reshape(2 * bins, hid), wp[...], 1, 0) + par[0:1, :]
+            out[some] = (xin[some].astype(F32) + more.reshape(2, bins, chans)).astype(BF)
+            return 0
+
+        lax.fori_loop(0, seqs // 2, branch, 0)
+        if inside:
+            for d in far_first:
+                point_x(d)
 
     both = plain_sum(2, fs3, fr3, cs3, cr3, point_work)
     shift_total, gain_total = both[0:1, :], both[1:2, :]
     owned(3, narrow_row, gain_total)
     owned(4, narrow_row, shift_total)
-    if inside:
-        for d in far_first:
-            point_f(d)
     outer = scale_two * gain_two
     level = shift_total / count[:, :hid]
     slant = gain_total / count[:, :hid]
 
+    dz_sum = outer * (
+        fs3[0:1, :] - level * count_narrow - slant * (sum_two - count_narrow * mean_two) * scale_two
+    )
     typical = jnp.concatenate([both[2:3, :], both[3:4, :]], axis=1) / (nb * nz * nf * seqs * bins)
     typical = jnp.concatenate([typical, jnp.zeros((7, chans), F32)], axis=0)
     middle_act = lax.dot_general(
         typical, jnp.ones((8, 128), F32), (((0,), (0,)), ((), ())),
         precision=lax.Precision.HIGHEST, preferred_element_type=F32,
     )
-    for k in range(3):
-        mcol[k * chans : (k + 1) * chans, :] = middle_act
-
-    def conv_grad(s, acc):
+    mcol[...] = middle_act
+
+    def conv_grad(s, _):
         for r in range(pieces):
             rows = slice(r * CHUNK, (r + 1) * CHUNK)
             d = outer * (gw[s, rows, :] - mask(s, r, narrow) * (level + z1[s, rows, :] * slant))
             dz[s, PAD + r * CHUNK : PAD + (r + 1) * CHUNK, :] = d.astype(BF)
-            acc = acc + fold(d)
-        return acc
-
-    acc = lax.fori_loop(0, seqs, conv_grad, jnp.zeros((8, hid), F32))
-    dz_sum = jnp.sum(acc, axis=0, keepdims=True)
+        return 0
+
+    lax.fori_loop(0, seqs, conv_grad, 0)
 
     def rank_one(first, count, row):
         m = mcol[pl.ds(pl.multiple_of(first, 8), count), :]
@@ -732,9 +772,6 @@
         return 0
 
     lax.fori_loop(0, seqs, shift_taps, 0)
-    if inside:
-        for d in far_first:
-            point_x(d)
 
     def kernel_grad(m, _):
         cols = pl.ds(pl.multiple_of(m * hid, 128), hid)
@@ -749,7 +786,12 @@
 
     lax.fori_loop(0, 1, kernel_grad, 0)
     z_onward()
+    if inside:
+        for d in far_first:
+            point_z(d)
     lax.fori_loop(1, chans // hid, kernel_grad, 0)
+    if inside:
+        point_a()
 
     z_last()
 
@@ -781,8 +823,6 @@
     if inside:
         for d in far_first:
             wide_f(d)
-        for d in far_first:
-            point_z(d)
         wide_x(far_first[0])
 
     def back_conv(i):
@@ -814,15 +854,12 @@
     if inside:
         for d in far_first[1:]:
             wide_x(d)
-        point_a()
     a, b = lax.fori_loop(1, seqs // 2, input_side, (zero, zero))
     a, b = back_act(seqs // 2 - 1, (a, b))
     if inside:
         wide_z(far_first[0])
     fs4[0:1, :] = jnp.sum(a, axis=0, keepdims=True)
     fs4[1:2, :] = jnp.sum(b, axis=0, keepdims=True)
-    fs4[2:3, :] = jnp.concatenate([dz_sum, dz_sum], axis=1)
-    fs4[3:4, :] = fs4[2:3, :]
 
     def weight_work():
         if inside:
@@ -850,8 +887,7 @@
     if inside:
 
         def put_wide(j, v):
-            more = rank_one(own * base + j * tall, tall, both[2:3, :hid])
-            dwd_out[j * tall : (j + 1) * tall, :] = v + more
+            dwd_out[j * tall : (j + 1) * tall, :] = v
 
         def put_point(j, v):
             dwp_out[j % 2 * small : (j % 2 + 1) * small, j // 2 * hid : (j // 2 + 1) * hid] = v
@@ -863,26 +899,19 @@
     for k in range(nz):
         for c in par_near[k]:
             c.wait_send()
-
-    def sent(h):
-        for c in w_side[h] + w_near[h]:
-            c.wait_send()
-
-    for_hops(sends, lambda h: w_far[h].wait_send())
-    for_hops(receives, sent)
-    if inside:
-        for c in w_own:
-            c.wait_send()
+    if inside:
+        spread_d.end()
+        spread_p.end()
 
 
 def call(sizes, inside, *refs):
     refs = list(refs)
     first = 17 + 17 + 16 + 9
     if inside:
-        red = first + 5
+        red = first + 6
         refs[red : red + 14] = [refs[red : red + 7], refs[red + 7 : red + 14]]
     else:
-        refs[first:first] = [refs[first - 7], refs[first - 6], None, refs[14], refs[15], None, None]
+        refs[first:first] = [refs[first - 7], refs[first - 6], None, None, refs[14], refs[15], None, None]
     block(sizes, *refs)
 
 
@@ -910,14 +939,14 @@
         nf == 2
         and nb == 4
         and wd.shape[0] % (8 * nb) == 0
-        and wp.shape[0] % 16 == 0
-        and (wd.shape[0] + 2 * wp.shape[0]) % (16 * nb) == 0
+        and 2 * wp.shape[0] % (8 * nb) == 0
         and chans == 2 * hid
     )
     if not inside:
         wd = lax.all_gather(wd.astype(BF), groups, axis=0, tiled=True)
         wp = lax.all_gather(wp.astype(BF), groups, axis=0, tiled=True)
     near, far = nf - 1, nb * nz - 1
+    steps = 2 * nz if inside else 1
     vmem = pl.BlockSpec(memory_space=pltpu.VMEM)
     hbm = pl.BlockSpec(memory_space=pl.ANY)
     dma = pltpu.SemaphoreType.DMA
@@ -946,7 +975,8 @@
         scratch += [
             pltpu.VMEM((3 * chans, hid), BF),
             pltpu.VMEM((hid, chans), BF),
-            pltpu.VMEM((nz * nf, wd.shape[0] + 2 * wp.shape[0], hid), BF),
+            pltpu.VMEM((nz * nf, nb, wd.shape[0] // nb, hid), BF),
+            pltpu.VMEM((nz * nf, nb, 2 * wp.shape[0] // nb, hid), BF),
             pltpu.VMEM((3 * chans, hid), F32),
             pltpu.VMEM((hid, chans), F32),
         ]
@@ -988,19 +1018,19 @@
             pltpu.VMEM((seqs // 2 * STEP, hid), BF),
             pltpu.VMEM((seqs, PAD, hid), BF),
             pltpu.VMEM((seqs, PAD, hid), BF),
-            pltpu.VMEM((3 * chans, 128), F32),
+            pltpu.VMEM((chans, 128), F32),
         ]
-        + sums(4, chans) + sums(4, hid) + sums(4, hid) + sums(4, chans)
+        + sums(2, chans + 128) + sums(4, hid) + sums(4, hid) + sums(2, chans)
         + scratch
         + [
             dma((seqs,)), dma((seqs,)), dma((4,)),
             dma((2, 5)), dma((2, 5)),
             dma((4, near)), dma((4, near)), dma((4, far)), dma((4, far)),
-            dma((2 * nz,)), dma((2 * nz,)), dma((2 * nz, nb)), dma((2 * nz, nb)),
-            dma((2 * nz, nb)), dma((2 * nz, nb)),
+            dma((2, steps)), dma((2, steps)), dma((2, steps, nb)), dma((2, steps, nb)),
+            dma((2, steps, nb)), dma((2, steps, nb)),
             dma((nz,)), dma((nz,)), dma((near, nz)), dma((near, nz)),
-            dma((2, nz)), dma((2, nz)), dma((2, nb, nz)), dma((2, nb, nz)),
-            dma((2, nz)), dma((2, nz)), dma((2, nb)), dma((2, nb)),
+            dma((2, steps)), dma((2, steps)), dma((2, nb, steps)), dma((2, nb, steps)),
+            dma((2, steps)), dma((2, steps)), dma((2, nb)), dma((2, nb)),
         ],
         compiler_params=pltpu.CompilerParams(
             collective_id=0, has_side_effects=True, vmem_limit_bytes=(54 if inside else 50) * 2**20

time: 95.1 us -> 89.8 us (0.944)
  Pallas kernels: 94.1 us -> 88.8 us
    pallas_call x1, Pallas kernels: 90.7 us -> 85.3 us  [local(): pl.pallas_call(functools.partial(call, sizes, inside), out_shape=(pltpu.V...]
where the time goes in v5:
time: 89.8 us; the launch traced here: 89.6 us
  Pallas kernels  88.8 us (99%)
    pallas_call x1, Pallas kernels, local(): pl.pallas_call(functools.partial(call, sizes, inside), out_shape=(pltpu.V...  85.3 us
    pallas_call x1, Pallas kernels, local(): pl.pallas_call(write_out, out_shape=tuple((jax.ShapeDtypeStruct(r.shape,...  3.43 us

profile of v5, /device:TPU:0, one launch (start us, length us, event | category | flops | bytes accessed | tf_op | source)
XLA Modules:
  0.0 89.6 jit_solution(10852463288765643668)
XLA Ops:
  0.6 85.3 %shard_map.187 = (bf16[8,256,768]{2,1,0:T(8,128)(2,1)S(1)}, bf16[8,256,768]{2,1,0:T(8,128)(2,1)S(1)}, f32[288,384]{1,0:T(8,128)S(1)}, f32[48,768]{1,0:T(8,128)S(1)}, f32[8,128]{1,0:T(8,128)S(1)}) custom-call(bf16[8,256,768]{2,1,0:T(8,128)(2,1)} %refs_0_.1, bf16[8,256,768]{2,1,0:T(8,128)(2,1)} %refs_1_.1, s32[8,256]{1,0:T(8,128)} %refs_2_.1, ...), custom_call_target="tpu_custom_call" | custom-call | tf_op jit(solution)/shard_map/pallas_call | solution.py:993
  86.0 3.4 %shard_map.188 = (bf16[8,256,768]{2,1,0:T(8,128)(2,1)}, bf16[8,256,768]{2,1,0:T(8,128)(2,1)}, f32[288,384]{1,0:T(8,128)}, f32[48,768]{1,0:T(8,128)}, f32[96]{0:T...) custom-call(bf16[8,256,768]{2,1,0:T(8,128)(2,1)S(1)} %get-tuple-element.14.out, ...), custom_call_target="tpu_custom_call" | custom-call | tf_op jit(solution)/shard_map/pallas_call | solution.py:1045

commit v6 on v5

--- a/solution.py
+++ b/solution.py
@@ -10,7 +10,7 @@
 STEP = 26
 EPS = 1e-5
 PAD = 32
-CHUNK = 32
+CHUNK = 16
 MESH = pl.DeviceIdType.MESH
 BF = jnp.bfloat16
 F32 = jnp.float32
@@ -333,13 +333,14 @@
             for j, (k,) in enumerate(mates)
         ]
 
-    def chip_copies(i, src, dst):
+    def chip_copies(i, src, dst, only=lambda b, z: True):
         return [
             pltpu.make_async_remote_copy(
                 src_ref=src, dst_ref=dst.at[j], send_sem=css.at[i, j], recv_sem=crs.at[i, j],
                 device_id=chip(b, z), device_id_type=MESH,
             )
             for j, (b, z) in enumerate(chips)
+            if only(b, z)
         ]
 
     def plain_sum(i, fs, fr, cs, cr, filler):
@@ -746,24 +747,27 @@
     )
     mcol[...] = middle_act
 
-    def conv_grad(s, _):
-        for r in range(pieces):
+    def conv_grad(some, s, _):
+        for r in some:
             rows = slice(r * CHUNK, (r + 1) * CHUNK)
             d = outer * (gw[s, rows, :] - mask(s, r, narrow) * (level + z1[s, rows, :] * slant))
             dz[s, PAD + r * CHUNK : PAD + (r + 1) * CHUNK, :] = d.astype(BF)
         return 0
 
-    lax.fori_loop(0, seqs, conv_grad, 0)
-
-    def rank_one(first, count, row):
-        m = mcol[pl.ds(pl.multiple_of(first, 8), count), :]
-        return jnp.concatenate([m] * narrow, axis=1) * row
-
+    ends_of = -(-STEP // CHUNK)
+    outside = [*range(ends_of), *range(pieces - ends_of, pieces)]
+    lax.fori_loop(0, seqs, functools.partial(conv_grad, outside), 0)
     for s in range(seqs):
         zs_out[(0,) + packed(s)] = dz[s, PAD : PAD + STEP, :]
         zs_out[(1,) + packed(s)] = dz[s, PAD + bins - STEP : PAD + bins, :]
     z_first, z_onward, z_last = edges(zs_out, zs_in, mid_z, zsem)
     z_first()
+
+    lax.fori_loop(0, seqs, functools.partial(conv_grad, range(ends_of, pieces - ends_of)), 0)
+
+    def rank_one(first, count, row):
+        m = mcol[pl.ds(pl.multiple_of(first, 8), count), :]
+        return jnp.concatenate([m] * narrow, axis=1) * row
 
     def shift_taps(s, _):
         for k in range(3):
@@ -865,9 +869,31 @@
         if inside:
             for d in far_first[1:]:
                 wide_z(d)
-            wide_a()
-
-    both = plain_sum(3, fs4, fr4, cs4, cr4, weight_work)
+
+    mine = mate_copies(3, fs4, fr4)
+    start(mine)
+    wait(mine)
+    total = fs4[...]
+    for j in range(len(mates)):
+        total = total + fr4[j]
+    cs4[...] = total
+    far = chip_copies(3, cs4, cr4, lambda b, z: z == 0)
+    side = [j for j, (b, z) in enumerate(chips) if z == 0]
+    start(far)
+    weight_work()
+    wait(far)
+    for j in side:
+        total = total + cr4[j]
+    fs4[...] = total
+    far = chip_copies(3, fs4, cr4, lambda b, z: b == 0)
+    side = [j for j, (b, z) in enumerate(chips) if b == 0]
+    start(far)
+    if inside:
+        wide_a()
+    wait(far)
+    for j in side:
+        total = total + cr4[j]
+    both = total
     shift_total, gain_total = both[0:1, :], both[1:2, :]
     owned(1, wide_row, gain_total)
     owned(2, wide_row, shift_total)

time: 89.8 us -> 87.5 us (0.974)
  Pallas kernels: 88.8 us -> 86.5 us
    pallas_call x1, Pallas kernels: 85.3 us -> 83.1 us  [local(): pl.pallas_call(functools.partial(call, sizes, inside), out_shape=(pltpu.V...]
where the time goes in v6:
time: 87.5 us; the launch traced here: 87.3 us
  Pallas kernels  86.5 us (99%)
    pallas_call x1, Pallas kernels, local(): pl.pallas_call(functools.partial(call, sizes, inside), out_shape=(pltpu.V...  83.1 us
    pallas_call x1, Pallas kernels, local(): pl.pallas_call(write_out, out_shape=tuple((jax.ShapeDtypeStruct(r.shape,...  3.43 us

profile of v6, /device:TPU:0, one launch (start us, length us, event | category | flops | bytes accessed | tf_op | source)
XLA Modules:
  0.0 87.3 jit_solution(18303507367913917498)
XLA Ops:
  0.6 83.1 %shard_map.187 = (bf16[8,256,768]{2,1,0:T(8,128)(2,1)S(1)}, bf16[8,256,768]{2,1,0:T(8,128)(2,1)S(1)}, f32[288,384]{1,0:T(8,128)S(1)}, f32[48,768]{1,0:T(8,128)S(1)}, f32[8,128]{1,0:T(8,128)S(1)}) custom-call(bf16[8,256,768]{2,1,0:T(8,128)(2,1)} %refs_0_.1, bf16[8,256,768]{2,1,0:T(8,128)(2,1)} %refs_1_.1, s32[8,256]{1,0:T(8,128)} %refs_2_.1, ...), custom_call_target="tpu_custom_call" | custom-call | tf_op jit(solution)/shard_map/pallas_call | solution.py:1019
  83.7 3.4 %shard_map.188 = (bf16[8,256,768]{2,1,0:T(8,128)(2,1)}, bf16[8,256,768]{2,1,0:T(8,128)(2,1)}, f32[288,384]{1,0:T(8,128)}, f32[48,768]{1,0:T(8,128)}, f32[96]{0:T...) custom-call(bf16[8,256,768]{2,1,0:T(8,128)(2,1)S(1)} %get-tuple-element.14.out, ...), custom_call_target="tpu_custom_call" | custom-call | tf_op jit(solution)/shard_map/pallas_call | solution.py:1071

commit v7 on v6

--- a/solution.py
+++ b/solution.py
@@ -816,14 +816,14 @@
     ahead = ahead.reshape(seqs * PAD, hid)
 
     def kernel_edge(m, _):
-        cols = pl.ds(pl.multiple_of(m * 256, 256), 256)
+        cols = pl.ds(pl.multiple_of(m * hid, 128), hid)
         for k, rows, right in ((0, bins, after), (2, PAD, ahead)):
-            left = h1[:, rows : rows + PAD, cols].reshape(seqs * PAD, 256)
-            where = pl.ds(pl.multiple_of(k * chans + m * 256, 256), 256)
+            left = h1[:, rows : rows + PAD, cols].reshape(seqs * PAD, hid)
+            where = pl.ds(pl.multiple_of(k * chans + m * hid, 128), hid)
             dwd[where, :] = dwd[where, :] + dot(left, right, 0, 0)
         return 0
 
-    lax.fori_loop(0, chans // 256, kernel_edge, 0)
+    lax.fori_loop(0, chans // hid, kernel_edge, 0)
     if inside:
         for d in far_first:
             wide_f(d)

time: 87.5 us -> 87.3 us (level)
  no operation moved by 1% of the time
where the time goes in v7:
time: 87.3 us; the launch traced here: 87.1 us
  Pallas kernels  86.3 us (99%)
    pallas_call x1, Pallas kernels, local(): pl.pallas_call(functools.partial(call, sizes, inside), out_shape=(pltpu.V...  82.9 us
    pallas_call x1, Pallas kernels, local(): pl.pallas_call(write_out, out_shape=tuple((jax.ShapeDtypeStruct(r.shape,...  3.43 us

profile of v7, /device:TPU:0, one launch (start us, length us, event | category | flops | bytes accessed | tf_op | source)
XLA Modules:
  0.0 87.1 jit_solution(7260861538918232332)
XLA Ops:
  0.6 82.9 %shard_map.187 = (bf16[8,256,768]{2,1,0:T(8,128)(2,1)S(1)}, bf16[8,256,768]{2,1,0:T(8,128)(2,1)S(1)}, f32[288,384]{1,0:T(8,128)S(1)}, f32[48,768]{1,0:T(8,128)S(1)}, f32[8,128]{1,0:T(8,128)S(1)}) custom-call(bf16[8,256,768]{2,1,0:T(8,128)(2,1)} %refs_0_.1, bf16[8,256,768]{2,1,0:T(8,128)(2,1)} %refs_1_.1, s32[8,256]{1,0:T(8,128)} %refs_2_.1, ...), custom_call_target="tpu_custom_call" | custom-call | tf_op jit(solution)/shard_map/pallas_call | solution.py:1019
  83.5 3.4 %shard_map.188 = (bf16[8,256,768]{2,1,0:T(8,128)(2,1)}, bf16[8,256,768]{2,1,0:T(8,128)(2,1)}, f32[288,384]{1,0:T(8,128)}, f32[48,768]{1,0:T(8,128)}, f32[96]{0:T...) custom-call(bf16[8,256,768]{2,1,0:T(8,128)(2,1)S(1)} %get-tuple-element.14.out, ...), custom_call_target="tpu_custom_call" | custom-call | tf_op jit(solution)/shard_map/pallas_call | solution.py:1071
